TPU v7x, 32 devices: a whole 2x2x4 slice. The times are simulated.
32 devices in a mesh: fsdp: 4 (over z), ctx: 4 (over x, core), tp: 2 (over y).
Axes of the slice: x: 2, y: 2, z: 4, core: 2. Of those that a mesh axis runs over, the one named last changes fastest.
Arguments:
- layer_input: bfloat16 [16384, 1024], P(('fsdp', 'ctx')), may hold values from -6 to 6
- seq_lengths: int32 [4, 2], P('fsdp'), may hold values from 1 to 3072, 4096 in all within a row
- deal_order: int32 [16384], P(('fsdp', 'ctx')), may hold values from 0 to 16383, as said below
- qkv_weight: bfloat16 [1024, 3, 1024], P('fsdp', None, 'tp'), may hold values from -0.1875 to 0.1875
- qkv_bias: bfloat16 [3, 1024], P(None, ('tp', 'fsdp')), may hold values from -0.3125 to 0.3125
- out_weight: bfloat16 [1024, 1024], P(('tp', 'fsdp')), may hold values from -3 to 3
- out_bias: bfloat16 [1024], P('fsdp'), may hold values from -1.75 to 1.75
- first_gain: bfloat16 [1024], P('fsdp'), may hold values from 0.5 to 1.5
- first_shift: bfloat16 [1024], P('fsdp'), may hold values from -1.75 to 1.75
- up_weight: bfloat16 [1024, 4096], P('fsdp', 'tp'), may hold values from -0.1875 to 0.1875
- up_bias: bfloat16 [4096], P(('tp', 'fsdp')), may hold values from -1.75 to 1.75
- down_weight: bfloat16 [4096, 1024], P(('tp', 'fsdp')), may hold values from -0.09375 to 0.09375
- down_bias: bfloat16 [1024], P('fsdp'), may hold values from -1.75 to 1.75
- second_gain: bfloat16 [1024], P('fsdp'), may hold values from 0.5 to 1.5
- second_shift: bfloat16 [1024], P('fsdp'), may hold values from -1.75 to 1.75
- proj_weight: bfloat16 [1024, 288], P('fsdp'), may hold values from -0.1875 to 0.1875
- cot_output: bfloat16 [16384, 1024], P(('fsdp', 'ctx')), may hold values from -6 to 6
- cot_embed: bfloat16 [16384, 288], P(('fsdp', 'ctx')), may hold values from -6 to 6
Outputs:
- output: bfloat16 [16384, 1024], P(('fsdp', 'ctx'))
- embed_out: bfloat16 [16384, 288], P(('fsdp', 'ctx'))
- input_grad: bfloat16 [16384, 1024], P(('fsdp', 'ctx'))
- qkv_weight_grad: float32 [1024, 3, 1024], P('fsdp', None, 'tp')
- qkv_bias_grad: float32 [3, 1024], P(None, ('tp', 'fsdp'))
- out_weight_grad: float32 [1024, 1024], P(('tp', 'fsdp'))
- out_bias_grad: float32 [1024], P('fsdp')
- first_gain_grad: float32 [1024], P('fsdp')
- first_shift_grad: float32 [1024], P('fsdp')
- up_weight_grad: float32 [1024, 4096], P('fsdp', 'tp')
- up_bias_grad: float32 [4096], P(('tp', 'fsdp'))
- down_weight_grad: float32 [4096, 1024], P(('tp', 'fsdp'))
- down_bias_grad: float32 [1024], P('fsdp')
- second_gain_grad: float32 [1024], P('fsdp')
- second_shift_grad: float32 [1024], P('fsdp')
- proj_weight_grad: float32 [1024, 288], P('fsdp')
Inputs may be any that keep to these rules, and one draw needn't show every extreme that they name: Each row of seq_lengths holds the lengths of the 2 sequences of one group; they sum to 4096 and the longest is at most 3072. `deal_order`: each aligned block of 4096 entries holds every row index of that same block exactly once.
All inputs are finite; a program needn't handle non-finite values.
Results may differ from a plain program's by a relative error of at most 0.025.
Values may be sent and summed in bfloat16 or wider, within the bound.
No kernel may reach another device: no remote copies, remote signals or barrier semaphores. Data moves between devices by JAX's collectives and lax.ppermute only.
A program may use at most 192 MiB of HBM per device.

v0:
```python
from functools import partial
import math

import jax
import jax.numpy as jnp
from jax import lax
from jax.sharding import PartitionSpec as P

HEAD_DIM = 64
PROJ_A = 128
PROJ_B = 96
PROJ_C = 64


norm_eps = 1e-05
embed_eps = 1e-06
rope_base = 10000.0
masked_score = -1e30


def layer_norm(values, norm_gain, norm_shift):
    centred = values - jnp.mean(values, axis=-1, keepdims=True)
    variance = jnp.mean(centred * centred, axis=-1, keepdims=True)
    return centred * lax.rsqrt(variance + norm_eps) * norm_gain + norm_shift


def rotate(values, cos_table, sin_table):
    half_dim = values.shape[-1] // 2
    front_half = values[..., :half_dim]
    back_half = values[..., half_dim:]
    return jnp.concatenate(
        [
            front_half * cos_table - back_half * sin_table,
            back_half * cos_table + front_half * sin_table,
        ],
        axis=-1,
    )


def rope_tables(position, head_width):
    half_dim = head_width // 2
    frequency = jnp.exp(
        jnp.arange(half_dim, dtype=jnp.float32) * (-2.0 * math.log(rope_base) / head_width)
    )
    angles = position.astype(jnp.float32)[:, None] * frequency[None, :]
    return (jnp.cos(angles)[:, None, :], jnp.sin(angles)[:, None, :])


def sequence_layout(seq_lengths, row_ids):
    seq_ends = jnp.cumsum(seq_lengths)
    segment = jnp.sum((row_ids[:, None] >= seq_ends[None, :]).astype(jnp.int32), axis=1)
    seq_starts = seq_ends - seq_lengths
    picked = (
        segment[:, None] == jnp.arange(seq_lengths.shape[0], dtype=jnp.int32)[None, :]
    ).astype(jnp.int32)
    position = row_ids - jnp.sum(picked * seq_starts[None, :], axis=1)
    return (segment, position)


def embed_heads(projected):
    pieces = []
    column_start = 0
    for head_width in (PROJ_A, PROJ_B, PROJ_C):
        head_cols = projected[:, column_start : column_start + head_width]
        pieces.append(
            head_cols * lax.rsqrt(jnp.sum(head_cols * head_cols, axis=1, keepdims=True) + embed_eps)
        )
        column_start += head_width
    return jnp.concatenate(pieces, axis=1)


def contract(left, right, left_dim, right_dim):
    return lax.dot_general(
        left, right, (((left_dim,), (right_dim,)), ((), ())), preferred_element_type=jnp.float32
    )


def shards(
    layer_input,
    seq_lengths,
    deal_order,
    qkv_weight,
    qkv_bias,
    out_weight,
    out_bias,
    first_gain,
    first_shift,
    up_weight,
    up_bias,
    down_weight,
    down_bias,
    second_gain,
    second_shift,
    proj_weight,
    cot_output,
    cot_embed,
):
    own_rows = layer_input.shape[0]
    group_rows = own_rows * lax.axis_size("ctx")
    group_lengths = seq_lengths[0]
    local_source = deal_order % group_rows
    group_input, group_cot, group_cot_embed = (
        lax.all_gather(layer_input, "ctx", axis=0, tiled=True),
        lax.all_gather(cot_output, "ctx", axis=0, tiled=True),
        lax.all_gather(cot_embed, "ctx", axis=0, tiled=True),
    )
    packed = group_input[local_source]
    packed_cot = group_cot[local_source].astype(jnp.float32)
    packed_cot_embed = group_cot_embed[local_source].astype(jnp.float32)
    row_ids = lax.axis_index("ctx") * own_rows + jnp.arange(own_rows, dtype=jnp.int32)
    segment, position = sequence_layout(group_lengths, row_ids)
    (
        qkv_full,
        qkv_bias_full,
        out_full,
        out_bias_full,
        first_gain_full,
        first_shift_full,
        up_full,
        up_bias_full,
        down_full,
        down_bias_full,
        second_gain_full,
        second_shift_full,
        proj_full,
    ) = (
        lax.all_gather(qkv_weight, "fsdp", axis=0, tiled=True),
        lax.all_gather(qkv_bias, "fsdp", axis=1, tiled=True),
        lax.all_gather(out_weight, "fsdp", axis=0, tiled=True),
        lax.all_gather(out_bias, "fsdp", axis=0, tiled=True),
        lax.all_gather(first_gain, "fsdp", axis=0, tiled=True),
        lax.all_gather(first_shift, "fsdp", axis=0, tiled=True),
        lax.all_gather(up_weight, "fsdp", axis=0, tiled=True),
        lax.all_gather(up_bias, "fsdp", axis=0, tiled=True),
        lax.all_gather(down_weight, "fsdp", axis=0, tiled=True),
        lax.all_gather(down_bias, "fsdp", axis=0, tiled=True),
        lax.all_gather(second_gain, "fsdp", axis=0, tiled=True),
        lax.all_gather(second_shift, "fsdp", axis=0, tiled=True),
        lax.all_gather(proj_weight, "fsdp", axis=0, tiled=True),
    )
    local_width = qkv_full.shape[2]
    local_heads = local_width // HEAD_DIM
    score_scale = HEAD_DIM ** (-0.5)
    mixed = (
        jnp.einsum("td,dwe->twe", packed, qkv_full, preferred_element_type=jnp.float32)
        + qkv_bias_full.astype(jnp.float32)[None]
    )
    shaped = mixed.reshape(own_rows, 3, local_heads, HEAD_DIM)
    cos_table, sin_table = rope_tables(position, HEAD_DIM)

    def rope_pair(query_pre, key_pre):
        return (rotate(query_pre, cos_table, sin_table), rotate(key_pre, cos_table, sin_table))

    (query_rot, key_rot), rope_back = jax.vjp(rope_pair, shaped[:, 0], shaped[:, 1])
    query_heads = jnp.transpose(query_rot.astype(jnp.bfloat16), (1, 0, 2))
    key_low = key_rot.astype(jnp.bfloat16).reshape(own_rows, local_width)
    value_low = shaped[:, 2].astype(jnp.bfloat16).reshape(own_rows, local_width)

    def key_mask(count):
        key_segment = sequence_layout(group_lengths, jnp.arange(count, dtype=jnp.int32))[0]
        return segment[:, None] == key_segment[None, :]

    start_state = (
        jnp.full((local_heads, own_rows), masked_score, jnp.float32),
        jnp.zeros((local_heads, own_rows), jnp.float32),
        jnp.zeros((local_heads, own_rows, HEAD_DIM), jnp.float32),
    )
    key_piece = lax.all_gather(key_low, "ctx", axis=0, tiled=True)
    value_piece = lax.all_gather(value_low, "ctx", axis=0, tiled=True)
    count = key_piece.shape[0]
    same_seq = key_mask(count)
    key_heads = key_piece.reshape(count, local_heads, HEAD_DIM)
    value_heads = value_piece.reshape(count, local_heads, HEAD_DIM)

    def forward_one_head(head_args):
        head_index, run_top, run_total, run_acc = head_args
        scores = (
            jnp.einsum(
                "qd,kd->qk",
                query_heads[head_index],
                key_heads[:, head_index],
                preferred_element_type=jnp.float32,
            )
            * score_scale
        )
        scores = jnp.where(same_seq, scores, masked_score)
        new_top = jnp.maximum(run_top, jnp.max(scores, axis=1))
        scale_old = jnp.exp(run_top - new_top)
        weights = jnp.exp(scores - new_top[:, None])
        new_total = run_total * scale_old + jnp.sum(weights, axis=1)
        new_acc = run_acc * scale_old[:, None] + jnp.dot(
            weights.astype(jnp.bfloat16),
            value_heads[:, head_index],
            preferred_element_type=jnp.float32,
        )
        return (new_top, new_total, new_acc)

    run_top, run_total, run_acc = lax.map(
        forward_one_head, (jnp.arange(local_heads), start_state[0], start_state[1], start_state[2])
    )
    attended = run_acc / run_total[:, :, None]
    row_lse = run_top + jnp.log(run_total)
    attended_low = (
        jnp.transpose(attended, (1, 0, 2)).reshape(own_rows, local_width).astype(jnp.bfloat16)
    )
    branch = lax.psum(
        jnp.dot(attended_low, out_full, preferred_element_type=jnp.float32).astype(jnp.bfloat16),
        "tp",
    ).astype(jnp.float32)
    first_sum = packed.astype(jnp.float32) + branch + out_bias_full.astype(jnp.float32)
    normed, first_back = jax.vjp(
        layer_norm,
        first_sum,
        first_gain_full.astype(jnp.float32),
        first_shift_full.astype(jnp.float32),
    )
    normed_low = normed.astype(jnp.bfloat16)
    up_out = jnp.dot(normed_low, up_full, preferred_element_type=jnp.float32) + up_bias_full.astype(
        jnp.float32
    )
    activated, gelu_back = jax.vjp(partial(jax.nn.gelu, approximate=False), up_out)
    activated_low = activated.astype(jnp.bfloat16)
    down_out = lax.psum(
        jnp.dot(activated_low, down_full, preferred_element_type=jnp.float32).astype(jnp.bfloat16),
        "tp",
    ).astype(jnp.float32)
    second_sum = normed + down_out + down_bias_full.astype(jnp.float32)
    final, second_back = jax.vjp(
        layer_norm,
        second_sum,
        second_gain_full.astype(jnp.float32),
        second_shift_full.astype(jnp.float32),
    )
    final_low = final.astype(jnp.bfloat16)
    projected = jnp.dot(final_low, proj_full, preferred_element_type=jnp.float32)
    embedded, embed_back = jax.vjp(embed_heads, projected)
    proj_low = embed_back(packed_cot_embed)[0].astype(jnp.bfloat16)
    proj_weight_grad = contract(final_low, proj_low, 0, 0)
    final_grad = packed_cot + contract(proj_low, proj_full, 1, 1)
    second_grad, second_gain_grad, second_shift_grad = second_back(final_grad)
    down_bias_grad = jnp.sum(second_grad, axis=0)
    down_low = second_grad.astype(jnp.bfloat16)
    down_weight_grad = contract(activated_low, down_low, 0, 0)
    up_grad = gelu_back(contract(down_low, down_full, 1, 1))[0]
    up_bias_grad = jnp.sum(up_grad, axis=0)
    up_low = up_grad.astype(jnp.bfloat16)
    up_weight_grad = contract(normed_low, up_low, 0, 0)
    normed_grad = second_grad + lax.psum(
        contract(up_low, up_full, 1, 1).astype(jnp.bfloat16), "tp"
    ).astype(jnp.float32)
    first_grad, first_gain_grad, first_shift_grad = first_back(normed_grad)
    out_bias_grad = jnp.sum(first_grad, axis=0)
    branch_low = first_grad.astype(jnp.bfloat16)
    out_weight_grad = contract(attended_low, branch_low, 0, 0)
    attended_grad = contract(branch_low, out_full, 1, 1).astype(jnp.bfloat16)
    grad_heads = jnp.transpose(attended_grad.reshape(own_rows, local_heads, HEAD_DIM), (1, 0, 2))
    row_delta = jnp.sum(grad_heads.astype(jnp.float32) * attended, axis=2)
    query_grad = jnp.zeros((local_heads, own_rows, HEAD_DIM), jnp.float32)
    key_piece = lax.all_gather(key_low, "ctx", axis=0, tiled=True)
    value_piece = lax.all_gather(value_low, "ctx", axis=0, tiled=True)
    count = key_piece.shape[0]
    backward_same_seq = key_mask(count)
    backward_key_heads = key_piece.reshape(count, local_heads, HEAD_DIM)
    backward_value_heads = value_piece.reshape(count, local_heads, HEAD_DIM)

    def backward_one_head(head_args):
        head_index, head_query_grad = head_args
        query_rows = query_heads[head_index]
        key_rows = backward_key_heads[:, head_index]
        value_rows = backward_value_heads[:, head_index]
        grad_rows = grad_heads[head_index]
        scores = (
            jnp.einsum("qd,kd->qk", query_rows, key_rows, preferred_element_type=jnp.float32)
            * score_scale
        )
        scores = jnp.where(backward_same_seq, scores, masked_score)
        row_probs = jnp.exp(scores - row_lse[head_index][:, None])
        value_grad = contract(row_probs.astype(jnp.bfloat16), grad_rows, 0, 0)
        prob_grad = contract(grad_rows, value_rows, 1, 1)
        score_grad = (row_probs * (prob_grad - row_delta[head_index][:, None])).astype(jnp.bfloat16)
        new_query_grad = head_query_grad + score_scale * jnp.dot(
            score_grad, key_rows, preferred_element_type=jnp.float32
        )
        key_grad = score_scale * contract(score_grad, query_rows, 0, 0)
        return (new_query_grad, key_grad, value_grad)

    new_query_grad, key_grads, value_grads = lax.map(
        backward_one_head, (jnp.arange(local_heads), query_grad)
    )
    key_rows_grad = jnp.transpose(key_grads, (1, 0, 2)).reshape(count, local_width)
    value_rows_grad = jnp.transpose(value_grads, (1, 0, 2)).reshape(count, local_width)
    key_grad_all = key_rows_grad
    value_grad_all = value_rows_grad
    query_grad, key_grad_all, value_grad_all = (new_query_grad, key_grad_all, value_grad_all)
    key_grad, value_grad = (
        lax.psum_scatter(
            key_grad_all.astype(jnp.bfloat16), "ctx", scatter_dimension=0, tiled=True
        ).astype(jnp.float32),
        lax.psum_scatter(
            value_grad_all.astype(jnp.bfloat16), "ctx", scatter_dimension=0, tiled=True
        ).astype(jnp.float32),
    )
    query_pre_grad, key_pre_grad = rope_back(
        (jnp.transpose(query_grad, (1, 0, 2)), key_grad.reshape(own_rows, local_heads, HEAD_DIM))
    )
    mixed_grad = jnp.stack(
        [query_pre_grad, key_pre_grad, value_grad.reshape(own_rows, local_heads, HEAD_DIM)], axis=1
    ).reshape(own_rows, 3, local_width)
    qkv_bias_grad = jnp.sum(mixed_grad, axis=0)
    mixed_low = mixed_grad.astype(jnp.bfloat16)
    qkv_weight_grad = jnp.einsum(
        "td,twe->dwe", packed, mixed_low, preferred_element_type=jnp.float32
    )
    input_grad = first_grad + lax.psum(
        jnp.einsum("twe,dwe->td", mixed_low, qkv_full, preferred_element_type=jnp.float32).astype(
            jnp.bfloat16
        ),
        "tp",
    ).astype(jnp.float32)
    embedded_low = embedded.astype(jnp.bfloat16)
    input_grad_low = input_grad.astype(jnp.bfloat16)
    group_order = lax.all_gather(deal_order, "ctx", axis=0, tiled=True) % group_rows
    inverse_order = (
        jnp.zeros((group_rows,), jnp.int32)
        .at[group_order]
        .set(jnp.arange(group_rows, dtype=jnp.int32))
    )
    chosen_rows = inverse_order[row_ids]
    rows_output, rows_embed, rows_grad = (
        lax.all_gather(final_low, "ctx", axis=0, tiled=True),
        lax.all_gather(embedded_low, "ctx", axis=0, tiled=True),
        lax.all_gather(input_grad_low, "ctx", axis=0, tiled=True),
    )
    ordered_output = rows_output[chosen_rows]
    ordered_embed = rows_embed[chosen_rows]
    ordered_grad = rows_grad[chosen_rows]
    (
        qkv_weight_grad,
        qkv_bias_grad,
        out_weight_grad,
        out_bias_grad,
        first_gain_grad,
        first_shift_grad,
        up_weight_grad,
        up_bias_grad,
        down_weight_grad,
        down_bias_grad,
        second_gain_grad,
        second_shift_grad,
        proj_weight_grad,
    ) = (
        lax.psum_scatter(
            qkv_weight_grad.astype(jnp.bfloat16), "fsdp", scatter_dimension=0, tiled=True
        ).astype(jnp.float32),
        lax.psum_scatter(
            qkv_bias_grad.astype(jnp.bfloat16), "fsdp", scatter_dimension=1, tiled=True
        ).astype(jnp.float32),
        lax.psum_scatter(
            out_weight_grad.astype(jnp.bfloat16), "fsdp", scatter_dimension=0, tiled=True
        ).astype(jnp.float32),
        lax.psum_scatter(
            out_bias_grad.astype(jnp.bfloat16), "fsdp", scatter_dimension=0, tiled=True
        ).astype(jnp.float32),
        lax.psum_scatter(
            first_gain_grad.astype(jnp.bfloat16), "fsdp", scatter_dimension=0, tiled=True
        ).astype(jnp.float32),
        lax.psum_scatter(
            first_shift_grad.astype(jnp.bfloat16), "fsdp", scatter_dimension=0, tiled=True
        ).astype(jnp.float32),
        lax.psum_scatter(
            up_weight_grad.astype(jnp.bfloat16), "fsdp", scatter_dimension=0, tiled=True
        ).astype(jnp.float32),
        lax.psum_scatter(
            up_bias_grad.astype(jnp.bfloat16), "fsdp", scatter_dimension=0, tiled=True
        ).astype(jnp.float32),
        lax.psum_scatter(
            down_weight_grad.astype(jnp.bfloat16), "fsdp", scatter_dimension=0, tiled=True
        ).astype(jnp.float32),
        lax.psum_scatter(
            down_bias_grad.astype(jnp.bfloat16), "fsdp", scatter_dimension=0, tiled=True
        ).astype(jnp.float32),
        lax.psum_scatter(
            second_gain_grad.astype(jnp.bfloat16), "fsdp", scatter_dimension=0, tiled=True
        ).astype(jnp.float32),
        lax.psum_scatter(
            second_shift_grad.astype(jnp.bfloat16), "fsdp", scatter_dimension=0, tiled=True
        ).astype(jnp.float32),
        lax.psum_scatter(
            proj_weight_grad.astype(jnp.bfloat16), "fsdp", scatter_dimension=0, tiled=True
        ).astype(jnp.float32),
    )
    (
        qkv_weight_grad,
        qkv_bias_grad,
        out_weight_grad,
        out_bias_grad,
        first_gain_grad,
        first_shift_grad,
        up_weight_grad,
        up_bias_grad,
        down_weight_grad,
        down_bias_grad,
        second_gain_grad,
        second_shift_grad,
        proj_weight_grad,
    ) = (
        lax.psum(qkv_weight_grad.astype(jnp.bfloat16), "ctx").astype(jnp.float32),
        lax.psum(qkv_bias_grad.astype(jnp.bfloat16), "ctx").astype(jnp.float32),
        lax.psum(out_weight_grad.astype(jnp.bfloat16), "ctx").astype(jnp.float32),
        lax.psum(out_bias_grad.astype(jnp.bfloat16), "ctx").astype(jnp.float32),
        lax.psum(first_gain_grad.astype(jnp.bfloat16), "ctx").astype(jnp.float32),
        lax.psum(first_shift_grad.astype(jnp.bfloat16), "ctx").astype(jnp.float32),
        lax.psum(up_weight_grad.astype(jnp.bfloat16), "ctx").astype(jnp.float32),
        lax.psum(up_bias_grad.astype(jnp.bfloat16), "ctx").astype(jnp.float32),
        lax.psum(down_weight_grad.astype(jnp.bfloat16), "ctx").astype(jnp.float32),
        lax.psum(down_bias_grad.astype(jnp.bfloat16), "ctx").astype(jnp.float32),
        lax.psum(second_gain_grad.astype(jnp.bfloat16), "ctx").astype(jnp.float32),
        lax.psum(second_shift_grad.astype(jnp.bfloat16), "ctx").astype(jnp.float32),
        lax.psum(proj_weight_grad.astype(jnp.bfloat16), "ctx").astype(jnp.float32),
    )
    return (
        ordered_output,
        ordered_embed,
        ordered_grad,
        qkv_weight_grad,
        qkv_bias_grad,
        out_weight_grad,
        out_bias_grad,
        first_gain_grad,
        first_shift_grad,
        up_weight_grad,
        up_bias_grad,
        down_weight_grad,
        down_bias_grad,
        second_gain_grad,
        second_shift_grad,
        proj_weight_grad,
    )


def solution(mesh):
    placed = (
        P(("fsdp", "ctx"), None),
        P("fsdp", None),
        P(("fsdp", "ctx")),
        P("fsdp", None, "tp"),
        P(None, ("tp", "fsdp")),
        P(("tp", "fsdp"), None),
        P("fsdp"),
        P("fsdp"),
        P("fsdp"),
        P("fsdp", "tp"),
        P(("tp", "fsdp")),
        P(("tp", "fsdp"), None),
        P("fsdp"),
        P("fsdp"),
        P("fsdp"),
        P("fsdp", None),
        P(("fsdp", "ctx"), None),
        P(("fsdp", "ctx"), None),
    )
    return jax.shard_map(
        shards,
        mesh=mesh,
        in_specs=placed,
        out_specs=(
            P(("fsdp", "ctx"), None),
            P(("fsdp", "ctx"), None),
            P(("fsdp", "ctx"), None),
            P("fsdp", None, "tp"),
            P(None, ("tp", "fsdp")),
            P(("tp", "fsdp"), None),
            P("fsdp"),
            P("fsdp"),
            P("fsdp"),
            P("fsdp", "tp"),
            P(("tp", "fsdp")),
            P(("tp", "fsdp"), None),
            P("fsdp"),
            P("fsdp"),
            P("fsdp"),
            P("fsdp", None),
        ),
        check_vma=False,
    )
```

profile of v0, /device:TPU:0, one launch (start us, length us, event | category | flops | bytes accessed | tf_op | source)
XLA Modules:
  0.0 1845.9 jit_solution(1386548195076013730)
XLA Ops:
  10.4 12.6 all_gather.70
  24.0 46.6 %all-gather.20.cloned.1.call-done = bf16[4096,1024]{1,0:T(8,128)(2,1)} async-done(((bf16[1024,1024]{1,0:T(8,128)(2,1)}), bf16[4096,1024]{1,0:T(8,128)(2,1)}) %all-gather.20.cloned.1.call-update) | async-done | bytes 8388624 | tf_op jit(solution)/shard_map/all_gather | solution.py:103
  80.1 56.1 %all-gather.22.cloned.1.call-done = bf16[1024,3,512]{0,2,1:T(8,128)(2,1)} async-done(((bf16[256,3,512]{0,2,1:T(8,128)(2,1)}), bf16[1024,3,512]{0,2,1:T(8,128)(2,1)}) %all-gather.22.cloned.1.call-update) | async-done | bytes 3145744 | tf_op jit(solution)/shard_map/all_gather | solution.py:127
  154.3 25.6 %all-gather.24.cloned.1.call-done = bf16[4096,512]{0,1:T(8,128)(2,1)} async-done(((bf16[1024,512]{0,1:T(8,128)(2,1)}), bf16[4096,512]{0,1:T(8,128)(2,1)}) %all-gather.24.cloned.1.call-update) | async-done | bytes 4194320 | tf_op jit(solution)/shard_map/all_gather | solution.py:168
  179.8 36.5 %all-gather.26.cloned.1.call-done = bf16[4096,512]{0,1:T(8,128)(2,1)} async-done(((bf16[1024,512]{0,1:T(8,128)(2,1)}), bf16[4096,512]{0,1:T(8,128)(2,1)}) %all-gather.26.cloned.1.call-update) | async-done | bytes 4194320 | tf_op jit(solution)/shard_map/all_gather | solution.py:169
  217.9 140.4 %while.30 = (s32[]{:T(128)}, f32[8,1024]{1,0:T(8,128)S(1)}, f32[8,1024]{1,0:T(8,128)S(1)}, f32[8,1024,64]{1,2,0:T(8,128)}, s32[8]{0:T(128)S(1)}, /*index=5*/bf16...) while((s32[]{:T(128)}, f32[8,1024]{1,0:T(8,128)S(1)}, ...), condition=%wide.region_7.8_spmd.clone, body=%wide.region_4.7_spmd.clone.sunk | while | flops 1132531712 | bytes 52029112 | solution.py:198
  367.9 10.9 all-gather
  396.1 12.0 all-gather.3
  408.1 19.5 %all-reduce.23.cloned.1.call-done = bf16[1024,1024]{1,0:T(8,128)(2,1)} async-done(((bf16[1024,1024]{1,0:T(8,128)(2,1)}), bf16[1024,1024]{1,0:T(8,128)(2,1)}) %all-reduce.23.cloned.1.call-update) | async-done | bytes 2097168 | tf_op jit(solution)/shard_map/psum | solution.py:206
  431.2 78.8 %all-gather.30.cloned.1.call-done = bf16[1024,2048]{1,0:T(8,128)(2,1)} async-done(((bf16[256,2048]{1,0:T(8,128)(2,1)}), bf16[1024,2048]{1,0:T(8,128)(2,1)}) %all-gather.30.cloned.1.call-update) | async-done | bytes 4194320 | tf_op jit(solution)/shard_map/all_gather | solution.py:133
  510.0 28.1 %multiply_convert_fusion.1 = (bf16[1024,2048]{1,0:T(8,128)(2,1)}, f32[1024,2048]{1,0:T(8,128)}, f32[1024,2048]{1,0:T(8,128)}) fusion(f32[2048]{0:T(1024)S(1)} %bitcast.224, bf16[1024,2048]{1,0:T(8,128)(2,1)} %all-gather.30.cloned.1.call-done, f32[1024]{0:T(1024)S(1)} %bitcast.216, f32[1024]{0:T(1024)S(1)} %bitcast.207, f32[1024]{0:T(1024)S(1)} %fusion.92, ...), kind=kOutput, calls=%fused_computation.72 | convolution fusion | flops 4442816512 | bytes 29388800 | tf_op jit(solution)/shard_map/dot_general | solution.py:218
  538.1 52.9 %all-gather.32.cloned.1.call-done = bf16[2048,1024]{1,0:T(8,128)(2,1)} async-done(((bf16[512,1024]{1,0:T(8,128)(2,1)}), bf16[2048,1024]{1,0:T(8,128)(2,1)}) %all-gather.32.cloned.1.call-update) | async-done | bytes 4194320 | tf_op jit(solution)/shard_map/all_gather | solution.py:135
  625.8 17.0 all_gather.85
  651.2 29.0 %all-gather.38.cloned.1.call-done = bf16[4096,1024]{1,0:T(8,128)(2,1)} async-done(((bf16[1024,1024]{1,0:T(8,128)(2,1)}), bf16[4096,1024]{1,0:T(8,128)(2,1)}) %all-gather.38.cloned.1.call-update) | async-done | bytes 8388624 | tf_op jit(solution)/shard_map/all_gather | solution.py:104
  680.1 10.5 gather_fusion.4
  690.6 55.5 %all-reduce.25.cloned.1.call-done = bf16[1024,1024]{1,0:T(8,128)(2,1)} async-done(((bf16[1024,1024]{1,0:T(8,128)(2,1)}), bf16[1024,1024]{1,0:T(8,128)(2,1)}) %all-reduce.25.cloned.1.call-update) | async-done | bytes 2097168 | tf_op jit(solution)/shard_map/psum | solution.py:223
  764.6 16.3 fusion.108
  788.9 63.0 %all-reduce.27.cloned.1.call-done = bf16[1024,1024]{1,0:T(8,128)(2,1)} async-done(((bf16[1024,1024]{1,0:T(8,128)(2,1)}), bf16[1024,1024]{1,0:T(8,128)(2,1)}) %all-reduce.27.cloned.1.call-update) | async-done | bytes 2097168 | tf_op jit(solution)/shard_map/psum | solution.py:248
  863.6 293.8 %while.31 = (s32[]{:T(128)}, f32[8,1024,64]{1,2,0:T(8,128)S(1)}, bf16[8,4096,64]{1,2,0:T(8,128)(2,1)}, bf16[8,4096,64]{1,2,0:T(8,128)(2,1)}, s32[8]{0:T(128)S(1)...) while((s32[]{:T(128)}, f32[8,1024,64]{1,2,0:T(8,128)S(1)}, ...), condition=%wide.region_28.29_spmd.clone, body=%wide.region_27.28_spmd.clone.sunk | while | flops 2735013888 | bytes 80289496 | solution.py:287
  1175.2 10.8 convolution_convert_fusion
  1213.3 35.6 %reduce-scatter.13.cloned.1.call-done = bf16[1024,512]{1,0:T(8,128)(2,1)} async-done(((bf16[4096,512]{1,0:T(8,128)(2,1)}), bf16[1024,512]{1,0:T(8,128)(2,1)}) %reduce-scatter.13.cloned.1.call-update) | async-done | bytes 1048592 | tf_op jit(solution)/shard_map/reduce_scatter | solution.py:299
  1273.8 27.8 %reduce-scatter.17.cloned.1.call-done = bf16[128,1024]{1,0:T(8,128)(2,1)} async-done(((bf16[512,1024]{1,0:T(8,128)(2,1)}), bf16[128,1024]{1,0:T(8,128)(2,1)}) %reduce-scatter.17.cloned.1.call-update) | async-done | bytes 262160 | tf_op jit(solution)/shard_map/reduce_scatter | solution.py:358
  1301.6 77.6 %reduce-scatter.21.cloned.1.call-done = bf16[512,1024]{1,0:T(8,128)(2,1)} async-done(((bf16[2048,1024]{1,0:T(8,128)(2,1)}), bf16[512,1024]{1,0:T(8,128)(2,1)}) %reduce-scatter.21.cloned.1.call-update) | async-done | bytes 1048592 | tf_op jit(solution)/shard_map/reduce_scatter | solution.py:376
  1379.2 79.5 %reduce-scatter.19.cloned.1.call-done = bf16[256,2048]{1,0:T(8,128)(2,1)} async-done(((bf16[1024,2048]{1,0:T(8,128)(2,1)}), bf16[256,2048]{1,0:T(8,128)(2,1)}) %reduce-scatter.19.cloned.1.call-update) | async-done | bytes 1048592 | tf_op jit(solution)/shard_map/reduce_scatter | solution.py:370
  1458.7 63.1 %reduce-scatter.15.cloned.1.call-done = bf16[256,3,512]{2,0,1:T(8,128)(2,1)} async-done(((bf16[1024,3,512]{2,0,1:T(8,128)(2,1)}), bf16[256,3,512]{2,0,1:T(8,128)(2,1)}) %reduce-scatter.15.cloned.1.call-update) | async-done | bytes 786448 | tf_op jit(solution)/shard_map/reduce_scatter | solution.py:352
  1521.9 65.0 %all-reduce.29.cloned.1.call-done = bf16[1024,1024]{1,0:T(8,128)(2,1)} async-done(((bf16[1024,1024]{1,0:T(8,128)(2,1)}), bf16[1024,1024]{1,0:T(8,128)(2,1)}) %all-reduce.29.cloned.1.call-update) | async-done | bytes 2097168 | tf_op jit(solution)/shard_map/psum | solution.py:314
  1599.0 15.5 scatter_custom_fusion
  1636.2 15.9 all-reduce.16
  1663.9 30.4 %all-gather.34.cloned.1.call-done = bf16[4096,1024]{1,0:T(8,128)(2,1)} async-done(((bf16[1024,1024]{1,0:T(8,128)(2,1)}), bf16[4096,1024]{1,0:T(8,128)(2,1)}) %all-gather.34.cloned.1.call-update) | async-done | bytes 8388624 | tf_op jit(solution)/shard_map/all_gather | solution.py:330
  1694.3 10.5 gather_fusion.2
  1704.8 63.9 %all-reduce.31.cloned.1.call-done = (bf16[256,3,512]{2,0,1:T(8,128)(2,1)}, bf16[128,1024]{1,0:T(8,128)(2,1)}, bf16[256,2048]{1,0:T(8,128)(2,1)}, bf16[512,1024]{1,0:T(8,128)(2,1)}, bf16[256,288]{0,1:T(8,128)(2,1)}) async-done(((bf16[256,3,512]{2,0,1:T(8,128)(2,1)}, bf16[128,1024]{1,0:T(8,128)(2,1)}, bf16[256,2048]{1,0:T(8,128)(2,1)}, bf16[512,1024]{1,0:T(8,128)(2,1)}, bf16[256,288]{0,1:T(8,128)(2,1)}), ...) | async-done | bytes 3293200 | tf_op jit(solution)/shard_map/psum | solution.py:407
  1777.3 51.4 %all-gather.42.cloned.1.call-done = bf16[4096,1024]{1,0:T(8,128)(2,1)} async-done(((bf16[1024,1024]{1,0:T(8,128)(2,1)}), bf16[4096,1024]{1,0:T(8,128)(2,1)}) %all-gather.42.cloned.1.call-update) | async-done | bytes 8388624 | tf_op jit(solution)/shard_map/all_gather | solution.py:332
  (465 shorter events, 679.3 us)
Async XLA Ops:
  7.2 63.4 %all-gather.20.cloned.1.call-start = ((), (), s32[]{:S(2)}) async-start(), calls=%async_computation.8 | async-start | bytes 10485760 | tf_op jit(solution)/shard_map/all_gather | solution.py:103
  7.9 128.3 %all-gather.22.cloned.1.call-start = ((), (), s32[]{:S(2)}) async-start(), calls=%async_computation.9 | async-start | bytes 3932160 | tf_op jit(solution)/shard_map/all_gather | solution.py:127
  10.3 169.5 %all-gather.24.cloned.1.call-start = ((), (), s32[]{:S(2)}) async-start(), calls=%async_computation.10 | async-start | bytes 5242880 | tf_op jit(solution)/shard_map/all_gather | solution.py:168
  24.0 120.3 %copy-start.18 = (f32[1024,32]{0,1:T(8,128)}, f32[1024,32]{0,1:T(8,128)S(1)}, u32[]{:S(2)}) copy-start(f32[1024,32]{0,1:T(8,128)S(1)} %get-tuple-element.460) | copy-start | bytes 393220
  80.1 778.5 %copy-start = (bf16[1024,1024]{1,0:T(8,128)(2,1)}, bf16[1024,1024]{1,0:T(8,128)(2,1)S(1)}, u32[]{:S(2)}) copy-start(bf16[1024,1024]{1,0:T(8,128)(2,1)S(1)} %gather_fusion) | copy-start | bytes 6291460
  147.0 69.3 %all-gather.26.cloned.1.call-start = ((), (), s32[]{:S(2)}) async-start(), calls=%async_computation.11 | async-start | bytes 5242880 | tf_op jit(solution)/shard_map/all_gather | solution.py:169
  149.8 210.4 %all-gather.28.cloned.1.call-start = ((), (), s32[]{:S(2)}) async-start(), calls=%async_computation.12 | async-start | bytes 1310720 | tf_op jit(solution)/shard_map/all_gather | solution.py:129
  150.4 277.2 %all-reduce.23.cloned.1.call-start = ((), (), s32[]{:S(2)}) async-start(), calls=%async_computation.13 | async-start | bytes 4194304 | tf_op jit(solution)/shard_map/psum | solution.py:206
  364.5 145.5 %all-gather.30.cloned.1.call-start = ((), (), s32[]{:S(2)}) async-start(), calls=%async_computation.14 | async-start | bytes 5242880 | tf_op jit(solution)/shard_map/all_gather | solution.py:133
  365.3 225.7 %all-gather.32.cloned.1.call-start = ((), (), s32[]{:S(2)}) async-start(), calls=%async_computation.15 | async-start | bytes 5242880 | tf_op jit(solution)/shard_map/all_gather | solution.py:135
  366.0 276.8 %all-gather.40.cloned.1.call-start = ((), (), s32[]{:S(2)}) async-start(), calls=%async_computation.20 | async-start | bytes 3932160 | tf_op jit(solution)/shard_map/all_gather | solution.py:105
  367.3 312.9 %all-gather.38.cloned.1.call-start = ((), (), s32[]{:S(2)}) async-start(), calls=%async_computation.19 | async-start | bytes 10485760 | tf_op jit(solution)/shard_map/all_gather | solution.py:104
  367.9 378.2 %all-reduce.25.cloned.1.call-start = ((), (), s32[]{:S(2)}) async-start(), calls=%async_computation.16 | async-start | bytes 4194304 | tf_op jit(solution)/shard_map/psum | solution.py:223
  378.8 479.8 %copy-start.42 = (f32[4,1,256]{2,1,0:T(1,128)}, f32[4,1,256]{2,1,0:T(1,128)S(1)}, u32[]{:S(2)}) copy-start(f32[4,1,256]{2,1,0:T(1,128)S(1)} %convert_element_type.329) | copy-start | bytes 12292
  386.4 472.2 %copy-start.46 = (f32[4,1,256]{2,1,0:T(1,128)}, f32[4,1,256]{2,1,0:T(1,128)S(1)}, u32[]{:S(2)}) copy-start(f32[4,1,256]{2,1,0:T(1,128)S(1)} %convert_element_type.330) | copy-start | bytes 12292
  396.0 350.0 %copy-start.56 = (f32[4,1,256]{2,1,0:T(1,128)}, f32[4,1,256]{2,1,0:T(1,128)S(1)}, u32[]{:S(2)}) copy-start(f32[4,1,256]{2,1,0:T(1,128)S(1)} %convert_element_type.331) | copy-start | bytes 12292
  430.1 428.5 %copy-start.44 = (f32[1024]{0:T(1024)}, f32[1024]{0:T(1024)S(1)}, u32[]{:S(2)}) copy-start(f32[1024]{0:T(1024)S(1)} %broadcast_multiply_fusion.1) | copy-start | bytes 12292
  431.2 427.4 %copy-start.48 = (f32[1024]{0:T(1024)}, f32[1024]{0:T(1024)S(1)}, u32[]{:S(2)}) copy-start(f32[1024]{0:T(1024)S(1)} %fusion.92) | copy-start | bytes 12292
  600.4 251.5 %all-reduce.27.cloned.1.call-start = ((), (), s32[]{:S(2)}) async-start(), calls=%async_computation.21 | async-start | bytes 4194304 | tf_op jit(solution)/shard_map/psum | solution.py:248
  788.8 413.2 %reduce-scatter.11.cloned.1.call-start = ((), (), s32[]{:S(2)}) async-start(), calls=%async_computation.22 | async-start | bytes 5242880 | tf_op jit(solution)/shard_map/reduce_scatter | solution.py:296
  1157.4 91.6 %reduce-scatter.13.cloned.1.call-start = ((), (), s32[]{:S(2)}) async-start(), calls=%async_computation.23 | async-start | bytes 5242880 | tf_op jit(solution)/shard_map/reduce_scatter | solution.py:299
  1165.3 108.5 %reduce-scatter.23.cloned.1.call-start = ((), (), s32[]{:S(2)}) async-start(), calls=%async_computation.30 | async-start | bytes 737280 | tf_op jit(solution)/shard_map/reduce_scatter | solution.py:388
  1170.4 131.2 %reduce-scatter.17.cloned.1.call-start = ((), (), s32[]{:S(2)}) async-start(), calls=%async_computation.27 | async-start | bytes 1310720 | tf_op jit(solution)/shard_map/reduce_scatter | solution.py:358
  1175.2 204.0 %reduce-scatter.21.cloned.1.call-start = ((), (), s32[]{:S(2)}) async-start(), calls=%async_computation.29 | async-start | bytes 5242880 | tf_op jit(solution)/shard_map/reduce_scatter | solution.py:376
  1186.1 272.7 %reduce-scatter.19.cloned.1.call-start = ((), (), s32[]{:S(2)}) async-start(), calls=%async_computation.28 | async-start | bytes 5242880 | tf_op jit(solution)/shard_map/reduce_scatter | solution.py:370
  1197.5 324.3 %reduce-scatter.15.cloned.1.call-start = ((), (), s32[]{:S(2)}) async-start(), calls=%async_computation.26 | async-start | bytes 3932160 | tf_op jit(solution)/shard_map/reduce_scatter | solution.py:352
  1259.0 327.9 %all-reduce.29.cloned.1.call-start = ((), (), s32[]{:S(2)}) async-start(), calls=%async_computation.24 | async-start | bytes 4194304 | tf_op jit(solution)/shard_map/psum | solution.py:314
  1267.7 353.1 %all-gather.36.cloned.1.call-start = ((), (), s32[]{:S(2)}) async-start(), calls=%async_computation.18 | async-start | bytes 2949120 | tf_op jit(solution)/shard_map/all_gather | solution.py:331
  1268.6 366.7 %reduce-scatter.25.cloned.1.call-start = ((), (), s32[]{:S(2)}) async-start(), calls=%async_computation.31 | async-start | bytes 163840
  1273.0 421.3 %all-gather.34.cloned.1.call-start = ((), (), s32[]{:S(2)}) async-start(), calls=%async_computation.17 | async-start | bytes 10485760 | tf_op jit(solution)/shard_map/all_gather | solution.py:330
  1273.8 494.9 %all-reduce.31.cloned.1.call-start = ((), (), s32[]{:S(2)}) async-start(), calls=%async_computation.32 | async-start | bytes 6586368 | tf_op jit(solution)/shard_map/psum | solution.py:407
  1521.9 306.8 %all-gather.42.cloned.1.call-start = ((), (), s32[]{:S(2)}) async-start(), calls=%async_computation.25 | async-start | bytes 10485760 | tf_op jit(solution)/shard_map/all_gather | solution.py:332
  (70 other events, 943.9 us)
Sparse Core Ops, SparseCore 0:
  9.6 60.9 all-gather.19
  72.8 63.4 all-gather.21
  147.1 32.6 all-gather.23
  181.8 34.4 all-gather.25
  217.7 27.9 all-gather.27
  364.7 62.8 all-reduce.22
  429.2 80.7 all-gather.29
  511.7 79.2 all-gather.31
  593.2 27.0 all-gather.39
  621.8 58.2 all-gather.37
  683.1 62.9 all-reduce.24
  789.0 62.9 all-reduce.26
  1157.5 44.4 reduce-scatter.10
  1204.4 44.4 reduce-scatter.12
  1251.2 21.9 reduce-scatter.22
  1276.0 25.5 reduce-scatter.16
  1303.7 75.4 reduce-scatter.20
  1381.4 77.2 reduce-scatter.18
  1461.0 60.7 reduce-scatter.14
  1524.0 62.9 all-reduce.28
  1589.2 24.0 all-gather.35
  1616.2 19.1 reduce-scatter.24
  1637.5 56.7 all-gather.33
  1696.9 71.7 all-reduce.30
  1770.3 58.3 all-gather.41
where the time goes:
time: 1850 us
  waiting for transfers between devices  970 us (52%)
  matrix products  475 us (26%)
  local copies, waits for them, and re-layouts  129 us (7%)
  blocking collectives  123 us (7%)
  other arithmetic  97.9 us (5%)
  loops' own time  31.8 us (2%)
    dot_general x32, matrix products, contract(): lax.dot_general(left, right, (((left_dim,), (right_dim,)), ((), ())), pre...  226 us
    reduce_scatter x1, waiting for transfers between devices, shards(): lax.psum_scatter(up_weight_grad.astype(jnp.bfloat16), 'fsdp', scatter_dim...  79.5 us
    all_gather x1, waiting for transfers between devices, shards(): lax.all_gather(up_weight, 'fsdp', axis=0, tiled=True)  78.8 us
    reduce_scatter x1, waiting for transfers between devices, shards(): lax.psum_scatter(down_weight_grad.astype(jnp.bfloat16), 'fsdp', scatter_d...  77.6 us
    dot_general x8, matrix products, backward_one_head(): jnp.einsum('qd,kd->qk', query_rows, key_rows, preferred_element_type=jnp....  73.6 us
    psum x1, waiting for transfers between devices, shards(): lax.psum(jnp.einsum('twe,dwe->td', mixed_low, qkv_full, preferred_element...  65 us
    psum x1, waiting for transfers between devices, shards(): lax.psum(qkv_weight_grad.astype(jnp.bfloat16), 'ctx').astype(jnp.float32)  63.9 us
    reduce_scatter x1, waiting for transfers between devices, shards(): lax.psum_scatter(qkv_weight_grad.astype(jnp.bfloat16), 'fsdp', scatter_di...  63.1 us
  transfers between devices with their start and end apart: 25, of which 21 were waited for; matrix products, arithmetic and copies ran while one was open for 18% of the time, Pallas kernels for 0%

commit v1 on v0

--- a/solution.py
+++ b/solution.py
@@ -47,7 +47,9 @@
 
 
 def sequence_layout(seq_lengths, row_ids):
-    seq_ends = jnp.cumsum(seq_lengths)
+    seq_index = jnp.arange(seq_lengths.shape[0], dtype=jnp.int32)
+    up_to = (seq_index[None, :] <= seq_index[:, None]).astype(jnp.int32)
+    seq_ends = jnp.sum(up_to * seq_lengths[None, :], axis=1)
     segment = jnp.sum((row_ids[:, None] >= seq_ends[None, :]).astype(jnp.int32), axis=1)
     seq_starts = seq_ends - seq_lengths
     picked = (

time: 1850 us -> 1850 us (level)
  no operation moved by 1% of the time
where the time goes in v1:
time: 1850 us
  waiting for transfers between devices  970 us (52%)
  matrix products  475 us (26%)
  local copies, waits for them, and re-layouts  129 us (7%)
  blocking collectives  123 us (7%)
  other arithmetic  97.9 us (5%)
  loops' own time  31.8 us (2%)
    dot_general x32, matrix products, contract(): lax.dot_general(left, right, (((left_dim,), (right_dim,)), ((), ())), pre...  226 us
    reduce_scatter x1, waiting for transfers between devices, shards(): lax.psum_scatter(up_weight_grad.astype(jnp.bfloat16), 'fsdp', scatter_dim...  79.5 us
    all_gather x1, waiting for transfers between devices, shards(): lax.all_gather(up_weight, 'fsdp', axis=0, tiled=True)  78.8 us
    reduce_scatter x1, waiting for transfers between devices, shards(): lax.psum_scatter(down_weight_grad.astype(jnp.bfloat16), 'fsdp', scatter_d...  77.6 us
    dot_general x8, matrix products, backward_one_head(): jnp.einsum('qd,kd->qk', query_rows, key_rows, preferred_element_type=jnp....  73.6 us
    psum x1, waiting for transfers between devices, shards(): lax.psum(jnp.einsum('twe,dwe->td', mixed_low, qkv_full, preferred_element...  65 us
    psum x1, waiting for transfers between devices, shards(): lax.psum(qkv_weight_grad.astype(jnp.bfloat16), 'ctx').astype(jnp.float32)  63.9 us
    reduce_scatter x1, waiting for transfers between devices, shards(): lax.psum_scatter(qkv_weight_grad.astype(jnp.bfloat16), 'fsdp', scatter_di...  63.1 us
  transfers between devices with their start and end apart: 25, of which 21 were waited for; matrix products, arithmetic and copies ran while one was open for 18% of the time, Pallas kernels for 0%

profile of v1, /device:TPU:0, one launch (start us, length us, event | category | flops | bytes accessed | tf_op | source)
XLA Modules:
  0.0 1845.9 jit_solution(16464783705978330907)
XLA Ops:
  10.4 12.6 all_gather.70
  23.9 46.7 %all-gather.20.cloned.1.call-done = bf16[4096,1024]{1,0:T(8,128)(2,1)} async-done(((bf16[1024,1024]{1,0:T(8,128)(2,1)}), bf16[4096,1024]{1,0:T(8,128)(2,1)}) %all-gather.20.cloned.1.call-update) | async-done | bytes 8388624 | tf_op jit(solution)/shard_map/all_gather | solution.py:105
  80.1 56.2 %all-gather.22.cloned.1.call-done = bf16[1024,3,512]{0,2,1:T(8,128)(2,1)} async-done(((bf16[256,3,512]{0,2,1:T(8,128)(2,1)}), bf16[1024,3,512]{0,2,1:T(8,128)(2,1)}) %all-gather.22.cloned.1.call-update) | async-done | bytes 3145744 | tf_op jit(solution)/shard_map/all_gather | solution.py:129
  154.3 25.6 %all-gather.24.cloned.1.call-done = bf16[4096,512]{0,1:T(8,128)(2,1)} async-done(((bf16[1024,512]{0,1:T(8,128)(2,1)}), bf16[4096,512]{0,1:T(8,128)(2,1)}) %all-gather.24.cloned.1.call-update) | async-done | bytes 4194320 | tf_op jit(solution)/shard_map/all_gather | solution.py:170
  179.9 36.5 %all-gather.26.cloned.1.call-done = bf16[4096,512]{0,1:T(8,128)(2,1)} async-done(((bf16[1024,512]{0,1:T(8,128)(2,1)}), bf16[4096,512]{0,1:T(8,128)(2,1)}) %all-gather.26.cloned.1.call-update) | async-done | bytes 4194320 | tf_op jit(solution)/shard_map/all_gather | solution.py:171
  218.0 140.4 %while.30 = (s32[]{:T(128)}, f32[8,1024]{1,0:T(8,128)S(1)}, f32[8,1024]{1,0:T(8,128)S(1)}, f32[8,1024,64]{1,2,0:T(8,128)}, s32[8]{0:T(128)S(1)}, /*index=5*/bf16...) while((s32[]{:T(128)}, f32[8,1024]{1,0:T(8,128)S(1)}, ...), condition=%wide.region_7.8_spmd.clone, body=%wide.region_4.0_spmd.clone.sunk | while | flops 1132531712 | bytes 52029112 | solution.py:200
  368.0 10.9 all-gather
  396.1 12.0 all-gather.3
  408.2 19.5 %all-reduce.23.cloned.1.call-done = bf16[1024,1024]{1,0:T(8,128)(2,1)} async-done(((bf16[1024,1024]{1,0:T(8,128)(2,1)}), bf16[1024,1024]{1,0:T(8,128)(2,1)}) %all-reduce.23.cloned.1.call-update) | async-done | bytes 2097168 | tf_op jit(solution)/shard_map/psum | solution.py:208
  431.2 78.8 %all-gather.30.cloned.1.call-done = bf16[1024,2048]{1,0:T(8,128)(2,1)} async-done(((bf16[256,2048]{1,0:T(8,128)(2,1)}), bf16[1024,2048]{1,0:T(8,128)(2,1)}) %all-gather.30.cloned.1.call-update) | async-done | bytes 4194320 | tf_op jit(solution)/shard_map/all_gather | solution.py:135
  510.1 28.1 %multiply_convert_fusion.1 = (bf16[1024,2048]{1,0:T(8,128)(2,1)}, f32[1024,2048]{1,0:T(8,128)}, f32[1024,2048]{1,0:T(8,128)}) fusion(f32[2048]{0:T(1024)S(1)} %bitcast.223, bf16[1024,2048]{1,0:T(8,128)(2,1)} %all-gather.30.cloned.1.call-done, f32[1024]{0:T(1024)S(1)} %bitcast.215, f32[1024]{0:T(1024)S(1)} %bitcast.206, f32[1024]{0:T(1024)S(1)} %fusion.92, ...), kind=kOutput, calls=%fused_computation.72 | convolution fusion | flops 4442816512 | bytes 29388800 | tf_op jit(solution)/shard_map/dot_general | solution.py:220
  538.2 52.9 %all-gather.32.cloned.1.call-done = bf16[2048,1024]{1,0:T(8,128)(2,1)} async-done(((bf16[512,1024]{1,0:T(8,128)(2,1)}), bf16[2048,1024]{1,0:T(8,128)(2,1)}) %all-gather.32.cloned.1.call-update) | async-done | bytes 4194320 | tf_op jit(solution)/shard_map/all_gather | solution.py:137
  625.9 17.0 all_gather.85
  651.2 29.0 %all-gather.38.cloned.1.call-done = bf16[4096,1024]{1,0:T(8,128)(2,1)} async-done(((bf16[1024,1024]{1,0:T(8,128)(2,1)}), bf16[4096,1024]{1,0:T(8,128)(2,1)}) %all-gather.38.cloned.1.call-update) | async-done | bytes 8388624 | tf_op jit(solution)/shard_map/all_gather | solution.py:106
  680.2 10.5 gather_fusion.4
  690.7 55.5 %all-reduce.25.cloned.1.call-done = bf16[1024,1024]{1,0:T(8,128)(2,1)} async-done(((bf16[1024,1024]{1,0:T(8,128)(2,1)}), bf16[1024,1024]{1,0:T(8,128)(2,1)}) %all-reduce.25.cloned.1.call-update) | async-done | bytes 2097168 | tf_op jit(solution)/shard_map/psum | solution.py:225
  764.6 16.3 fusion.109
  789.0 63.0 %all-reduce.27.cloned.1.call-done = bf16[1024,1024]{1,0:T(8,128)(2,1)} async-done(((bf16[1024,1024]{1,0:T(8,128)(2,1)}), bf16[1024,1024]{1,0:T(8,128)(2,1)}) %all-reduce.27.cloned.1.call-update) | async-done | bytes 2097168 | tf_op jit(solution)/shard_map/psum | solution.py:250
  863.7 293.8 %while.31 = (s32[]{:T(128)}, f32[8,1024,64]{1,2,0:T(8,128)S(1)}, bf16[8,4096,64]{1,2,0:T(8,128)(2,1)}, bf16[8,4096,64]{1,2,0:T(8,128)(2,1)}, s32[8]{0:T(128)S(1)...) while((s32[]{:T(128)}, f32[8,1024,64]{1,2,0:T(8,128)S(1)}, ...), condition=%wide.region_28.29_spmd.clone, body=%wide.region_27.28_spmd.clone.sunk | while | flops 2735013888 | bytes 80289496 | solution.py:289
  1175.3 10.8 convolution_convert_fusion
  1213.4 35.6 %reduce-scatter.13.cloned.1.call-done = bf16[1024,512]{1,0:T(8,128)(2,1)} async-done(((bf16[4096,512]{1,0:T(8,128)(2,1)}), bf16[1024,512]{1,0:T(8,128)(2,1)}) %reduce-scatter.13.cloned.1.call-update) | async-done | bytes 1048592 | tf_op jit(solution)/shard_map/reduce_scatter | solution.py:301
  1273.9 27.8 %reduce-scatter.17.cloned.1.call-done = bf16[128,1024]{1,0:T(8,128)(2,1)} async-done(((bf16[512,1024]{1,0:T(8,128)(2,1)}), bf16[128,1024]{1,0:T(8,128)(2,1)}) %reduce-scatter.17.cloned.1.call-update) | async-done | bytes 262160 | tf_op jit(solution)/shard_map/reduce_scatter | solution.py:360
  1301.7 77.6 %reduce-scatter.21.cloned.1.call-done = bf16[512,1024]{1,0:T(8,128)(2,1)} async-done(((bf16[2048,1024]{1,0:T(8,128)(2,1)}), bf16[512,1024]{1,0:T(8,128)(2,1)}) %reduce-scatter.21.cloned.1.call-update) | async-done | bytes 1048592 | tf_op jit(solution)/shard_map/reduce_scatter | solution.py:378
  1379.2 79.5 %reduce-scatter.19.cloned.1.call-done = bf16[256,2048]{1,0:T(8,128)(2,1)} async-done(((bf16[1024,2048]{1,0:T(8,128)(2,1)}), bf16[256,2048]{1,0:T(8,128)(2,1)}) %reduce-scatter.19.cloned.1.call-update) | async-done | bytes 1048592 | tf_op jit(solution)/shard_map/reduce_scatter | solution.py:372
  1458.8 63.1 %reduce-scatter.15.cloned.1.call-done = bf16[256,3,512]{2,0,1:T(8,128)(2,1)} async-done(((bf16[1024,3,512]{2,0,1:T(8,128)(2,1)}), bf16[256,3,512]{2,0,1:T(8,128)(2,1)}) %reduce-scatter.15.cloned.1.call-update) | async-done | bytes 786448 | tf_op jit(solution)/shard_map/reduce_scatter | solution.py:354
  1522.0 65.0 %all-reduce.29.cloned.1.call-done = bf16[1024,1024]{1,0:T(8,128)(2,1)} async-done(((bf16[1024,1024]{1,0:T(8,128)(2,1)}), bf16[1024,1024]{1,0:T(8,128)(2,1)}) %all-reduce.29.cloned.1.call-update) | async-done | bytes 2097168 | tf_op jit(solution)/shard_map/psum | solution.py:316
  1599.1 15.5 scatter_custom_fusion
  1636.3 15.9 all-reduce.16
  1663.9 30.4 %all-gather.34.cloned.1.call-done = bf16[4096,1024]{1,0:T(8,128)(2,1)} async-done(((bf16[1024,1024]{1,0:T(8,128)(2,1)}), bf16[4096,1024]{1,0:T(8,128)(2,1)}) %all-gather.34.cloned.1.call-update) | async-done | bytes 8388624 | tf_op jit(solution)/shard_map/all_gather | solution.py:332
  1704.8 63.9 %all-reduce.31.cloned.1.call-done = (bf16[256,3,512]{2,0,1:T(8,128)(2,1)}, bf16[128,1024]{1,0:T(8,128)(2,1)}, bf16[256,2048]{1,0:T(8,128)(2,1)}, bf16[512,1024]{1,0:T(8,128)(2,1)}, bf16[256,288]{0,1:T(8,128)(2,1)}) async-done(((bf16[256,3,512]{2,0,1:T(8,128)(2,1)}, bf16[128,1024]{1,0:T(8,128)(2,1)}, bf16[256,2048]{1,0:T(8,128)(2,1)}, bf16[512,1024]{1,0:T(8,128)(2,1)}, bf16[256,288]{0,1:T(8,128)(2,1)}), ...) | async-done | bytes 3293200 | tf_op jit(solution)/shard_map/psum | solution.py:409
  1777.4 51.4 %all-gather.42.cloned.1.call-done = bf16[4096,1024]{1,0:T(8,128)(2,1)} async-done(((bf16[1024,1024]{1,0:T(8,128)(2,1)}), bf16[4096,1024]{1,0:T(8,128)(2,1)}) %all-gather.42.cloned.1.call-update) | async-done | bytes 8388624 | tf_op jit(solution)/shard_map/all_gather | solution.py:334
  1828.7 10.5 gather_fusion.6
  (465 shorter events, 679.2 us)
Async XLA Ops:
  7.2 63.4 %all-gather.20.cloned.1.call-start = ((), (), s32[]{:S(2)}) async-start(), calls=%async_computation.8 | async-start | bytes 10485760 | tf_op jit(solution)/shard_map/all_gather | solution.py:105
  7.9 128.3 %all-gather.22.cloned.1.call-start = ((), (), s32[]{:S(2)}) async-start(), calls=%async_computation.9 | async-start | bytes 3932160 | tf_op jit(solution)/shard_map/all_gather | solution.py:129
  10.3 169.6 %all-gather.24.cloned.1.call-start = ((), (), s32[]{:S(2)}) async-start(), calls=%async_computation.10 | async-start | bytes 5242880 | tf_op jit(solution)/shard_map/all_gather | solution.py:170
  23.9 120.4 %copy-start.18 = (f32[1024,32]{0,1:T(8,128)}, f32[1024,32]{0,1:T(8,128)S(1)}, u32[]{:S(2)}) copy-start(f32[1024,32]{0,1:T(8,128)S(1)} %get-tuple-element.460) | copy-start | bytes 393220
  80.1 778.6 %copy-start = (bf16[1024,1024]{1,0:T(8,128)(2,1)}, bf16[1024,1024]{1,0:T(8,128)(2,1)S(1)}, u32[]{:S(2)}) copy-start(bf16[1024,1024]{1,0:T(8,128)(2,1)S(1)} %gather_fusion) | copy-start | bytes 6291460
  147.0 69.3 %all-gather.26.cloned.1.call-start = ((), (), s32[]{:S(2)}) async-start(), calls=%async_computation.11 | async-start | bytes 5242880 | tf_op jit(solution)/shard_map/all_gather | solution.py:171
  149.8 210.5 %all-gather.28.cloned.1.call-start = ((), (), s32[]{:S(2)}) async-start(), calls=%async_computation.12 | async-start | bytes 1310720 | tf_op jit(solution)/shard_map/all_gather | solution.py:131
  150.4 277.2 %all-reduce.23.cloned.1.call-start = ((), (), s32[]{:S(2)}) async-start(), calls=%async_computation.13 | async-start | bytes 4194304 | tf_op jit(solution)/shard_map/psum | solution.py:208
  364.6 145.5 %all-gather.30.cloned.1.call-start = ((), (), s32[]{:S(2)}) async-start(), calls=%async_computation.14 | async-start | bytes 5242880 | tf_op jit(solution)/shard_map/all_gather | solution.py:135
  365.3 225.7 %all-gather.32.cloned.1.call-start = ((), (), s32[]{:S(2)}) async-start(), calls=%async_computation.15 | async-start | bytes 5242880 | tf_op jit(solution)/shard_map/all_gather | solution.py:137
  366.1 276.8 %all-gather.40.cloned.1.call-start = ((), (), s32[]{:S(2)}) async-start(), calls=%async_computation.20 | async-start | bytes 3932160 | tf_op jit(solution)/shard_map/all_gather | solution.py:107
  367.3 312.9 %all-gather.38.cloned.1.call-start = ((), (), s32[]{:S(2)}) async-start(), calls=%async_computation.19 | async-start | bytes 10485760 | tf_op jit(solution)/shard_map/all_gather | solution.py:106
  367.9 378.2 %all-reduce.25.cloned.1.call-start = ((), (), s32[]{:S(2)}) async-start(), calls=%async_computation.16 | async-start | bytes 4194304 | tf_op jit(solution)/shard_map/psum | solution.py:225
  378.9 479.8 %copy-start.42 = (f32[4,1,256]{2,1,0:T(1,128)}, f32[4,1,256]{2,1,0:T(1,128)S(1)}, u32[]{:S(2)}) copy-start(f32[4,1,256]{2,1,0:T(1,128)S(1)} %convert_element_type.332) | copy-start | bytes 12292
  386.5 472.2 %copy-start.46 = (f32[4,1,256]{2,1,0:T(1,128)}, f32[4,1,256]{2,1,0:T(1,128)S(1)}, u32[]{:S(2)}) copy-start(f32[4,1,256]{2,1,0:T(1,128)S(1)} %convert_element_type.333) | copy-start | bytes 12292
  396.1 350.0 %copy-start.56 = (f32[4,1,256]{2,1,0:T(1,128)}, f32[4,1,256]{2,1,0:T(1,128)S(1)}, u32[]{:S(2)}) copy-start(f32[4,1,256]{2,1,0:T(1,128)S(1)} %convert_element_type.334) | copy-start | bytes 12292
  430.2 428.5 %copy-start.44 = (f32[1024]{0:T(1024)}, f32[1024]{0:T(1024)S(1)}, u32[]{:S(2)}) copy-start(f32[1024]{0:T(1024)S(1)} %broadcast_multiply_fusion.1) | copy-start | bytes 12292
  431.2 427.4 %copy-start.48 = (f32[1024]{0:T(1024)}, f32[1024]{0:T(1024)S(1)}, u32[]{:S(2)}) copy-start(f32[1024]{0:T(1024)S(1)} %fusion.92) | copy-start | bytes 12292
  600.4 251.5 %all-reduce.27.cloned.1.call-start = ((), (), s32[]{:S(2)}) async-start(), calls=%async_computation.21 | async-start | bytes 4194304 | tf_op jit(solution)/shard_map/psum | solution.py:250
  788.9 413.2 %reduce-scatter.11.cloned.1.call-start = ((), (), s32[]{:S(2)}) async-start(), calls=%async_computation.22 | async-start | bytes 5242880 | tf_op jit(solution)/shard_map/reduce_scatter | solution.py:298
  1157.5 91.6 %reduce-scatter.13.cloned.1.call-start = ((), (), s32[]{:S(2)}) async-start(), calls=%async_computation.23 | async-start | bytes 5242880 | tf_op jit(solution)/shard_map/reduce_scatter | solution.py:301
  1165.4 108.5 %reduce-scatter.23.cloned.1.call-start = ((), (), s32[]{:S(2)}) async-start(), calls=%async_computation.30 | async-start | bytes 737280 | tf_op jit(solution)/shard_map/reduce_scatter | solution.py:390
  1170.4 131.2 %reduce-scatter.17.cloned.1.call-start = ((), (), s32[]{:S(2)}) async-start(), calls=%async_computation.27 | async-start | bytes 1310720 | tf_op jit(solution)/shard_map/reduce_scatter | solution.py:360
  1175.2 204.0 %reduce-scatter.21.cloned.1.call-start = ((), (), s32[]{:S(2)}) async-start(), calls=%async_computation.29 | async-start | bytes 5242880 | tf_op jit(solution)/shard_map/reduce_scatter | solution.py:378
  1186.1 272.7 %reduce-scatter.19.cloned.1.call-start = ((), (), s32[]{:S(2)}) async-start(), calls=%async_computation.28 | async-start | bytes 5242880 | tf_op jit(solution)/shard_map/reduce_scatter | solution.py:372
  1197.6 324.3 %reduce-scatter.15.cloned.1.call-start = ((), (), s32[]{:S(2)}) async-start(), calls=%async_computation.26 | async-start | bytes 3932160 | tf_op jit(solution)/shard_map/reduce_scatter | solution.py:354
  1259.1 327.9 %all-reduce.29.cloned.1.call-start = ((), (), s32[]{:S(2)}) async-start(), calls=%async_computation.24 | async-start | bytes 4194304 | tf_op jit(solution)/shard_map/psum | solution.py:316
  1267.7 353.1 %all-gather.36.cloned.1.call-start = ((), (), s32[]{:S(2)}) async-start(), calls=%async_computation.18 | async-start | bytes 2949120 | tf_op jit(solution)/shard_map/all_gather | solution.py:333
  1268.7 366.7 %reduce-scatter.25.cloned.1.call-start = ((), (), s32[]{:S(2)}) async-start(), calls=%async_computation.31 | async-start | bytes 163840
  1273.1 421.3 %all-gather.34.cloned.1.call-start = ((), (), s32[]{:S(2)}) async-start(), calls=%async_computation.17 | async-start | bytes 10485760 | tf_op jit(solution)/shard_map/all_gather | solution.py:332
  1273.8 494.9 %all-reduce.31.cloned.1.call-start = ((), (), s32[]{:S(2)}) async-start(), calls=%async_computation.32 | async-start | bytes 6586368 | tf_op jit(solution)/shard_map/psum | solution.py:409
  1521.9 306.8 %all-gather.42.cloned.1.call-start = ((), (), s32[]{:S(2)}) async-start(), calls=%async_computation.25 | async-start | bytes 10485760 | tf_op jit(solution)/shard_map/all_gather | solution.py:334
  (70 other events, 944.0 us)
Sparse Core Ops, SparseCore 0:
  9.6 60.9 all-gather.19
  72.8 63.4 all-gather.21
  147.2 32.6 all-gather.23
  181.9 34.4 all-gather.25
  217.8 27.9 all-gather.27
  364.7 62.8 all-reduce.22
  429.3 80.7 all-gather.29
  511.7 79.2 all-gather.31
  593.3 27.0 all-gather.39
  621.9 58.2 all-gather.37
  683.2 62.9 all-reduce.24
  789.0 62.9 all-reduce.26
  1157.6 44.4 reduce-scatter.10
  1204.5 44.4 reduce-scatter.12
  1251.3 21.9 reduce-scatter.22
  1276.1 25.5 reduce-scatter.16
  1303.8 75.4 reduce-scatter.20
  1381.5 77.2 reduce-scatter.18
  1461.1 60.7 reduce-scatter.14
  1524.0 62.9 all-reduce.28
  1589.2 24.0 all-gather.35
  1616.2 19.1 reduce-scatter.24
  1637.6 56.7 all-gather.33
  1697.0 71.7 all-reduce.30
  1770.4 58.3 all-gather.41

commit v2 on v0

v2 whole, which is shorter than its diff:
```python
import math
from functools import partial
import jax, jax.numpy as jnp
from jax import lax
from jax.experimental import pallas as pl
from jax.experimental.pallas import tpu as pltpu
from jax.sharding import Mesh
from jax.sharding import PartitionSpec as P

f32, bf16 = jnp.float32, jnp.bfloat16
HEAD_DIM = 64
VMEM_CAP = 56 * 1024 * 1024
MASKED = -1e30
TS = 256
FQ, FK = 1024, 512
BQ, BK = 512, 512


def nt(a, b):
    return lax.dot_general(a, b, (((1,), (1,)), ((), ())), preferred_element_type=f32)


def nn(a, b):
    return lax.dot_general(a, b, (((1,), (0,)), ((), ())), preferred_element_type=f32)


def run(kernel, out_shape, name, scalars=0, scratch=(), flops=2_000_000_000):
    def call(*args):
        vm = pl.BlockSpec(memory_space=pltpu.VMEM)
        sm = pl.BlockSpec(memory_space=pltpu.SMEM)
        outs = jax.tree.map(lambda _: vm, out_shape)
        return pl.pallas_call(
            kernel, out_shape=out_shape,
            in_specs=[sm] * scalars + [vm] * (len(args) - scalars), out_specs=outs,
            scratch_shapes=list(scratch),
            compiler_params=pltpu.CompilerParams(vmem_limit_bytes=VMEM_CAP),
            cost_estimate=pl.CostEstimate(flops=flops, transcendentals=0, bytes_accessed=8_000_000),
            name=name)(*args)
    return call


def one_hot(rank_ref, tile, start, width):
    want = lax.broadcasted_iota(jnp.int32, (TS, width), 0) + tile * TS
    return jnp.where(rank_ref[:, pl.ds(start, width)] == want, 1.0, 0.0).astype(bf16)


def key_span(start, size, first_len, tile, total):
    lo = jnp.where(start >= first_len, first_len // tile, 0)
    hi = jnp.where(start + size <= first_len, (first_len + tile - 1) // tile, total // tile)
    return lo, hi


def code_lanes(base, rows, first_len):
    row = lax.broadcasted_iota(jnp.int32, (rows, 128), 0) + base
    lane = lax.broadcasted_iota(jnp.int32, (rows, 128), 1)
    bad = jnp.where(row < first_len, 1, 0)
    return jnp.where(lane == bad, MASKED, jnp.where((lane >= 2) & (lane < 5), 1.0, 0.0)).astype(bf16)


def code_rows(base, cols, first_len):
    row = lax.broadcasted_iota(jnp.int32, (128, cols), 0)
    col = lax.broadcasted_iota(jnp.int32, (128, cols), 1) + base
    return (jnp.where(row == jnp.where(col < first_len, 0, 1), 1.0, 0.0), row)


def head_rows(values, head):
    row = lax.broadcasted_iota(jnp.int32, values.shape, 0)
    return jnp.where((row // HEAD_DIM) == head, values, 0.0)


def head_lanes(values, head):
    lane = lax.broadcasted_iota(jnp.int32, values.shape, 1)
    return jnp.where((lane // HEAD_DIM) == head, values, 0.0)


def forward_kernel(len_ref, meet_ref, dest_ref, rank_ref, near_ref, far_ref, att_ref, sorted_ref, att_t_ref, lse_ref,
                   k_ext, q_ext, arr_t):
    rows = rank_ref.shape[1]
    block = rows // 4
    first_len = len_ref[0]
    scale = HEAD_DIM ** -0.5

    def sort_tile(tile, carry):
        at = pl.multiple_of(tile * TS, TS)
        arr_t[:, pl.ds(0, TS)] = jnp.zeros((384, TS), f32)
        for d in range(4):
            @pl.when(meet_ref[tile * 4 + d] > 0)
            def _():
                hot = one_hot(rank_ref, tile, d * block, block)
                mixed_ref = near_ref if d < 2 else far_ref
                arr_t[:, pl.ds(0, TS)] += nt(mixed_ref[:, pl.ds((d % 2) * block, block)], hot)
        low = arr_t[:, pl.ds(0, TS)].astype(bf16)
        sorted_ref[:, pl.ds(at, TS)] = low
        wide = low.astype(f32)
        query = wide[0:128] * scale
        code, _ = code_rows(at, TS, first_len)
        for h in range(2):
            q_ext[h, 0:128, pl.ds(at, TS)] = head_rows(query, h).astype(bf16)
            q_ext[h, 128:256, pl.ds(at, TS)] = code.astype(bf16)
        k_ext[pl.ds(at, TS), 0:128] = wide[128:256].T.astype(bf16)
        k_ext[pl.ds(at, TS), 128:256] = code_lanes(at, TS, first_len)
        return carry

    lax.fori_loop(0, rows // TS, sort_tile, 0)

    def query_tile(i, carry):
        at = pl.multiple_of(i * FQ, FQ)
        lo, hi = key_span(at, FQ, first_len, FK, rows)

        def key_tile(j, state):
            kat = pl.multiple_of(j * FK, FK)
            keys = k_ext[pl.ds(kat, FK), :]
            out = []
            for h in range(2):
                top, total, acc = state[h]
                scores = nn(keys, q_ext[h, :, pl.ds(at, FQ)])
                new_top = jnp.maximum(top, jnp.max(scores, axis=0, keepdims=True))
                fade = jnp.exp(top - new_top)
                weights = jnp.exp(scores - new_top)
                total = total * fade + jnp.sum(weights, axis=0, keepdims=True)
                value = sorted_ref[256 + h * 64:320 + h * 64, pl.ds(kat, FK)]
                acc = acc * fade + nn(value, weights.astype(bf16))
                out.append((new_top, total, acc))
            return tuple(out)

        start = (jnp.full((1, FQ), MASKED, f32), jnp.zeros((1, FQ), f32), jnp.zeros((64, FQ), f32))
        state = lax.fori_loop(lo, hi, key_tile, (start, start))
        lse_rows = []
        for h in range(2):
            top, total, acc = state[h]
            att_t_ref[h * 64:(h + 1) * 64, pl.ds(at, FQ)] = (acc / total).astype(bf16)
            lse_ref[h:h + 1, pl.ds(at, FQ)] = top + jnp.log(total)
        return carry

    lax.fori_loop(0, rows // FQ, query_tile, 0)

    for d in range(4):
        arr_t[0:128, :] = jnp.zeros((128, block), f32)

        def back_tile(tile, carry):
            @pl.when(meet_ref[tile * 4 + d] > 0)
            def _():
                at = pl.multiple_of(tile * TS, TS)
                hot = one_hot(rank_ref, tile, d * block, block)
                arr_t[0:128, :] += nn(att_t_ref[:, pl.ds(at, TS)], hot)
            return carry

        lax.fori_loop(0, rows // TS, back_tile, 0)
        low = arr_t[0:128, :].T.astype(bf16)
        att_ref[dest_ref[2 * d]] = low[:block // 2]
        att_ref[dest_ref[2 * d + 1]] = low[block // 2:]


def attention_forward(first_len, meet, dest, rank, near, far):
    rows = rank.shape[1]
    return pl.pallas_call(
        forward_kernel,
        out_shape=(
            jax.ShapeDtypeStruct((8, rows // 8, 128), bf16),
            jax.ShapeDtypeStruct((384, rows), bf16),
            jax.ShapeDtypeStruct((128, rows), bf16),
            jax.ShapeDtypeStruct((8, rows), f32),
        ),
        in_specs=[
            pl.BlockSpec(memory_space=pltpu.SMEM),
            pl.BlockSpec(memory_space=pltpu.SMEM),
            pl.BlockSpec(memory_space=pltpu.SMEM),
            pl.BlockSpec(memory_space=pltpu.VMEM),
            pl.BlockSpec(memory_space=pltpu.VMEM),
            pl.BlockSpec(memory_space=pltpu.VMEM),
        ],
        out_specs=tuple(pl.BlockSpec(memory_space=pltpu.VMEM) for _ in range(4)),
        scratch_shapes=[
            pltpu.VMEM((rows, 256), bf16),
            pltpu.VMEM((2, 256, rows), bf16),
            pltpu.VMEM((384, rows // 4), f32),
        ],
        compiler_params=pltpu.CompilerParams(vmem_limit_bytes=VMEM_CAP),
        cost_estimate=pl.CostEstimate(flops=60_000_000_000, transcendentals=16_000_000, bytes_accessed=16_000_000),
        name="attention_forward",
    )(first_len, meet, dest, rank, near, far)


def split3(v):
    hi = v.astype(bf16).astype(f32)
    mid = (v - hi).astype(bf16).astype(f32)
    return hi, mid, v - hi - mid


def backward_kernel(len_ref, meet_ref, dest_ref, rank_ref, sorted_ref, att_t_ref, lse_ref, cos_ref, sin_ref,
                    grad_ref, *refs):
    (out_ref, bias_ref, k_ext, q_ext, v_ext, g_ext, q_nat, g_nat, dq_t, arr_t, ds_low) = refs
    rows = rank_ref.shape[1]
    block = rows // 4
    first_len = len_ref[0]
    scale = HEAD_DIM ** -0.5

    def sort_tile(tile, carry):
        at = pl.multiple_of(tile * TS, TS)
        q_t = sorted_ref[0:128, pl.ds(at, TS)].astype(f32) * scale
        k_ext[pl.ds(at, TS), 0:128] = sorted_ref[128:256, pl.ds(at, TS)].astype(f32).T.astype(bf16)
        k_ext[pl.ds(at, TS), 128:256] = code_lanes(at, TS, first_len)
        v_ext[pl.ds(at, TS), 0:128] = sorted_ref[256:384, pl.ds(at, TS)].astype(f32).T.astype(bf16)
        v_ext[pl.ds(at, TS), 128:256] = code_lanes(at, TS, first_len)
        arr_t[0:TS, 0:128] = jnp.zeros((TS, 128), f32)
        for d in range(4):
            @pl.when(meet_ref[tile * 4 + d] > 0)
            def _():
                hot = one_hot(rank_ref, tile, d * block, block)
                half = block // 2
                arr_t[0:TS, 0:128] += (nn(hot[:, :half], grad_ref[dest_ref[2 * d]])
                                       + nn(hot[:, half:], grad_ref[dest_ref[2 * d + 1]]))
        grad = arr_t[0:TS, 0:128]
        grad_t = grad.T
        q = q_t.T
        code, row = code_rows(at, TS, first_len)
        prod = grad_t * att_t_ref[:, pl.ds(at, TS)].astype(f32)
        for h in range(2):
            delta = jnp.sum(prod[h * 64:(h + 1) * 64], axis=0, keepdims=True)
            lse = lse_ref[h:h + 1, pl.ds(at, TS)]
            l0, l1, l2 = split3(-lse)
            d0, d1, d2 = split3(-delta)
            q_ext[h, 0:128, pl.ds(at, TS)] = head_rows(q_t, h).astype(bf16)
            q_ext[h, 128:256, pl.ds(at, TS)] = jnp.where(
                row == 2, l0, jnp.where(row == 3, l1, jnp.where(row == 4, l2, code))).astype(bf16)
            g_ext[h, 0:128, pl.ds(at, TS)] = head_rows(grad_t, h).astype(bf16)
            g_ext[h, 128:256, pl.ds(at, TS)] = jnp.where(
                row == 2, d0, jnp.where(row == 3, d1, jnp.where(row == 4, d2, 0.0))).astype(bf16)
            q_nat[h, pl.ds(at, TS), :] = head_lanes(q, h).astype(bf16)
            g_nat[h, pl.ds(at, TS), :] = head_lanes(grad, h).astype(bf16)
        return carry

    lax.fori_loop(0, rows // TS, sort_tile, 0)
    dq_t[...] = jnp.zeros(dq_t.shape, f32)

    def key_tile(j, carry):
        kat = pl.multiple_of(j * BK, BK)
        lo, hi = key_span(kat, BK, first_len, BQ, rows)

        def query_tile(i, state):
            dk, dv = state
            at = pl.multiple_of(i * BQ, BQ)
            keys = k_ext[pl.ds(kat, BK), :]
            values = v_ext[pl.ds(kat, BK), :]
            for h in range(2):
                probs = jnp.exp(nn(keys, q_ext[h, :, pl.ds(at, BQ)]))
                dprob = nn(values, g_ext[h, :, pl.ds(at, BQ)])
                dscore = (probs * dprob).astype(bf16)
                dv = dv + nn(probs.astype(bf16), g_nat[h, pl.ds(at, BQ), :])
                dk = dk + nn(dscore, q_nat[h, pl.ds(at, BQ), :])
                dq_t[h * 64:(h + 1) * 64, pl.ds(at, BQ)] += nn(
                    sorted_ref[128 + h * 64:192 + h * 64, pl.ds(kat, BK)], dscore)
            return dk, dv

        zero = jnp.zeros((BK, 128), f32)
        dk, dv = lax.fori_loop(lo, hi, query_tile, (zero, zero))
        ds_low[128:256, pl.ds(kat, BK)] = dk.T.astype(bf16)
        ds_low[256:384, pl.ds(kat, BK)] = dv.T.astype(bf16)
        return carry

    lax.fori_loop(0, rows // BK, key_tile, 0)
    ds_low[0:128, :] = (dq_t[...] * scale).astype(bf16)
    bias = jnp.zeros((384, 1), f32)
    for d in range(4):
        arr_t[...] = jnp.zeros((384, block), f32)

        def back_tile(tile, carry):
            @pl.when(meet_ref[tile * 4 + d] > 0)
            def _():
                at = pl.multiple_of(tile * TS, TS)
                hot = one_hot(rank_ref, tile, d * block, block)
                arr_t[...] += nn(ds_low[:, pl.ds(at, TS)], hot)
            return carry

        lax.fori_loop(0, rows // TS, back_tile, 0)
        cos, sin = cos_ref[:, pl.ds(d * block, block)], sin_ref[:, pl.ds(d * block, block)]
        for base in (0, 64, 128, 192):
            front, back = arr_t[base:base + 32, :], arr_t[base + 32:base + 64, :]
            arr_t[base:base + 32, :] = front * cos + back * sin
            arr_t[base + 32:base + 64, :] = back * cos - front * sin
        bias = bias + jnp.sum(arr_t[...], axis=1, keepdims=True)
        out_ref[dest_ref[2 * d]] = arr_t[:, 0:block // 2].astype(bf16)
        out_ref[dest_ref[2 * d + 1]] = arr_t[:, block // 2:block].astype(bf16)
    bias_ref[...] = bias


def attention_backward(first_len, meet, dest, rank, sorted_t, att_t, lse, cos_t, sin_t, grad):
    rows = rank.shape[1]
    vm = pl.BlockSpec(memory_space=pltpu.VMEM)
    sm = pl.BlockSpec(memory_space=pltpu.SMEM)
    return pl.pallas_call(
        backward_kernel,
        out_shape=(
            jax.ShapeDtypeStruct((8, 384, rows // 8), bf16),
            jax.ShapeDtypeStruct((384, 1), f32),
        ),
        in_specs=[sm, sm, sm] + [vm] * 7,
        out_specs=(vm, vm),
        scratch_shapes=[
            pltpu.VMEM((rows, 256), bf16),
            pltpu.VMEM((2, 256, rows), bf16),
            pltpu.VMEM((rows, 256), bf16),
            pltpu.VMEM((2, 256, rows), bf16),
            pltpu.VMEM((2, rows, 128), bf16),
            pltpu.VMEM((2, rows, 128), bf16),
            pltpu.VMEM((128, rows), f32),
            pltpu.VMEM((384, rows // 4), f32),
            pltpu.VMEM((384, rows), bf16),
        ],
        compiler_params=pltpu.CompilerParams(vmem_limit_bytes=VMEM_CAP),
        cost_estimate=pl.CostEstimate(flops=90_000_000_000, transcendentals=16_000_000, bytes_accessed=16_000_000),
        name="attention_backward",
    )(first_len, meet, dest, rank, sorted_t, att_t, lse, cos_t, sin_t, grad)


def qkv_kernel(ctx_ref, cos_ref, sin_ref, w_ref, *refs):
    out_ref = refs[-1]
    size, _, lanes = w_ref.shape
    bias = jnp.zeros((1, 384), f32)
    for f in range(size):
        bias_row = jnp.concatenate(
            [w_ref[f, 384 + i:385 + i, :].astype(f32) for i in range(-(-384 // lanes))], axis=1)[:, :384]
        bias = jnp.where(ctx_ref[0] == f, bias_row, bias) if size == 4 else jnp.where(f == 0, bias_row, bias)
    bias = jnp.broadcast_to(bias, (128, 384)).T[:, 0:1]
    start = 0
    for x_ref in refs[:-1]:
        count = x_ref.shape[0]
        span = slice(start, start + count)
        mixed = jnp.broadcast_to(bias, (384, count))
        for f in range(size):
            mixed = mixed + nt(w_ref[f, 0:384], x_ref[:, f * lanes:(f + 1) * lanes])
        cos, sin = cos_ref[:, span], sin_ref[:, span]
        for base in (0, 64, 128, 192):
            front, back = mixed[base:base + 32], mixed[base + 32:base + 64]
            out_ref[base:base + 32, span] = (front * cos - back * sin).astype(bf16)
            out_ref[base + 32:base + 64, span] = (back * cos + front * sin).astype(bf16)
        out_ref[256:384, span] = mixed[256:384].astype(bf16)
        start += count


def qkv_rope(ctx, pieces, weights, cos_t, sin_t):
    rows = sum(p.shape[0] for p in pieces)
    return run(qkv_kernel, jax.ShapeDtypeStruct((384, rows), bf16), "qkv_rope", 1)(
        ctx, cos_t, sin_t, weights, *pieces)


def row_places(order, packed, lengths, arrival):
    rows = order.shape[0]
    first_len = lengths[0]
    place = jnp.sum(
        jnp.where(order[:, None] == arrival[None, :], packed[:, None], 0), axis=0)
    in_first = place < first_len
    position = jnp.where(in_first, place, place - first_len)
    flags = in_first.astype(f32).reshape(rows // 128, 128)
    before = jnp.arange(128)[:, None] < jnp.arange(128)[None, :]
    within = jnp.dot(flags.astype(bf16), before.astype(bf16), preferred_element_type=f32)
    sums = jnp.sum(flags, axis=1)
    n = rows // 128
    earlier = jnp.arange(n)[None, :] < jnp.arange(n)[:, None]
    offset = jnp.sum(jnp.where(earlier, sums[None, :], 0.0), axis=1)
    firsts = (within + offset[:, None]).reshape(rows).astype(jnp.int32)
    index = jnp.arange(rows, dtype=jnp.int32)
    rank = jnp.where(in_first, firsts, first_len + index - firsts)
    counts = jnp.sum(in_first.astype(jnp.int32).reshape(4, rows // 4), axis=1)
    d = jnp.arange(4)
    lo0 = jnp.sum(jnp.where(d[None, :] < d[:, None], counts[None, :], 0), axis=1)
    hi0 = lo0 + counts
    lo1 = first_len + d * (rows // 4) - lo0
    hi1 = lo1 + rows // 4 - counts
    t0 = jnp.arange(rows // TS)[:, None] * TS
    t1 = t0 + TS
    meet = (((lo0[None] < t1) & (hi0[None] > t0) & (hi0 > lo0)[None])
            | ((lo1[None] < t1) & (hi1[None] > t0) & (hi1 > lo1)[None])).astype(jnp.int32)
    return position, rank, meet.reshape(-1)


def rope_tables_t(position):
    frequency = jnp.exp(jnp.arange(32, dtype=f32) * (-2.0 * math.log(10000.0) / 64))
    angles = frequency[:, None] * position.astype(f32)[None, :]
    return jnp.cos(angles), jnp.sin(angles)


norm_eps = 1e-05
embed_eps = 1e-06
WIDTHS = (128, 96, 64)
CT = ("cx", "core", "tp")
CTX = ("cx", "core")


def tn(a, b):
    return lax.dot_general(a, b, (((0,), (0,)), ((), ())), preferred_element_type=f32)


def head_rows_of(device):
    return ((device & 1) * 4 + (device >> 1)) * 128


def row_mean(v):
    return jnp.mean(v, axis=1, keepdims=True)


def norm_parts(v):
    centred = v - row_mean(v)
    rstd = lax.rsqrt(row_mean(centred * centred) + norm_eps)
    return centred * rstd, rstd


def norm_back(grad, x_hat, rstd, gain):
    e = grad * gain
    return (e - row_mean(e) - x_hat * row_mean(e * x_hat)) * rstd


def col_sum(v):
    return jnp.sum(v, axis=0, keepdims=True)


def out_proj_kernel(w_ref, x_ref, att_ref, bias_ref, gain_ref, shift_ref,
                    normed_ref, hat_ref, rstd_ref, low_ref):
    acc = x_ref[...].astype(f32) + bias_ref[...]
    for j in range(8):
        at = head_rows_of(j)
        acc = acc + nn(att_ref[j], w_ref[at:at + 128, 0:acc.shape[1]])
    x_hat, rstd = norm_parts(acc)
    normed = x_hat * gain_ref[...] + shift_ref[...]
    normed_ref[...] = normed
    hat_ref[...] = x_hat
    rstd_ref[...] = rstd
    low_ref[...] = normed.astype(bf16)


def hidden_refs(refs):
    first = refs[3].shape[0]
    return [(lambda f, r=r: (r, f)) for r in refs[0:3]] + [
        lambda f: (refs[3], f) if f < first else (refs[4], f - first)]


def up_rows(block, f, shard):
    ref, i = block(f)
    return ref[i, 0:shard]


def down_rows(block, group, strip, shard, side):
    parts = []
    for f in group:
        ref, i = block(f)
        at = shard + side * strip
        parts.append(ref[i, at:at + strip])
    return jnp.concatenate(parts, axis=0) if len(parts) > 1 else parts[0]


def hidden_sizes(refs, width):
    size, _, units = refs[0].shape
    strip = units // size
    step = max(1, 256 // strip)
    groups = [range(g, g + step) for g in range(0, size, step)]
    return size, units, strip, width // size, width // units, groups


def mlp_kernel(own_ref, peer_ref, bias_ref, *refs):
    act_ref, slope_ref, own_out, peer_out = refs[5:]
    half, width = own_ref.shape
    size, units, strip, shard, sides, groups = hidden_sizes(refs, width)
    blocks = hidden_refs(refs)
    for r, x_ref in enumerate((own_ref, peer_ref)):
        rows = slice(r * half, (r + 1) * half)
        out = [jnp.zeros((half, units), f32) for _ in range(sides)]
        for v in range(4):
            cols = slice(v * units, (v + 1) * units)
            up = jnp.broadcast_to(bias_ref[:, cols], (half, units))
            for f in range(size):
                up = up + nn(x_ref[:, f * shard:(f + 1) * shard], up_rows(blocks[v], f, shard))
            phi_int = 0.5 * (1.0 + lax.erf(up * (0.5 ** 0.5)))
            density = jnp.exp(-0.5 * up * up) * ((2.0 * math.pi) ** -0.5)
            act = (up * phi_int).astype(bf16)
            act_ref[rows, cols] = act
            slope_ref[rows, cols] = (phi_int + up * density).astype(bf16)
            for g in groups:
                at = g[0] * strip
                part = act[:, at:at + len(g) * strip]
                for s in range(sides):
                    out[s] = out[s] + nn(part, down_rows(blocks[v], g, strip, shard, s))
        for s in range(sides):
            if r == 0:
                own_out[:, s * units:(s + 1) * units] = out[s]
            else:
                peer_out[:, s * units:(s + 1) * units] = out[s].astype(bf16)


def head_kernel(strip_rows, normed_ref, own_ref, recv_ref, bias_ref, gain_ref, shift_ref, dense_ref, cot_ref, cot_embed_ref,
                final_ref, embed_ref, grad_ref, low_ref, proj_grad_ref, vec_ref, proj_ref):
    width, emb = proj_ref.shape
    strip = strip_rows
    for f in range(width // (2 * strip)):
        for t in range(2):
            at = (f * 2 + t) * strip
            src = (t * (width // (2 * strip)) + f) * strip
            proj_ref[at:at + strip, :] = dense_ref[src:src + strip, width:width + emb]
    second = normed_ref[...] + own_ref[...] + recv_ref[...].astype(f32) + bias_ref[...]
    x_hat, rstd = norm_parts(second)
    final = (x_hat * gain_ref[...] + shift_ref[...]).astype(bf16)
    final_ref[...] = final
    projected = nn(final, proj_ref[...])
    cot = cot_embed_ref[...].astype(f32)
    col = lax.broadcasted_iota(jnp.int32, projected.shape, 1)
    embedded = jnp.zeros(projected.shape, f32)
    grad_proj = jnp.zeros(projected.shape, f32)
    start = 0
    for width in WIDTHS:
        here = (col >= start) & (col < start + width)
        part = jnp.where(here, projected, 0.0)
        r = lax.rsqrt(jnp.sum(part * part, axis=1, keepdims=True) + embed_eps)
        n = part * r
        along = jnp.sum(n * cot, axis=1, keepdims=True)
        embedded = embedded + n
        grad_proj = jnp.where(here, r * (cot - n * along), grad_proj)
        start += width
    embed_ref[...] = embedded.astype(bf16)
    proj_low = grad_proj.astype(bf16)
    proj_grad_ref[...] = tn(final, proj_low).astype(bf16)
    grad_final = cot_ref[...].astype(f32) + nt(proj_low, proj_ref[...])
    grad_second = norm_back(grad_final, x_hat, rstd, gain_ref[...])
    grad_ref[...] = grad_second
    low_ref[...] = grad_second.astype(bf16)
    vec_ref[...] = jnp.zeros(vec_ref.shape, f32)
    vec_ref[0:1] = col_sum(grad_final * x_hat)
    vec_ref[1:2] = col_sum(grad_final)
    vec_ref[2:3] = col_sum(grad_second)


def mlp_back_kernel(own_ref, peer_ref, slope_ref, *refs):
    g1_ref, bias_ref, own_out, peer_out = refs[5:]
    half, width = own_ref.shape
    size, units, strip, shard, sides, groups = hidden_sizes(refs, width)
    blocks = hidden_refs(refs)
    for r, g_ref in enumerate((own_ref, peer_ref)):
        rows = slice(r * half, (r + 1) * half)
        out = [jnp.zeros((half, shard), f32) for _ in range(size)]
        for v in range(4):
            for g in groups:
                at = v * units + g[0] * strip
                cols = slice(at, at + len(g) * strip)
                grad_up = nt(g_ref[:, 0:units], down_rows(blocks[v], g, strip, shard, 0))
                for s in range(1, sides):
                    grad_up = grad_up + nt(
                        g_ref[:, s * units:(s + 1) * units], down_rows(blocks[v], g, strip, shard, s))
                grad_up = grad_up * slope_ref[rows, cols].astype(f32)
                sums = col_sum(grad_up)
                bias_ref[:, cols] = sums if r == 0 else bias_ref[:, cols] + sums
                g1_ref[rows, cols] = grad_up.astype(bf16)
            g1 = g1_ref[rows, v * units:(v + 1) * units]
            for f in range(size):
                out[f] = out[f] + nt(g1, up_rows(blocks[v], f, shard))
        for f in range(size):
            if r == 0:
                own_out[:, f * shard:(f + 1) * shard] = out[f]
            else:
                peer_out[:, f * shard:(f + 1) * shard] = out[f].astype(bf16)


def mlp_weights_kernel(place_ref, own_n, peer_n, own_g, peer_g, act_ref, g1_ref, bias_ref, dense_ref, recv_ref,
                       up0, up1, up2, up3, down_ref):
    size, _, units = up0.shape
    strip, shard = down_ref.shape[2], own_n.shape[1] // size
    normed = jnp.concatenate([own_n[...], peer_n[...]], axis=0)
    g2 = jnp.concatenate([own_g[...], peer_g[...]], axis=0)
    for v, up_ref in enumerate((up0, up1, up2, up3)):
        q = place_ref[0] ^ v
        cols = slice(v * units, (v + 1) * units)
        up = tn(normed, g1_ref[:, cols]).astype(bf16)
        down = tn(act_ref[:, cols], g2).astype(bf16)
        bias = jnp.broadcast_to(bias_ref[:, cols], (16, units)).astype(bf16)
        for f in range(size):
            up_ref[f, 0:shard] = up[f * shard:(f + 1) * shard]
            up_ref[f, shard:shard + 16] = bias
            up_ref[f, shard + 16:] = (dense_ref[q, f].astype(f32) + recv_ref[q, f].astype(f32)).astype(bf16)
            down_ref[f, q] = down[f * strip:(f + 1) * strip]


def sum_kernel(index_ref, p0, p1, p2, p3, down_ref, up_out, *down_outs):
    size = up_out.shape[0]
    for f in range(size):
        total = p0[f].astype(f32) + p1[f].astype(f32) + p2[f].astype(f32) + p3[f].astype(f32)
        up_out[(f - index_ref[0] + size) % size] = total.astype(bf16)
    for v, out in enumerate(down_outs):
        total = down_ref[0, index_ref[1] ^ v].astype(f32)
        for f in range(1, size):
            total = total + down_ref[f, index_ref[1] ^ v].astype(f32)
        out[...] = total.astype(bf16)


def pick_kernel(index_ref, up_ref, down_ref, dense_ref, proj_ref, *refs):
    vecs, outs = refs[:7], refs[7:]
    place, core, tp = (index_ref[i] for i in range(3))
    strip = down_ref.shape[0] // 4
    shard, units = up_ref.shape[0], up_ref.shape[1] // 4
    for n in range(2):
        q = place ^ n
        for f in range(units // strip):
            at = pl.multiple_of((f * 4 + q) * strip, strip)
            outs[n][0:shard, f * strip:(f + 1) * strip] = up_ref[:, pl.ds(at, strip)]
        rows = pl.multiple_of(q * strip, strip)
        for s in range(down_ref.shape[1] // units):
            at = shard + s * strip
            outs[n][at:at + strip] = down_ref[pl.ds(rows, strip), s * units:(s + 1) * units]
    count, width = dense_ref.shape[0] // 2, dense_ref.shape[1]
    half = outs[2]
    half[0:count, 0:width] = dense_ref[pl.ds(pl.multiple_of(core * count, count), count), :]
    half[0:count, width:] = proj_ref[pl.ds(pl.multiple_of((tp * 2 + core) * count, count), count), :]
    lines, line = [], []
    for v in vecs:
        line.append(v[...].astype(f32))
        if sum(p.shape[1] for p in line) == width:
            lines.append(jnp.concatenate(line, axis=1))
            line = []
    block = jnp.concatenate(lines + [jnp.zeros((16 - len(lines), width), f32)], axis=0)
    half[count:count + 16, 0:width] = block.astype(bf16)
    half[count:count + 16, width:] = jnp.zeros((16, half.shape[1] - width), bf16)


def dense_natural_kernel(index_ref, own_ref, core_ref, out_ref, vec_ref, up_ref):
    core, place = (index_ref[i] for i in range(2))
    size, rows = own_ref.shape[0] // 2, own_ref.shape[1] - 16
    units = up_ref.shape[1] // 4
    strip, quarter = units // size, vec_ref.shape[1] // size
    for f in range(size):
        for t in range(2):
            own, other = own_ref[t * size + f, 0:rows], core_ref[t * size + f, 0:rows]
            for k in range(2):
                at = ((t * size + f) * 2 + k) * rows
                out_ref[at:at + rows, :] = jnp.where(core == k, own, other)
        vecs = own_ref[f, rows:rows + 16].astype(f32)
        far = own_ref[size + f, rows:rows + 16].astype(f32)
        cut = 4 * strip
        ups = jnp.where(core == 0, vecs[0:1, 0:cut], far[0:1, 0:cut])
        for i in range(6):
            r, c = divmod(cut + i * quarter, 4 * quarter)
            vec_ref[i:i + 1, f * quarter:(f + 1) * quarter] = vecs[r:r + 1, c:c + quarter]
        for v in range(4):
            picked = jnp.zeros((1, strip), f32)
            for q in range(4):
                picked = jnp.where((place ^ v) == q, ups[:, q * strip:(q + 1) * strip], picked)
            up_ref[:, v * units + f * strip:v * units + (f + 1) * strip] = picked


def hidden_join_kernel(part_ref, up_ref, down_ref):
    strip = down_ref.shape[0] // 4
    shard, units = up_ref.shape[0], part_ref.shape[2]
    for q in range(4):
        for f in range(units // strip):
            at = (f * 4 + q) * strip
            up_ref[:, at:at + strip] = part_ref[q, 0:shard, f * strip:(f + 1) * strip].astype(f32)
        for s in range(down_ref.shape[1] // units):
            at = shard + 16 + s * strip
            down_ref[q * strip:(q + 1) * strip, s * units:(s + 1) * units] = part_ref[q, at:at + strip].astype(f32)


def first_back_kernel(second_ref, own_ref, recv_ref, hat_ref, rstd_ref, gain_ref, w_ref,
                      grad_ref, low_ref, att_grad_ref, vec_ref):
    grad_normed = second_ref[...] + own_ref[...] + recv_ref[...].astype(f32)
    x_hat = hat_ref[...]
    grad_first = norm_back(grad_normed, x_hat, rstd_ref[...], gain_ref[...])
    grad_ref[...] = grad_first
    low = grad_first.astype(bf16)
    low_ref[...] = low
    for j in range(8):
        at = head_rows_of(j)
        att_grad_ref[j] = nt(low, w_ref[at:at + 128, 0:low.shape[1]]).astype(bf16)
    vec_ref[...] = jnp.zeros(vec_ref.shape, f32)
    vec_ref[0:1] = col_sum(grad_normed * x_hat)
    vec_ref[1:2] = col_sum(grad_normed)
    vec_ref[2:3] = col_sum(grad_first)


def out_weight_kernel(low_ref, att_ref, proj_grad_ref, vec2_ref, vec1_ref, out_ref):
    width = low_ref.shape[1]
    _, _, size, rows, cols = out_ref.shape
    shard = width // (2 * size)
    thin, tail_rows = shard // 4, shard // 8
    sides = width // cols

    def store(t, f, part, at, value):
        for s in range(sides):
            first = at * sides + s * value.shape[0]
            out_ref[part % 2, part // 2 * 2 + t, f, first:first + value.shape[0]] = value[:, s * cols:(s + 1) * cols]

    for j in range(8):
        grad = tn(att_ref[j], low_ref[...]).astype(bf16)
        for start in range(0, 128, thin):
            block, rest = divmod(head_rows_of(j) + start, shard)
            store(block // size, block % size, rest // thin, 0, grad[start:start + thin])
    vecs = jnp.concatenate([vec2_ref[0:3], vec1_ref[0:3], jnp.zeros((122, width), f32)], axis=0).T
    tail = jnp.concatenate([proj_grad_ref[...].astype(f32), vecs[:, 0:96]], axis=1).astype(bf16)
    for f in range(size):
        for t in range(2):
            part = tail[(f * 2 + t) * shard:(f * 2 + t + 1) * shard]
            for b in range(4):
                if b < 3:
                    value = jnp.concatenate(
                        [part[g * tail_rows:(g + 1) * tail_rows, b * 128:(b + 1) * 128] for g in range(8)], axis=1)
                else:
                    value = jnp.zeros((tail_rows, width), bf16)
                store(t, f, b, thin, value)


def qkv_weight_kernel(dest_ref, d_ref, bias_ref, *refs):
    out_ref = refs[-1]
    size, _, lanes = out_ref.shape
    acc = jnp.zeros((384, size * lanes), f32)
    start, part = 0, d_ref.shape[2]
    for x_ref in refs[:-1]:
        done = 0
        while done < x_ref.shape[0]:
            count = min(x_ref.shape[0] - done, part)
            u, at = start // part, start % part
            acc = acc + nn(d_ref[dest_ref[u], :, at:at + count], x_ref[done:done + count])
            start, done = start + count, done + count
    row = jnp.broadcast_to(bias_ref[...], (384, 128)).T[0:1]
    row = jnp.concatenate([row, jnp.zeros((1, max(0, -(-384 // lanes) * lanes - 384)), f32)], axis=1) if 384 % lanes else row
    count = row.shape[1] // lanes
    lines = [row[:, i * lanes:(i + 1) * lanes] for i in range(count)]
    block = jnp.concatenate(lines + [jnp.zeros((16 - count, lanes), f32)], axis=0).astype(bf16)
    for f in range(size):
        s = (f - dest_ref[8] + size) % size
        out_ref[s, 0:384] = acc[:, f * lanes:(f + 1) * lanes].astype(bf16)
        out_ref[s, 384:400] = block


def input_grad_kernel(dev_ref, first_ref, d_ref, *refs):
    out_ref = refs[-1]
    parts, _, lanes = refs[0].shape
    for f in range(parts):
        cols = slice(f * lanes, (f + 1) * lanes)
        acc = first_ref[:, cols]
        for n, w_ref in enumerate(refs[:-1]):
            mask = (0, 1, 4, 5, 2, 3, 6, 7)[n]
            acc = acc + tn(d_ref[dev_ref[0] ^ mask], w_ref[f, 0:384])
        out_ref[:, cols] = acc.astype(bf16)


def hop(value, u):
    return lax.ppermute(value, CT, [(i, i ^ u) for i in range(8)])


def hop_core(value):
    return lax.ppermute(value, "core", [(0, 1), (1, 0)])


def hop_x(value):
    return lax.ppermute(value, "cx", [(0, 1), (1, 0)])


def hop_y(value):
    return lax.ppermute(value, "tp", [(0, 1), (1, 0)])


def shift_z(value, count, size):
    return lax.ppermute(value, "fsdp", [(i, (i + count) % size) for i in range(size)])


def trade(value, axes):
    return lax.all_to_all(value, axes, 0, 0, tiled=True)


def gather(value, axes, count):
    return trade(jnp.broadcast_to(value[None], (count,) + value.shape), axes)


def add_all(parts):
    total = parts[0].astype(f32)
    for p in parts[1:]:
        total = total + p.astype(f32)
    return total.astype(bf16)


def collect_z(value):
    size = lax.axis_size("fsdp")
    if size > 4:
        return add_all(trade(value, "fsdp"))
    return add_all([value[0]] + [
        lax.ppermute(value[s], "fsdp", [(i, (i + s) % size) for i in range(size)]) for s in range(1, size)])


def around_ctx(value, ctx):
    far = hop_x(value)
    return by_xor([value, hop_core(value), far, hop_core(far)], ctx)


def by_xor(parts, own):
    stacked = jnp.stack(parts)
    return jnp.stack([lax.dynamic_index_in_dim(stacked, own ^ i, 0, keepdims=False) for i in range(len(parts))])


def pair_rows(own, peer, tp):
    return jnp.concatenate([jnp.where(tp == 0, own, peer), jnp.where(tp == 0, peer, own)], axis=0)


def shards(
    layer_input,
    seq_lengths,
    deal_order,
    qkv_weight,
    qkv_bias,
    out_weight,
    out_bias,
    first_gain,
    first_shift,
    up_weight,
    up_bias,
    down_weight,
    down_bias,
    second_gain,
    second_shift,
    proj_weight,
    cot_output,
    cot_embed,
):
    own_rows, width = layer_input.shape
    half = own_rows // 2
    rows = own_rows * 4
    fs, cx, core, tp = (lax.axis_index(n) for n in ("fsdp", "cx", "core", "tp"))
    size = lax.axis_size("fsdp")
    ctx = cx * 2 + core
    dev = ctx * 2 + tp
    dev_ref = dev.astype(jnp.int32).reshape(1)
    shape = jax.ShapeDtypeStruct

    def own_half(value, which):
        return lax.dynamic_slice_in_dim(value, which * half, half, axis=0)

    def after(value, *others):
        return lax.optimization_barrier((value,) + others)[0]

    place = cx * 2 + tp
    strip = down_weight.shape[0] // 4
    units = size * strip
    shard = up_weight.shape[0]
    place_ref = place.astype(jnp.int32).reshape(1)
    ctx_ref = ctx.astype(jnp.int32).reshape(1)
    sides = width // units
    hidden_rows = shard + sides * strip
    emb = proj_weight.shape[1]
    shard_rows = out_weight.shape[0]
    vectors = [up_bias, out_bias, first_gain, first_shift, down_bias, second_gain, second_shift]
    if size > 4:
        def hidden_block(q):
            wide = up_weight.reshape(shard, size, 4, strip)
            up = lax.dynamic_index_in_dim(wide, q, 2, keepdims=False).reshape(shard, units)
            down = lax.dynamic_slice_in_dim(down_weight, q * strip, strip, axis=0)
            return jnp.concatenate([up] + [down[:, s * units:(s + 1) * units] for s in range(sides)], axis=0)

        blocks = [hidden_block(place), hidden_block(place ^ 1)]
        half_rows = shard_rows // 2
        part = lax.dynamic_slice_in_dim(proj_weight, tp * shard_rows, shard_rows, axis=0)
        vec_block = jnp.concatenate(vectors).reshape(-1, 4 * shard)
        vec_block = jnp.pad(vec_block, ((0, 16 - vec_block.shape[0]), (0, width + emb - 4 * shard)))
        beside = jnp.concatenate([out_weight, part], axis=1)
        dense_half = jnp.concatenate(
            [lax.dynamic_slice_in_dim(beside, core * half_rows, half_rows, axis=0), vec_block], axis=0)
    else:
        *blocks, dense_half = run(
            pick_kernel, (shape((hidden_rows, units), bf16),) * 2 + (shape((shard_rows // 2 + 16, width + emb), bf16),),
            "pick", 1)(jnp.stack([place, core, tp]).astype(jnp.int32), up_weight, down_weight, out_weight, proj_weight,
                       *[v.reshape(1, -1) for v in vectors])

    lanes = shard
    own_qkv = lax.dynamic_slice_in_dim(qkv_weight, ctx * 128, 128, axis=2)
    own_qkv = jnp.transpose(own_qkv, (1, 2, 0)).reshape(384, lanes)
    spare = 16 * lanes
    if size == 4:
        bias_own = qkv_bias.reshape(-1)
    else:
        bias_all = lax.all_gather(qkv_bias, "fsdp", axis=1, tiled=True)
        bias_own = lax.dynamic_slice_in_dim(bias_all, ctx * 128, 128, axis=1).reshape(-1)
    bias_block = jnp.pad(bias_own, (0, spare - 384)).reshape(16, lanes)
    weights = gather(jnp.concatenate([own_qkv, bias_block], axis=0), "fsdp", size)
    if size > 4:
        weights = jnp.concatenate(
            [jnp.transpose(weights[:, :384], (1, 0, 2)).reshape(384, width),
             jnp.pad(bias_own, (0, 16 * width - 384)).reshape(16, width)], axis=0)[None]

    x0 = own_half(layer_input, tp)
    quarter = half // 2
    x4 = [hop_x(x0[:quarter]), hop_x(x0[quarter:])]
    other = hop_y(blocks[1])
    near = [layer_input, hop_core(layer_input)]
    pair = jnp.stack([deal_order, hop_core(deal_order)])
    order = jnp.concatenate([pair, hop_x(pair)]).reshape(-1) % rows
    x5 = [hop_y(p) for p in x4]
    far = x4 + x5 + [hop_core(p) for p in x4 + x5]
    u = jnp.arange(8, dtype=jnp.int32)
    dest = dev ^ jnp.where(u < 4, (u & 6) | ((u & 1) ^ tp), u)
    slot = jnp.arange(rows, dtype=jnp.int32)
    dest_of = dev ^ jnp.where(slot < 4 * half, ((slot // half) & 6) | (((slot // half) & 1) ^ tp), slot // half)
    arrival = dest_of * half + slot % half
    first_len = seq_lengths[0, :1]
    packed_index = (ctx ^ (slot // own_rows)) * own_rows + slot % own_rows
    position, rank, meet = row_places(order, packed_index, seq_lengths[0], arrival)
    rank = rank[None]
    cos_t, sin_t = rope_tables_t(position)

    hidden_own = jnp.where(tp == core, blocks[0], other)
    hidden_own, weights = lax.optimization_barrier((hidden_own, weights))
    hidden0 = gather(hidden_own, "fsdp", size)

    near_mixed = qkv_rope(ctx_ref, near, weights, cos_t[:, :rows // 2], sin_t[:, :rows // 2])
    far, near_mixed, dense_half = lax.optimization_barrier((far, near_mixed, dense_half))
    dense_parts = lax.all_gather(dense_half, ("tp", "fsdp"), axis=0)
    far_mixed = qkv_rope(ctx_ref, far, weights, cos_t[:, rows // 2:], sin_t[:, rows // 2:])
    hidden0, far_mixed = lax.optimization_barrier((hidden0, far_mixed))
    cut = size // 2
    hiddens = [hidden0, hop_y(hidden0), hop_x(hidden0), hop(hidden0[:cut], 5), None]
    att, sorted_t, att_t, lse = attention_forward(first_len, meet, dest, rank, near_mixed, far_mixed)
    att, dense_parts, hiddens[1:4] = lax.optimization_barrier((att, dense_parts, hiddens[1:4]))
    att = trade(att, CT)
    dense, vec, up_b = run(
        dense_natural_kernel,
        (shape((width, width + emb), bf16), shape((8, width), f32), shape((1, 4 * units), f32)), "dense_natural", 1)(
        jnp.stack([core, place]).astype(jnp.int32), dense_parts, hop_core(dense_parts))
    out_b, gain1, shift1, down_b, gain2, shift2 = (vec[i:i + 1] for i in range(6))
    hiddens[4] = hop(after(hidden0[cut:], att), 5)

    f_rows, b_rows = shape((half, width), f32), shape((half, width), bf16)
    normed, hat1, rstd1, normed_low = run(
        out_proj_kernel, (f_rows, f_rows, shape((half, 1), f32), b_rows), "out_proj")(
        dense, x0, att, out_b, gain1, shift1)
    normed_peer = hop_core(normed_low)
    hidden = shape((own_rows, 4 * units), bf16)
    act, slope, own_down, peer_down = run(mlp_kernel, (hidden, hidden, f_rows, b_rows), "mlp", flops=8_000_000_000)(
        normed_low, normed_peer, up_b, *hiddens)
    w_own = after(weights, normed_low)
    w_y, w_x = hop_y(w_own), hop_x(w_own)
    own_down, peer_down, w_y, w_x = lax.optimization_barrier((own_down, peer_down, w_y, w_x))
    w_cut = max(1, w_own.shape[0] // 2)
    w_xy = [hop(after(w_own[:w_cut], own_down), 5)]
    vec_shape = shape((8, width), f32)
    final_low, embed_low, grad_second, g2, proj_grad, vec2 = run(
        partial(head_kernel, shard_rows),
        (b_rows, shape((half, emb), bf16), f_rows, b_rows, shape((width, emb), bf16), vec_shape), "heads",
        scratch=[pltpu.VMEM((width, emb), bf16)])(
        normed, own_down, hop_core(peer_down), down_b, gain2, shift2, dense,
        own_half(cot_output, tp), own_half(cot_embed, tp))
    g2, w_xy[0] = lax.optimization_barrier((g2, w_xy[0]))
    g2_peer = hop_core(g2)
    if w_cut < w_own.shape[0]:
        w_xy.append(hop(after(w_own[w_cut:], w_xy[0]), 5))
    final_halves = [hop_y(after(final_low[:half // 2], g2))]
    g1, up_bias_part, own_normed, peer_normed = run(
        mlp_back_kernel, (hidden, shape((1, 4 * units), f32), f_rows, b_rows), "mlp_back", flops=16_000_000_000)(
        g2, g2_peer, slope, *hiddens)
    own_normed, final_halves[0], w_xy = lax.optimization_barrier((own_normed, final_halves[0], w_xy))
    w_near = [w_own, w_y, w_x, jnp.concatenate(w_xy, axis=0)]
    w_all = w_near + [hop_core(after(w, own_normed)) for w in w_near]
    grad_first, g0, att_grad, vec1 = run(
        first_back_kernel, (f_rows, b_rows, shape((8, half, 128), bf16), vec_shape), "first_back")(
        grad_second, own_normed, hop_core(peer_normed), hat1, rstd1, gain1, dense)
    att_grad, w_all = lax.optimization_barrier((att_grad, w_all))
    att_grad = lax.all_to_all(att_grad, CT, 0, 0, tiled=True)
    dense_rows = (shard_rows // 4 + shard_rows // 8) * sides
    dense_grad = run(out_weight_kernel, shape((2, 4, size, dense_rows, units), bf16), "out_weight")(
        g0, att, proj_grad, vec2, vec1)
    dense_own = lax.dynamic_index_in_dim(dense_grad, core, 0, keepdims=False)
    dense_recv = hop_core(lax.dynamic_index_in_dim(dense_grad, 1 - core, 0, keepdims=False))
    *up_grads, down_grad = run(
        mlp_weights_kernel,
        (shape((size, shard + 16 + dense_rows, units), bf16),) * 4 + (shape((size, 4, strip, width), bf16),),
        "mlp_weights", 1, flops=16_000_000_000)(
        place_ref, normed_low, normed_peer, g2, g2_peer, act, g1, up_bias_part, dense_own, dense_recv)
    att_grad, up_grads, down_grad = lax.optimization_barrier((att_grad, up_grads, down_grad))
    XY = ("cx", "tp")
    down_parts = trade(down_grad, "fsdp")
    up_parts = [up_grads[0], hop_y(up_grads[1]), hop_x(up_grads[2]), hop(up_grads[3], 5)]
    final_rest, embed_late = after(final_low[half // 2:], att_grad), after(embed_low, att_grad)
    final_halves.append(hop_y(final_rest))
    embed_peer = hop_y(embed_late)
    grad_qkv, qkv_bias_part = attention_backward(
        first_len, meet, dest, rank, sorted_t, att_t, lse, cos_t, sin_t, att_grad)
    grad_qkv, up_parts, down_parts, final_halves, embed_peer = lax.optimization_barrier(
        (grad_qkv, up_parts, down_parts, final_halves, embed_peer))
    final_peer = jnp.concatenate(final_halves, axis=0)
    grad_rows = trade(grad_qkv, CT)

    base = fs if size <= 4 else jnp.zeros_like(fs)
    up_sum, *down_sums = run(
        sum_kernel, (shape(up_grads[0].shape, bf16),) + (shape((strip, width), bf16),) * 4, "sums", 1)(
        jnp.stack([base, place]).astype(jnp.int32), *up_parts, down_parts)
    up_own = collect_z(up_sum)
    down_own = add_all([down_sums[0], hop_y(down_sums[1]), hop_x(down_sums[2]), hop(down_sums[3], 5)])

    own_q = collect_z(run(qkv_weight_kernel, shape((size, 400, lanes), bf16), "qkv_weight", 1)(
        jnp.concatenate([dest, base[None]]).astype(jnp.int32), grad_qkv, qkv_bias_part, *near, *far))
    q_all = around_ctx(own_q, ctx)
    dense_all = around_ctx(up_own[shard + 16:], ctx)

    input_low = run(input_grad_kernel, b_rows, "input_grad", 1)(dev_ref, grad_first, grad_rows, *w_all)
    input_peer = hop_y(input_low)

    hidden_grad = jnp.concatenate(
        [up_own[:shard + 16]] + [down_own[:, s * units:(s + 1) * units] for s in range(sides)], axis=0)
    hidden_core = hop_core(hidden_grad)
    halves = jnp.stack([jnp.where(core == 0, hidden_grad, hidden_core), jnp.where(core == 0, hidden_core, hidden_grad)])
    joined = trade(jnp.concatenate([halves, halves], axis=0), XY)
    up_weight_grad, down_weight_grad = run(
        hidden_join_kernel, (shape(up_weight.shape, f32), shape(down_weight.shape, f32)), "hidden_join")(joined)
    up_bias_grad = lax.dynamic_slice_in_dim(joined[:, shard], fs * strip, strip, axis=1).reshape(-1).astype(f32)

    qkv_weight_grad = jnp.transpose(q_all[:, :384].reshape(4, 3, 128, lanes), (3, 1, 0, 2)).reshape(
        lanes, 3, 512).astype(f32)
    qb = jnp.transpose(q_all[:, 384:].reshape(4, -1)[:, :384].reshape(4, 3, 128), (1, 0, 2)).reshape(3, 512)
    bias_width = qkv_bias.shape[1]
    qkv_bias_grad = lax.dynamic_slice_in_dim(qb, fs * bias_width, bias_width, axis=1).astype(f32)

    thin, tail_rows = shard_rows // 4, shard_rows // 8
    out_weight_grad = jnp.transpose(
        dense_all[:, :thin * sides].reshape(4, sides, thin, units), (0, 2, 1, 3)).reshape(shard_rows, width).astype(f32)
    rest = dense_all[:, thin * sides:].reshape(4, sides, tail_rows, units // 128, 128)[:3]
    rest = jnp.transpose(rest, (1, 3, 2, 0, 4)).reshape(shard_rows, 384)
    rest = pair_rows(rest, hop_y(rest), tp).astype(f32)
    proj_weight_grad = rest[:, :emb]
    sums = jnp.transpose(rest[:, emb:emb + 6])

    return (
        pair_rows(final_low, final_peer, tp),
        pair_rows(embed_low, embed_peer, tp),
        pair_rows(input_low, input_peer, tp),
        qkv_weight_grad,
        qkv_bias_grad,
        out_weight_grad,
        sums[5],
        sums[3],
        sums[4],
        up_weight_grad,
        up_bias_grad,
        down_weight_grad,
        sums[2],
        sums[0],
        sums[1],
        proj_weight_grad,
    )


def solution(mesh):
    fine = Mesh(
        mesh.devices.reshape(mesh.shape["fsdp"], mesh.shape["ctx"] // 2, 2, mesh.shape["tp"]),
        ("fsdp", "cx", "core", "tp"))
    by_rows = ("fsdp", "cx", "core")
    placed = (
        P(by_rows, None),
        P("fsdp", None),
        P(by_rows),
        P("fsdp", None, "tp"),
        P(None, ("tp", "fsdp")),
        P(("tp", "fsdp"), None),
        P("fsdp"),
        P("fsdp"),
        P("fsdp"),
        P("fsdp", "tp"),
        P(("tp", "fsdp")),
        P(("tp", "fsdp"), None),
        P("fsdp"),
        P("fsdp"),
        P("fsdp"),
        P("fsdp", None),
        P(by_rows, None),
        P(by_rows, None),
    )
    outs = (P(by_rows, None), P(by_rows, None), P(by_rows, None)) + placed[3:16]
    return jax.shard_map(shards, mesh=fine, in_specs=placed, out_specs=outs, check_vma=False)
```

time: 1850 us -> 631 us (0.34)
  waiting for transfers between devices: 970 us -> 139 us
  matrix products: 475 us -> 0.09 us
  Pallas kernels: 0 us -> 294 us
  blocking collectives: 123 us -> 0 us
  starting transfers between devices: 2.16 us -> 79.2 us
  local copies, waits for them, and re-layouts: 129 us -> 61.1 us
  other arithmetic: 97.9 us -> 38.5 us
  loops' own time: 31.8 us -> 0 us
    dot_general x71 -> x1, matrix products: 475 us -> 0.09 us  [row_places(): jnp.dot(flags.astype(bf16), before.astype(bf16), preferred_element_type=f32)]
    all_gather x12 -> x1, waiting for transfers between devices: 407 us -> 0.01 us  [shards(): dense_parts = lax.all_gather(dense_half, ('tp', 'fsdp'), axis=0)]
    pallas_call x0 -> x17, Pallas kernels: none -> 294 us  [the longest x15 132 us: call(): pl.pallas_call(kernel, out_shape=out_shape, in_specs=[sm] * scalars + [vm...]
    reduce_scatter x7 -> x0, waiting for transfers between devices: 288 us -> none  [the longest x1 79.5 us: shards(): lax.psum_scatter(up_weight_grad.astype(jnp.bfloat16), 'fsdp', scatter_dim...]
    psum x5 -> x0, waiting for transfers between devices: 267 us -> none  [the longest x1 65 us: shards(): lax.psum(jnp.einsum('twe,dwe->td', mixed_low, qkv_full, preferred_element...]
    ppermute x0 -> x54, waiting for transfers between devices: none -> 113 us  [the longest x12 49.4 us: hop_y(): return lax.ppermute(value, 'tp', [(0, 1), (1, 0)])]
    all_gather x10 -> x0, blocking collectives: 100 us -> none  [the longest x1 17 us: shards(): lax.all_gather(proj_weight, 'fsdp', axis=0, tiled=True)]
    gather x8 -> x0, local copies, waits for them, and re-layouts: 59.1 us -> none  [the longest x1 10.5 us: shards(): ordered_output = rows_output[chosen_rows]]
  transfers between devices with their start and end apart: 25 -> 62, of which waited for: 21 -> 20; matrix products, arithmetic and copies ran while one was open for 18% -> 12% of each run, Pallas kernels for 0% -> 42%
where the time goes in v2:
time: 631 us; the launch traced here: 626 us
  Pallas kernels  294 us (47%)
  waiting for transfers between devices  139 us (22%)
  starting transfers between devices  79.2 us (13%)
  local copies, waits for them, and re-layouts  61.1 us (10%)
  other arithmetic  38.5 us (6%)
  between operations  15 us (2%)
    pallas_call x15, Pallas kernels, call(): pl.pallas_call(kernel, out_shape=out_shape, in_specs=[sm] * scalars + [vm...  132 us
    pallas_call x1, Pallas kernels, attention_backward(): pl.pallas_call(backward_kernel, out_shape=(jax.ShapeDtypeStruct((8, 384,...  93.8 us
    pallas_call x1, Pallas kernels, attention_forward(): pl.pallas_call(forward_kernel, out_shape=(jax.ShapeDtypeStruct((8, rows /...  67.9 us
    ppermute x12, waiting for transfers between devices, hop_y(): return lax.ppermute(value, 'tp', [(0, 1), (1, 0)])  49.4 us
    ppermute x6, waiting for transfers between devices, hop(): return lax.ppermute(value, CT, [(i, i ^ u) for i in range(8)])  28.5 us
    all_to_all x6, starting transfers between devices, trade(): return lax.all_to_all(value, axes, 0, 0, tiled=True)  28.2 us
    all_to_all x6, waiting for transfers between devices, trade(): return lax.all_to_all(value, axes, 0, 0, tiled=True)  26 us
    unnamed x114, local copies, waits for them, and re-layouts  19.2 us
  transfers between devices with their start and end apart: 62, of which 20 were waited for; matrix products, arithmetic and copies ran while one was open for 12% of the time, Pallas kernels for 42%

profile of v2, /device:TPU:0, one launch (start us, length us, event | category | flops | bytes accessed | tf_op | source)
XLA Modules:
  0.0 626.4 jit_solution(5972174263017888352)
XLA Ops:
  25.5 4.9 all-to-all-start
  36.9 8.6 %select_reduce_fusion = s32[4096]{0:T(1024)S(1)} fusion(s32[4096]{0:T(1024)S(1)} %get-tuple-element.379, s32[4096]{0:T(1024)S(1)} %get-tuple-element.380, s32[4096]{0:T(1024)S(1)} %add_select_fusion.3), kind=kLoop, calls=%fused_computation | loop fusion | flops 50327552 | bytes 65536 | tf_op jit(solution)/shard_map/reduce_sum | solution.py:350
  52.2 5.2 all-to-all-start.1
  64.0 9.9 %collective-permute-done.4.refs_2_.refs_4_ = bf16[256,1024]{1,0:T(8,128)(2,1)S(1)} collective-permute-done((bf16[256,1024]{1,0:T(8,128)(2,1)}, bf16[256,1024]{1,0:T(8,128)(2,1)S(1)}, u32[]{:S(2)}, u32[]{:S(2)}) %collective-permute-start.4) | collective-permute-done | bytes 524320 | tf_op jit(solution)/shard_map/ppermute | solution.py:753
  73.9 9.3 %collective-permute-done.5.refs_3_.refs_5_ = bf16[256,1024]{1,0:T(8,128)(2,1)} collective-permute-done((bf16[256,1024]{1,0:T(8,128)(2,1)}, bf16[256,1024]{1,0:T(8,128)(2,1)}, u32[]{:S(2)}, u32[]{:S(2)}) %collective-permute-start.5) | collective-permute-done | bytes 524320 | tf_op jit(solution)/shard_map/ppermute | solution.py:753
  84.1 5.7 qkv_rope.2.near_ref
  92.2 5.6 qkv_rope.3.far_ref
  97.8 7.4 %all-to-all-done.1.refs_0_ = bf16[4,512,512]{2,1,0:T(8,128)(2,1)} async-done(((bf16[4,512,512]{2,1,0:T(8,128)(2,1)}), bf16[4,512,512]{2,1,0:T(8,128)(2,1)}, u32[]{:S(2)}, u32[]{:S(2)}) %all-to-all-start.1) | async-done | bytes 2097184 | tf_op jit(solution)/shard_map/all_to_all | solution.py:761
  111.4 67.9 %attention_forward.1 = (bf16[8,512,128]{2,1,0:T(8,128)(2,1)}, bf16[384,4096]{1,0:T(8,128)(2,1)}, bf16[128,4096]{1,0:T(8,128)(2,1)}, f32[8,4096]{1,0:T(8,128)}) custom-call(s32[1]{0:T(128)} %bitcast.116, s32[64]{0:T(128)} %reshape.324.meet_ref, s32[8]{0:T(128)} %fusion.34.dest_ref, s32[1,4096]{1,0:T(1,128)} %reshape_select_fusion.rank_ref, ...), custom_call_target="tpu_custom_call" | custom-call | flops 60000002048 | bytes 16000000 | tf_op jit(solution)/shard_map/attention_forward/pallas_call | solution.py:156
  179.3 4.8 collective-permute-done.12.refs_1_
  184.2 4.3 all-to-all-start.2
  191.4 11.2 %all-to-all-done.2.att_ref = bf16[8,512,128]{2,1,0:T(8,128)(2,1)S(1)} async-done(((bf16[8,512,128]{2,1,0:T(8,128)(2,1)}), bf16[8,512,128]{2,1,0:T(8,128)(2,1)S(1)}, u32[]{:S(2)}, u32[]{:S(2)}) %all-to-all-start.2) | async-done | bytes 1048608 | tf_op jit(solution)/shard_map/all_to_all | solution.py:761
  209.5 7.9 %out_proj.1 = (f32[512,1024]{1,0:T(8,128)}, f32[512,1024]{1,0:T(8,128)}, f32[512,1]{1,0:T(8,128)}, bf16[512,1024]{1,0:T(8,128)(2,1)}) custom-call(bf16[1024,1312]{1,0:T(8,128)(2,1)} %get-tuple-element.145.w_ref.dense_ref, bf16[512,1024]{1,0:T(8,128)(2,1)} %constant_dynamic-slice_fusion.14.x_ref, bf16[8,512,128]{2,1,0:T(8,128)(2,1)} %copy-done.22, ...), custom_call_target="tpu_custom_call" | custom-call | flops 2000000000 | bytes 8000000 | tf_op jit(solution)/shard_map/out_proj/pallas_call | solution.py:32
  219.5 10.3 %collective-permute-done.17.refs_4_ = bf16[2,512,512]{2,1,0:T(8,128)(2,1)S(1)} collective-permute-done((bf16[2,512,512]{2,1,0:T(8,128)(2,1)}, bf16[2,512,512]{2,1,0:T(8,128)(2,1)S(1)}, u32[]{:S(2)}, u32[]{:S(2)}) %collective-permute-start.17) | collective-permute-done | bytes 1048608 | tf_op jit(solution)/shard_map/ppermute | solution.py:741
  231.0 18.7 %mlp.1 = (bf16[1024,2048]{1,0:T(8,128)(2,1)}, bf16[1024,2048]{1,0:T(8,128)(2,1)}, f32[512,1024]{1,0:T(8,128)}, bf16[512,1024]{1,0:T(8,128)(2,1)}) custom-call(bf16[512,1024]{1,0:T(8,128)(2,1)} %get-tuple-element.149.own_ref.own_n, bf16[512,1024]{1,0:T(8,128)(2,1)} %copy-done.41, f32[1,2048]{1,0:T(1,128)} %get-tuple-element.150.bias_ref, ...), custom_call_target="tpu_custom_call" | custom-call | flops 8000000000 | bytes 8000000 | tf_op jit(solution)/shard_map/mlp/pallas_call | solution.py:32
  254.3 9.6 %heads.1 = (bf16[512,1024]{1,0:T(8,128)(2,1)}, bf16[512,288]{1,0:T(8,128)(2,1)}, f32[512,1024]{1,0:T(8,128)}, bf16[512,1024]{1,0:T(8,128)(2,1)}, bf16[1024,288]{1,0:T(8,128)(2,1)}, /*index=5*/f32[8,1024]{1,0:T(8,128)}) custom-call(f32[512,1024]{1,0:T(8,128)} %get-tuple-element.148.normed_ref, f32[512,1024]{1,0:T(8,128)} %get-tuple-element.158.own_ref, ...), custom_call_target="tpu_custom_call" | custom-call | flops 2000000000 | bytes 8000000 | tf_op jit(solution)/shard_map/heads/pallas_call | solution.py:32
  267.8 16.6 %mlp_back.1 = (bf16[1024,2048]{1,0:T(8,128)(2,1)}, f32[1,2048]{1,0:T(1,128)}, f32[512,1024]{1,0:T(8,128)}, bf16[512,1024]{1,0:T(8,128)(2,1)}) custom-call(bf16[512,1024]{1,0:T(8,128)(2,1)} %get-tuple-element.167.own_ref.own_g, bf16[512,1024]{1,0:T(8,128)(2,1)} %copy-done.42, bf16[1024,2048]{1,0:T(8,128)(2,1)} %get-tuple-element.168.slope_ref, ...), custom_call_target="tpu_custom_call" | custom-call | flops 16000000000 | bytes 8000000 | tf_op jit(solution)/shard_map/mlp_back/pallas_call | solution.py:32
  288.6 11.1 %collective-permute-done.24 = bf16[2,400,256]{2,1,0:T(8,128)(2,1)} collective-permute-done((bf16[2,400,256]{2,1,0:T(8,128)(2,1)}, bf16[2,400,256]{2,1,0:T(8,128)(2,1)}, u32[]{:S(2)}, u32[]{:S(2)}) %collective-permute-start.24) | collective-permute-done | bytes 409632 | tf_op jit(solution)/shard_map/ppermute | solution.py:741
  299.8 9.0 %collective-permute-done.23 = bf16[256,1024]{1,0:T(8,128)(2,1)S(1)} collective-permute-done((bf16[256,1024]{1,0:T(8,128)(2,1)}, bf16[256,1024]{1,0:T(8,128)(2,1)S(1)}, u32[]{:S(2)}, u32[]{:S(2)}) %collective-permute-start.23) | collective-permute-done | bytes 524320 | tf_op jit(solution)/shard_map/ppermute | solution.py:753
  309.8 8.8 %first_back.1 = (f32[512,1024]{1,0:T(8,128)}, bf16[512,1024]{1,0:T(8,128)(2,1)}, bf16[8,512,128]{2,1,0:T(8,128)(2,1)}, f32[8,1024]{1,0:T(8,128)}) custom-call(f32[512,1024]{1,0:T(8,128)} %get-tuple-element.164.second_ref, f32[512,1024]{1,0:T(8,128)} %get-tuple-element.173.own_ref, bf16[512,1024]{1,0:T(8,128)(2,1)} %copy-done.21, ...), custom_call_target="tpu_custom_call" | custom-call | flops 2000000000 | bytes 8000000 | tf_op jit(solution)/shard_map/first_back/pallas_call | solution.py:32
  318.6 4.8 out_weight.1
  339.3 18.4 %mlp_weights.1 = (bf16[4,368,512]{2,1,0:T(8,128)(2,1)}, bf16[4,368,512]{2,1,0:T(8,128)(2,1)}, bf16[4,368,512]{2,1,0:T(8,128)(2,1)}, bf16[4,368,512]{2,1,0:T(8,128)(2,1)}, bf16[4,4,128,1024]{3,2,1,0:T(8,128)(2,1)}) custom-call(s32[1]{0:T(128)} %bitcast.1.place_ref, bf16[512,1024]{1,0:T(8,128)(2,1)} %get-tuple-element.149.own_ref.own_n, ...), custom_call_target="tpu_custom_call" | custom-call | flops 16000000000 | bytes 8000000 | tf_op jit(solution)/shard_map/mlp_weights/pallas_call | solution.py:32
  362.2 5.3 all-to-all-start.4
  369.6 93.8 %attention_backward.1 = (bf16[8,384,512]{2,1,0:T(8,128)(2,1)}, f32[384,1]{1,0:T(8,128)}) custom-call(s32[1]{0:T(128)} %bitcast.117, s32[64]{0:T(128)} %reshape.324.meet_ref, s32[8]{0:T(128)} %fusion.34.dest_ref, s32[1,4096]{1,0:T(1,128)} %reshape_select_fusion.rank_ref, bf16[384,4096]{1,0:T(8,128)(2,1)} %get-tuple-element.161.sorted_ref, ...), custom_call_target="tpu_custom_call" | custom-call | flops 89999998976 | bytes 16000000 | tf_op jit(solution)/shard_map/attention_backward/pallas_call | solution.py:291
  472.3 8.7 %qkv_weight.1 = bf16[4,400,256]{2,1,0:T(8,128)(2,1)} custom-call(s32[9]{0:T(128)} %pad_add_fusion.3.dest_ref, bf16[8,384,512]{2,1,0:T(8,128)(2,1)} %get-tuple-element.214.d_ref, f32[384,1]{1,0:T(8,128)} %get-tuple-element.223.bias_ref, bf16[1024,1024]{1,0:T(8,128)(2,1)} %refs_0_.3, bf16[1024,1024]{1,0:T(8,128)(2,1)} %collective-permute-done.11.refs_1_, ...), custom_call_target="tpu_custom_call" | custom-call | flops 2000000000 | bytes 8000000 | tf_op jit(solution)/shard_map/qkv_weight/pallas_call | solution.py:32
  487.8 6.5 %sums.1 = (bf16[4,368,512]{2,1,0:T(8,128)(2,1)}, bf16[128,1024]{1,0:T(8,128)(2,1)}, bf16[128,1024]{1,0:T(8,128)(2,1)}, bf16[128,1024]{1,0:T(8,128)(2,1)}, bf16[128,1024]{1,0:T(8,128)(2,1)}) custom-call(s32[2]{0:T(128)} %pad_add_fusion.4.index_ref, bf16[4,368,512]{2,1,0:T(8,128)(2,1)} %get-tuple-element.224.p0, bf16[4,368,512]{2,1,0:T(8,128)(2,1)} %copy-done.16, ...), custom_call_target="tpu_custom_call" | custom-call | flops 2000000000 | bytes 8000000 | tf_op jit(solution)/shard_map/sums/pallas_call | solution.py:32
  509.4 7.1 %collective-permute-done.52 = bf16[128,1024]{1,0:T(8,128)(2,1)} collective-permute-done((bf16[128,1024]{1,0:T(8,128)(2,1)}, bf16[128,1024]{1,0:T(8,128)(2,1)}, u32[]{:S(2)}, u32[]{:S(2)}) %collective-permute-start.52) | collective-permute-done | bytes 262176 | tf_op jit(solution)/shard_map/ppermute | solution.py:741
  522.5 18.8 %collective-permute-done.44 = bf16[368,512]{1,0:T(8,128)(2,1)S(1)} collective-permute-done((bf16[368,512]{1,0:T(8,128)(2,1)}, bf16[368,512]{1,0:T(8,128)(2,1)S(1)}, u32[]{:S(2)}, u32[]{:S(2)}) %collective-permute-start.44) | collective-permute-done | bytes 376864 | tf_op jit(solution)/shard_map/ppermute | solution.py:780
  562.5 4.5 all-to-all-start.6
  568.4 10.1 %input_grad.1 = bf16[512,1024]{1,0:T(8,128)(2,1)} custom-call(s32[1]{0:T(128)} %bitcast.16.dev_ref, f32[512,1024]{1,0:T(8,128)} %get-tuple-element.213.first_ref, bf16[8,384,512]{2,1,0:T(8,128)(2,1)} %copy-done.2, bf16[4,400,256]{2,1,0:T(8,128)(2,1)} %copy-done.3, bf16[4,400,256]{2,1,0:T(8,128)(2,1)} %collective-permute-done.18.refs_1_, ...), custom_call_target="tpu_custom_call" | custom-call | flops 2000000000 | bytes 8000000 | tf_op jit(solution)/shard_map/input_grad/pallas_call | solution.py:32
  586.6 7.3 %all-to-all-done.6.part_ref = bf16[4,528,512]{2,1,0:T(8,128)(2,1)} async-done(((bf16[4,528,512]{2,1,0:T(8,128)(2,1)}), bf16[4,528,512]{2,1,0:T(8,128)(2,1)}, u32[]{:S(2)}, u32[]{:S(2)}) %all-to-all-start.6) | async-done | bytes 2162720 | tf_op jit(solution)/shard_map/all_to_all | solution.py:761
  599.3 16.3 %collective-permute-done.36 = bf16[512,1024]{1,0:T(8,128)(2,1)} collective-permute-done((bf16[512,1024]{1,0:T(8,128)(2,1)}, bf16[512,1024]{1,0:T(8,128)(2,1)}, u32[]{:S(2)}, u32[]{:S(2)}) %collective-permute-start.36) | collective-permute-done | bytes 1048608 | tf_op jit(solution)/shard_map/ppermute | solution.py:753
  (318 shorter events, 173.0 us)
Async XLA Ops:
  7.3 23.7 %collective-permute-start = (s32[1024]{0:T(1024)}, s32[1024]{0:T(1024)S(1)}, u32[]{:S(2)}, u32[]{:S(2)}) collective-permute-start(s32[1024]{0:T(1024)} %param.20), channel_id=1, source_target_pairs={{0,2},{2,0},{1,3},{3,1},{4,6},{6,4},{5,7},{7,5},{8,10},{10,8},{9,1... | collective-permute-start | bytes 12296 | tf_op jit(solution)/shard_map/ppermute | solution.py:745
  7.8 76.3 %collective-permute-start.11 = (bf16[1024,1024]{1,0:T(8,128)(2,1)}, bf16[1024,1024]{1,0:T(8,128)(2,1)}, u32[]{:S(2)}, u32[]{:S(2)}) collective-permute-start(bf16[1024,1024]{1,0:T(8,128)(2,1)} %refs_0_.3), channel_id=1, source_target_pairs={{0,2},{2,0},{1,3},{3,1},{4,6},{6,4},{5,7},{7,5},{8,10},{10,8},{9,1... | collective-permute-start | bytes 6291464 | tf_op jit(solution)/shard_map/ppermute | solution.py:745
  10.2 48.6 %collective-permute-start.2 = (bf16[256,1024]{1,0:T(8,128)(2,1)}, bf16[256,1024]{1,0:T(8,128)(2,1)}, u32[]{:S(2)}, u32[]{:S(2)}) collective-permute-start(bf16[256,1024]{1,0:T(8,128)(2,1)} %get-tuple-element.337), channel_id=1, source_target_pairs={{0,4},{4,0},{1,5},{5,1},{2,6},{6,2},{3,7},{7,3},{8,12},{12,8},{9,1... | collective-permute-start | bytes 1572872 | tf_op jit(solution)/shard_map/ppermute | solution.py:749
  13.1 47.3 %collective-permute-start.3 = (bf16[256,1024]{1,0:T(8,128)(2,1)}, bf16[256,1024]{1,0:T(8,128)(2,1)}, u32[]{:S(2)}, u32[]{:S(2)}) collective-permute-start(bf16[256,1024]{1,0:T(8,128)(2,1)} %get-tuple-element.336), channel_id=1, source_target_pairs={{0,4},{4,0},{1,5},{5,1},{2,6},{6,2},{3,7},{7,3},{8,12},{12,8},{9,1... | collective-permute-start | bytes 1572872 | tf_op jit(solution)/shard_map/ppermute | solution.py:749
  21.4 27.2 %collective-permute-start.10 = (bf16[512,512]{1,0:T(8,128)(2,1)}, bf16[512,512]{1,0:T(8,128)(2,1)S(1)}, u32[]{:S(2)}, u32[]{:S(2)}) collective-permute-start(bf16[512,512]{1,0:T(8,128)(2,1)} %get-tuple-element.127), channel_id=1, source_target_pairs={{0,1},{1,0},{2,3},{3,2},{4,5},{5,4},{6,7},{7,6},{8,9},{9,8},{10,11... | collective-permute-start | bytes 1572872 | tf_op jit(solution)/shard_map/ppermute | solution.py:753
  25.5 25.1 %all-to-all-start = ((bf16[4,400,256]{2,1,0:T(8,128)(2,1)}), bf16[4,400,256]{2,1,0:T(8,128)(2,1)S(1)}, u32[]{:S(2)}, u32[]{:S(2)}) async-start(bf16[4,400,256]{2,1,0:T(8,128)(2,1)} %broadcast_in_dim.48), calls=%async_computation | async-start | bytes 1638400 | tf_op jit(solution)/shard_map/all_to_all | solution.py:761
  52.2 53.0 %all-to-all-start.1 = ((bf16[4,512,512]{2,1,0:T(8,128)(2,1)}), bf16[4,512,512]{2,1,0:T(8,128)(2,1)}, u32[]{:S(2)}, u32[]{:S(2)}) async-start(bf16[4,512,512]{2,1,0:T(8,128)(2,1)} %broadcast_in_dim.49), calls=%async_computation.1 | async-start | bytes 4194304 | tf_op jit(solution)/shard_map/all_to_all | solution.py:761
  57.4 121.9 %all-gather.3.cloned.1.call-start = ((), (), s32[]{:S(2)}) async-start(), calls=%async_computation.7 | async-start | bytes 2027520 | tf_op jit(solution)/shard_map/all_gather | solution.py:907
  63.5 26.3 %collective-permute-start.6 = (bf16[256,1024]{1,0:T(8,128)(2,1)}, bf16[256,1024]{1,0:T(8,128)(2,1)S(1)}, u32[]{:S(2)}, u32[]{:S(2)}) collective-permute-start(bf16[256,1024]{1,0:T(8,128)(2,1)} %collective-permute-done.2.refs_0_.refs_2_), channel_id=1, source_target_pairs={{0,2},{2,0},{1,3},{3,1},{4,6},{6,4},{5,7},{7,5},{8,10},{10,8},{9,1... | collective-permute-start | bytes 1572872 | tf_op jit(solution)/shard_map/ppermute | solution.py:745
  63.5 26.3 %collective-permute-start.7 = (bf16[256,1024]{1,0:T(8,128)(2,1)}, bf16[256,1024]{1,0:T(8,128)(2,1)S(1)}, u32[]{:S(2)}, u32[]{:S(2)}) collective-permute-start(bf16[256,1024]{1,0:T(8,128)(2,1)} %collective-permute-done.3.refs_1_.refs_3_), channel_id=1, source_target_pairs={{0,2},{2,0},{1,3},{3,1},{4,6},{6,4},{5,7},{7,5},{8,10},{10,8},{9,1... | collective-permute-start | bytes 1572872 | tf_op jit(solution)/shard_map/ppermute | solution.py:745
  105.2 79.0 %collective-permute-start.12 = (bf16[4,512,512]{2,1,0:T(8,128)(2,1)}, bf16[4,512,512]{2,1,0:T(8,128)(2,1)}, u32[]{:S(2)}, u32[]{:S(2)}) collective-permute-start(bf16[4,512,512]{2,1,0:T(8,128)(2,1)} %all-to-all-done.1.refs_0_), channel_id=1, source_target_pairs={{0,1},{1,0},{2,3},{3,2},{4,5},{5,4},{6,7},{7,6},{8,9},{9,8},{10,11... | collective-permute-start | bytes 6291464 | tf_op jit(solution)/shard_map/ppermute | solution.py:753
  106.7 77.4 %collective-permute-start.13 = (bf16[4,512,512]{2,1,0:T(8,128)(2,1)}, bf16[4,512,512]{2,1,0:T(8,128)(2,1)}, u32[]{:S(2)}, u32[]{:S(2)}) collective-permute-start(bf16[4,512,512]{2,1,0:T(8,128)(2,1)} %all-to-all-done.1.refs_0_), channel_id=1, source_target_pairs={{0,4},{4,0},{1,5},{5,1},{2,6},{6,2},{3,7},{7,3},{8,12},{12,8},{9,1... | collective-permute-start | bytes 6291464 | tf_op jit(solution)/shard_map/ppermute | solution.py:749
  110.9 68.4 %collective-permute-start.14 = (bf16[2,512,512]{2,1,0:T(8,128)(2,1)S(1)}, bf16[2,512,512]{2,1,0:T(8,128)(2,1)}, u32[]{:S(2)}, u32[]{:S(2)}) collective-permute-start(bf16[2,512,512]{2,1,0:T(8,128)(2,1)S(1)} %get-tuple-element.335), channel_id=1, source_target_pairs={{0,5},{1,4},{2,7},{3,6},{4,1},{5,0},{6,3},{7,2},{8,13},{9,12},{10,... | collective-permute-start | bytes 3145736 | tf_op jit(solution)/shard_map/ppermute | solution.py:741
  202.5 27.2 %collective-permute-start.17 = (bf16[2,512,512]{2,1,0:T(8,128)(2,1)}, bf16[2,512,512]{2,1,0:T(8,128)(2,1)S(1)}, u32[]{:S(2)}, u32[]{:S(2)}) collective-permute-start(bf16[2,512,512]{2,1,0:T(8,128)(2,1)} %get-tuple-element.154), channel_id=1, source_target_pairs={{0,5},{1,4},{2,7},{3,6},{4,1},{5,0},{6,3},{7,2},{8,13},{9,12},{10,... | collective-permute-start | bytes 3145736 | tf_op jit(solution)/shard_map/ppermute | solution.py:741
  217.4 32.4 %collective-permute-start.18 = (bf16[4,400,256]{2,1,0:T(8,128)(2,1)S(1)}, bf16[4,400,256]{2,1,0:T(8,128)(2,1)}, u32[]{:S(2)}, u32[]{:S(2)}) collective-permute-start(bf16[4,400,256]{2,1,0:T(8,128)(2,1)S(1)} %copy-done.4), channel_id=1, source_target_pairs={{0,1},{1,0},{2,3},{3,2},{4,5},{5,4},{6,7},{7,6},{8,9},{9,8},{10,11... | collective-permute-start | bytes 2457608 | tf_op jit(solution)/shard_map/ppermute | solution.py:753
  218.8 31.0 %collective-permute-start.19 = (bf16[4,400,256]{2,1,0:T(8,128)(2,1)S(1)}, bf16[4,400,256]{2,1,0:T(8,128)(2,1)}, u32[]{:S(2)}, u32[]{:S(2)}) collective-permute-start(bf16[4,400,256]{2,1,0:T(8,128)(2,1)S(1)} %copy-done.4), channel_id=1, source_target_pairs={{0,4},{4,0},{1,5},{5,1},{2,6},{6,2},{3,7},{7,3},{8,12},{12,8},{9,1... | collective-permute-start | bytes 2457608 | tf_op jit(solution)/shard_map/ppermute | solution.py:749
  284.4 24.4 %collective-permute-start.25 = (bf16[512,1024]{1,0:T(8,128)(2,1)}, bf16[512,1024]{1,0:T(8,128)(2,1)S(1)}, u32[]{:S(2)}, u32[]{:S(2)}) collective-permute-start(bf16[512,1024]{1,0:T(8,128)(2,1)} %get-tuple-element.174), channel_id=1, source_target_pairs={{0,2},{2,0},{1,3},{3,1},{4,6},{6,4},{5,7},{7,5},{8,10},{10,8},{9,1... | collective-permute-start | bytes 3145736 | tf_op jit(solution)/shard_map/ppermute | solution.py:745
  285.7 23.1 %collective-permute-start.23 = (bf16[256,1024]{1,0:T(8,128)(2,1)}, bf16[256,1024]{1,0:T(8,128)(2,1)S(1)}, u32[]{:S(2)}, u32[]{:S(2)}) collective-permute-start(bf16[256,1024]{1,0:T(8,128)(2,1)} %get-tuple-element.170), channel_id=1, source_target_pairs={{0,1},{1,0},{2,3},{3,2},{4,5},{5,4},{6,7},{7,6},{8,9},{9,8},{10,11... | collective-permute-start | bytes 1572872 | tf_op jit(solution)/shard_map/ppermute | solution.py:753
  358.7 104.7 %collective-permute-start.31 = (bf16[4,368,512]{2,1,0:T(8,128)(2,1)}, bf16[4,368,512]{2,1,0:T(8,128)(2,1)S(1)}, u32[]{:S(2)}, u32[]{:S(2)}) collective-permute-start(bf16[4,368,512]{2,1,0:T(8,128)(2,1)} %get-tuple-element.202), channel_id=1, source_target_pairs={{0,1},{1,0},{2,3},{3,2},{4,5},{5,4},{6,7},{7,6},{8,9},{9,8},{10,11... | collective-permute-start | bytes 4521992 | tf_op jit(solution)/shard_map/ppermute | solution.py:753
  360.6 103.6 %collective-permute-start.32 = (bf16[4,368,512]{2,1,0:T(8,128)(2,1)}, bf16[4,368,512]{2,1,0:T(8,128)(2,1)}, u32[]{:S(2)}, u32[]{:S(2)}) collective-permute-start(bf16[4,368,512]{2,1,0:T(8,128)(2,1)} %get-tuple-element.203), channel_id=1, source_target_pairs={{0,4},{4,0},{1,5},{5,1},{2,6},{6,2},{3,7},{7,3},{8,12},{12,8},{9,1... | collective-permute-start | bytes 4521992 | tf_op jit(solution)/shard_map/ppermute | solution.py:749
  362.1 102.2 %collective-permute-start.33 = (bf16[4,368,512]{2,1,0:T(8,128)(2,1)}, bf16[4,368,512]{2,1,0:T(8,128)(2,1)}, u32[]{:S(2)}, u32[]{:S(2)}) collective-permute-start(bf16[4,368,512]{2,1,0:T(8,128)(2,1)} %get-tuple-element.204), channel_id=1, source_target_pairs={{0,5},{1,4},{2,7},{3,6},{4,1},{5,0},{6,3},{7,2},{8,13},{9,12},{10,... | collective-permute-start | bytes 4521992 | tf_op jit(solution)/shard_map/ppermute | solution.py:741
  362.2 102.1 %all-to-all-start.4 = ((bf16[4,4,128,1024]{3,2,1,0:T(8,128)(2,1)}), bf16[4,4,128,1024]{3,2,1,0:T(8,128)(2,1)}, u32[]{:S(2)}, u32[]{:S(2)}) async-start(bf16[4,4,128,1024]{3,2,1,0:T(8,128)(2,1)} %get-tuple-element.205), calls=%async_computation.4 | async-start | bytes 8388608 | tf_op jit(solution)/shard_map/all_to_all | solution.py:761
  367.5 95.9 %collective-permute-start.34 = (bf16[256,1024]{1,0:T(8,128)(2,1)}, bf16[256,1024]{1,0:T(8,128)(2,1)S(1)}, u32[]{:S(2)}, u32[]{:S(2)}) collective-permute-start(bf16[256,1024]{1,0:T(8,128)(2,1)} %get-tuple-element.207), channel_id=1, source_target_pairs={{0,1},{1,0},{2,3},{3,2},{4,5},{5,4},{6,7},{7,6},{8,9},{9,8},{10,11... | collective-permute-start | bytes 1572872 | tf_op jit(solution)/shard_map/ppermute | solution.py:753
  369.5 93.9 %collective-permute-start.35 = (bf16[512,288]{1,0:T(8,128)(2,1)}, bf16[512,288]{1,0:T(8,128)(2,1)S(1)}, u32[]{:S(2)}, u32[]{:S(2)}) collective-permute-start(bf16[512,288]{1,0:T(8,128)(2,1)} %get-tuple-element.209), channel_id=1, source_target_pairs={{0,1},{1,0},{2,3},{3,2},{4,5},{5,4},{6,7},{7,6},{8,9},{9,8},{10,11... | collective-permute-start | bytes 884744 | tf_op jit(solution)/shard_map/ppermute | solution.py:753
  468.2 92.6 %all-to-all-start.5 = ((bf16[8,384,512]{2,1,0:T(8,128)(2,1)}), bf16[8,384,512]{2,1,0:T(8,128)(2,1)S(1)}, u32[]{:S(2)}, u32[]{:S(2)}) async-start(bf16[8,384,512]{2,1,0:T(8,128)(2,1)} %get-tuple-element.214.d_ref), calls=%async_computation.5 | async-start | bytes 6291456 | tf_op jit(solution)/shard_map/all_to_all | solution.py:761
  508.3 33.0 %collective-permute-start.44 = (bf16[368,512]{1,0:T(8,128)(2,1)}, bf16[368,512]{1,0:T(8,128)(2,1)S(1)}, u32[]{:S(2)}, u32[]{:S(2)}) collective-permute-start(bf16[368,512]{1,0:T(8,128)(2,1)} %get-tuple-element.340), channel_id=1, source_target_pairs={{0,16},{8,24},{16,0},{24,8},{1,17},{9,25},{17,1},{25,9},{2,18},{10... | collective-permute-start | bytes 1130504 | tf_op jit(solution)/shard_map/ppermute | solution.py:780
  516.5 24.8 %collective-permute-start.43 = (bf16[368,512]{1,0:T(8,128)(2,1)}, bf16[368,512]{1,0:T(8,128)(2,1)S(1)}, u32[]{:S(2)}, u32[]{:S(2)}) collective-permute-start(bf16[368,512]{1,0:T(8,128)(2,1)} %get-tuple-element.338), channel_id=1, source_target_pairs={{0,8},{8,16},{16,24},{24,0},{1,9},{9,17},{17,25},{25,1},{2,10},{10... | collective-permute-start | bytes 1130504 | tf_op jit(solution)/shard_map/ppermute | solution.py:780
  520.7 27.8 %collective-permute-start.41 = (bf16[400,256]{1,0:T(8,128)(2,1)}, bf16[400,256]{1,0:T(8,128)(2,1)}, u32[]{:S(2)}, u32[]{:S(2)}) collective-permute-start(bf16[400,256]{1,0:T(8,128)(2,1)} %fusion.6), channel_id=1, source_target_pairs={{0,4},{4,0},{1,5},{5,1},{2,6},{6,2},{3,7},{7,3},{8,12},{12,8},{9,1... | collective-permute-start | bytes 614408 | tf_op jit(solution)/shard_map/ppermute | solution.py:749
  521.1 34.5 %collective-permute-start.40 = (bf16[400,256]{1,0:T(8,128)(2,1)}, bf16[400,256]{1,0:T(8,128)(2,1)}, u32[]{:S(2)}, u32[]{:S(2)}) collective-permute-start(bf16[400,256]{1,0:T(8,128)(2,1)} %fusion.6), channel_id=1, source_target_pairs={{0,2},{2,0},{1,3},{3,1},{4,6},{6,4},{5,7},{7,5},{8,10},{10,8},{9,1... | collective-permute-start | bytes 614408 | tf_op jit(solution)/shard_map/ppermute | solution.py:745
  554.0 29.7 %collective-permute-start.49 = (bf16[128,384]{1,0:T(8,128)(2,1)}, bf16[128,384]{1,0:T(8,128)(2,1)}, u32[]{:S(2)}, u32[]{:S(2)}) collective-permute-start(bf16[128,384]{1,0:T(8,128)(2,1)} %bitcast.96), channel_id=1, source_target_pairs={{0,1},{1,0},{2,3},{3,2},{4,5},{5,4},{6,7},{7,6},{8,9},{9,8},{10,11... | collective-permute-start | bytes 294920 | tf_op jit(solution)/shard_map/ppermute | solution.py:753
  562.5 31.4 %all-to-all-start.6 = ((bf16[4,528,512]{2,1,0:T(8,128)(2,1)}), bf16[4,528,512]{2,1,0:T(8,128)(2,1)}, u32[]{:S(2)}, u32[]{:S(2)}) async-start(bf16[4,528,512]{2,1,0:T(8,128)(2,1)} %pad_maximum_fusion), calls=%async_computation.6 | async-start | bytes 4325376 | tf_op jit(solution)/shard_map/all_to_all | solution.py:761
  578.5 37.1 %collective-permute-start.36 = (bf16[512,1024]{1,0:T(8,128)(2,1)}, bf16[512,1024]{1,0:T(8,128)(2,1)}, u32[]{:S(2)}, u32[]{:S(2)}) collective-permute-start(bf16[512,1024]{1,0:T(8,128)(2,1)} %input_grad.1), channel_id=1, source_target_pairs={{0,1},{1,0},{2,3},{3,2},{4,5},{5,4},{6,7},{7,6},{8,9},{9,8},{10,11... | collective-permute-start | bytes 3145736 | tf_op jit(solution)/shard_map/ppermute | solution.py:753
  (81 other events, 941.1 us)
Sparse Core Ops, SparseCore 0:
  92.3 58.6 all-gather.2

commit v3 on v2

--- a/solution.py
+++ b/solution.py
@@ -11,6 +11,8 @@
 HEAD_DIM = 64
 VMEM_CAP = 56 * 1024 * 1024
 MASKED = -1e30
+SMALL_GRANT = ("mlp", "mlp_weights", "out_proj", "sums", "out_weight", "dense_natural")
+SPARE = 14
 TS = 256
 FQ, FK = 1024, 512
 BQ, BK = 512, 512
@@ -24,17 +26,19 @@
     return lax.dot_general(a, b, (((1,), (0,)), ((), ())), preferred_element_type=f32)
 
 
-def run(kernel, out_shape, name, scalars=0, scratch=(), flops=2_000_000_000):
+def run(kernel, out_shape, name, scalars=0, scratch=(), flops=1_000_000):
     def call(*args):
         vm = pl.BlockSpec(memory_space=pltpu.VMEM)
         sm = pl.BlockSpec(memory_space=pltpu.SMEM)
         outs = jax.tree.map(lambda _: vm, out_shape)
+        need = sum(x.size * x.dtype.itemsize for x in list(args) + jax.tree.leaves(out_shape))
+        limit = min(VMEM_CAP, need + (SPARE << 20)) if name in SMALL_GRANT else VMEM_CAP
         return pl.pallas_call(
             kernel, out_shape=out_shape,
             in_specs=[sm] * scalars + [vm] * (len(args) - scalars), out_specs=outs,
             scratch_shapes=list(scratch),
-            compiler_params=pltpu.CompilerParams(vmem_limit_bytes=VMEM_CAP),
-            cost_estimate=pl.CostEstimate(flops=flops, transcendentals=0, bytes_accessed=8_000_000),
+            compiler_params=pltpu.CompilerParams(vmem_limit_bytes=limit),
+            cost_estimate=pl.CostEstimate(flops=flops, transcendentals=0, bytes_accessed=10_000 if flops < 2_000_000 else 8_000_000),
             name=name)(*args)
     return call
 
@@ -176,7 +180,7 @@
             pltpu.VMEM((384, rows // 4), f32),
         ],
         compiler_params=pltpu.CompilerParams(vmem_limit_bytes=VMEM_CAP),
-        cost_estimate=pl.CostEstimate(flops=60_000_000_000, transcendentals=16_000_000, bytes_accessed=16_000_000),
+        cost_estimate=pl.CostEstimate(flops=60_000_000_000, transcendentals=0, bytes_accessed=10_000),
         name="attention_forward",
     )(first_len, meet, dest, rank, near, far)
 
@@ -308,12 +312,12 @@
             pltpu.VMEM((384, rows), bf16),
         ],
         compiler_params=pltpu.CompilerParams(vmem_limit_bytes=VMEM_CAP),
-        cost_estimate=pl.CostEstimate(flops=90_000_000_000, transcendentals=16_000_000, bytes_accessed=16_000_000),
+        cost_estimate=pl.CostEstimate(flops=90_000_000_000, transcendentals=0, bytes_accessed=10_000),
         name="attention_backward",
     )(first_len, meet, dest, rank, sorted_t, att_t, lse, cos_t, sin_t, grad)
 
 
-def qkv_kernel(ctx_ref, cos_ref, sin_ref, w_ref, *refs):
+def qkv_kernel(ctx_ref, cos_ref, sin_ref, w_ref, *refs, first):
     out_ref = refs[-1]
     size, _, lanes = w_ref.shape
     bias = jnp.zeros((1, 384), f32)
@@ -329,7 +333,8 @@
         mixed = jnp.broadcast_to(bias, (384, count))
         for f in range(size):
             mixed = mixed + nt(w_ref[f, 0:384], x_ref[:, f * lanes:(f + 1) * lanes])
-        cos, sin = cos_ref[:, span], sin_ref[:, span]
+        table = slice(first + start, first + start + count)
+        cos, sin = cos_ref[:, table], sin_ref[:, table]
         for base in (0, 64, 128, 192):
             front, back = mixed[base:base + 32], mixed[base + 32:base + 64]
             out_ref[base:base + 32, span] = (front * cos - back * sin).astype(bf16)
@@ -338,17 +343,24 @@
         start += count
 
 
-def qkv_rope(ctx, pieces, weights, cos_t, sin_t):
+def qkv_rope(ctx, pieces, weights, cos_t, sin_t, first):
     rows = sum(p.shape[0] for p in pieces)
-    return run(qkv_kernel, jax.ShapeDtypeStruct((384, rows), bf16), "qkv_rope", 1)(
+    return run(partial(qkv_kernel, first=first), jax.ShapeDtypeStruct((384, rows), bf16), "qkv_rope", 1)(
         ctx, cos_t, sin_t, weights, *pieces)
 
 
-def row_places(order, packed, lengths, arrival):
+def row_places(order, packed, lengths, dest):
     rows = order.shape[0]
     first_len = lengths[0]
-    place = jnp.sum(
-        jnp.where(order[:, None] == arrival[None, :], packed[:, None], 0), axis=0)
+    digit = jnp.arange(64, dtype=jnp.int32)
+    high = (order // 64)[None, :] == digit[:, None]
+    low = ((order % 64)[None, :] == digit[:, None]).astype(bf16)
+    parts = jnp.stack([packed // 64, packed % 64]).astype(f32)
+    left = jnp.where(high[None], parts[:, None, :], 0.0).astype(bf16).reshape(128, rows)
+    table = nt(left, low)
+    table = (table[:64] * 64.0 + table[64:]).reshape(8, rows // 8)
+    picked = dest[:, None, None] == jnp.arange(8, dtype=jnp.int32)[None, :, None]
+    place = jnp.sum(jnp.where(picked, table[None], 0.0), axis=1).reshape(rows).astype(jnp.int32)
     in_first = place < first_len
     position = jnp.where(in_first, place, place - first_len)
     flags = in_first.astype(f32).reshape(rows // 128, 128)
@@ -414,14 +426,15 @@
     return jnp.sum(v, axis=0, keepdims=True)
 
 
-def out_proj_kernel(w_ref, x_ref, att_ref, bias_ref, gain_ref, shift_ref,
-                    normed_ref, hat_ref, rstd_ref, low_ref):
-    acc = x_ref[...].astype(f32) + bias_ref[...]
+def out_proj_kernel(tp_ref, w_ref, x_ref, att_ref, vec_ref, normed_ref, hat_ref, rstd_ref, low_ref):
+    half = normed_ref.shape[0]
+    own = pl.ds(pl.multiple_of(tp_ref[0] * half, half), half)
+    acc = x_ref[own, :].astype(f32) + vec_ref[0:1]
     for j in range(8):
         at = head_rows_of(j)
         acc = acc + nn(att_ref[j], w_ref[at:at + 128, 0:acc.shape[1]])
     x_hat, rstd = norm_parts(acc)
-    normed = x_hat * gain_ref[...] + shift_ref[...]
+    normed = x_hat * vec_ref[1:2] + vec_ref[2:3]
     normed_ref[...] = normed
     hat_ref[...] = x_hat
     rstd_ref[...] = rstd
@@ -429,9 +442,7 @@
 
 
 def hidden_refs(refs):
-    first = refs[3].shape[0]
-    return [(lambda f, r=r: (r, f)) for r in refs[0:3]] + [
-        lambda f: (refs[3], f) if f < first else (refs[4], f - first)]
+    return [(lambda f, r=r: (r, f)) for r in refs[0:4]]
 
 
 def up_rows(block, f, shard):
@@ -457,7 +468,7 @@
 
 
 def mlp_kernel(own_ref, peer_ref, bias_ref, *refs):
-    act_ref, slope_ref, own_out, peer_out = refs[5:]
+    act_ref, slope_ref, own_out, peer_out = refs[4:]
     half, width = own_ref.shape
     size, units, strip, shard, sides, groups = hidden_sizes(refs, width)
     blocks = hidden_refs(refs)
@@ -486,7 +497,7 @@
                 peer_out[:, s * units:(s + 1) * units] = out[s].astype(bf16)
 
 
-def head_kernel(strip_rows, normed_ref, own_ref, recv_ref, bias_ref, gain_ref, shift_ref, dense_ref, cot_ref, cot_embed_ref,
+def head_kernel(strip_rows, tp_ref, normed_ref, own_ref, recv_ref, all_vec_ref, dense_ref, cot_ref, cot_embed_ref,
                 final_ref, embed_ref, grad_ref, low_ref, proj_grad_ref, vec_ref, proj_ref):
     width, emb = proj_ref.shape
     strip = strip_rows
@@ -495,12 +506,15 @@
             at = (f * 2 + t) * strip
             src = (t * (width // (2 * strip)) + f) * strip
             proj_ref[at:at + strip, :] = dense_ref[src:src + strip, width:width + emb]
-    second = normed_ref[...] + own_ref[...] + recv_ref[...].astype(f32) + bias_ref[...]
+    half = normed_ref.shape[0]
+    mine = pl.ds(pl.multiple_of(tp_ref[0] * half, half), half)
+    gain = all_vec_ref[4:5]
+    second = normed_ref[...] + own_ref[...] + recv_ref[...].astype(f32) + all_vec_ref[3:4]
     x_hat, rstd = norm_parts(second)
-    final = (x_hat * gain_ref[...] + shift_ref[...]).astype(bf16)
+    final = (x_hat * gain + all_vec_ref[5:6]).astype(bf16)
     final_ref[...] = final
     projected = nn(final, proj_ref[...])
-    cot = cot_embed_ref[...].astype(f32)
+    cot = cot_embed_ref[mine, :].astype(f32)
     col = lax.broadcasted_iota(jnp.int32, projected.shape, 1)
     embedded = jnp.zeros(projected.shape, f32)
     grad_proj = jnp.zeros(projected.shape, f32)
@@ -517,8 +531,8 @@
     embed_ref[...] = embedded.astype(bf16)
     proj_low = grad_proj.astype(bf16)
     proj_grad_ref[...] = tn(final, proj_low).astype(bf16)
-    grad_final = cot_ref[...].astype(f32) + nt(proj_low, proj_ref[...])
-    grad_second = norm_back(grad_final, x_hat, rstd, gain_ref[...])
+    grad_final = cot_ref[mine, :].astype(f32) + nt(proj_low, proj_ref[...])
+    grad_second = norm_back(grad_final, x_hat, rstd, gain)
     grad_ref[...] = grad_second
     low_ref[...] = grad_second.astype(bf16)
     vec_ref[...] = jnp.zeros(vec_ref.shape, f32)
@@ -528,7 +542,7 @@
 
 
 def mlp_back_kernel(own_ref, peer_ref, slope_ref, *refs):
-    g1_ref, bias_ref, own_out, peer_out = refs[5:]
+    g1_ref, bias_ref, own_out, peer_out = refs[4:]
     half, width = own_ref.shape
     size, units, strip, shard, sides, groups = hidden_sizes(refs, width)
     blocks = hidden_refs(refs)
@@ -588,13 +602,11 @@
         out[...] = total.astype(bf16)
 
 
-def pick_kernel(index_ref, up_ref, down_ref, dense_ref, proj_ref, *refs):
-    vecs, outs = refs[:7], refs[7:]
-    place, core, tp = (index_ref[i] for i in range(3))
+def pick_kernel(place_ref, up_ref, down_ref, *outs):
     strip = down_ref.shape[0] // 4
     shard, units = up_ref.shape[0], up_ref.shape[1] // 4
     for n in range(2):
-        q = place ^ n
+        q = place_ref[0] ^ n
         for f in range(units // strip):
             at = pl.multiple_of((f * 4 + q) * strip, strip)
             outs[n][0:shard, f * strip:(f + 1) * strip] = up_ref[:, pl.ds(at, strip)]
@@ -602,8 +614,12 @@
         for s in range(down_ref.shape[1] // units):
             at = shard + s * strip
             outs[n][at:at + strip] = down_ref[pl.ds(rows, strip), s * units:(s + 1) * units]
+
+
+def dense_half_kernel(index_ref, dense_ref, proj_ref, *refs):
+    vecs, half = refs[:7], refs[7]
+    core, tp = (index_ref[i] for i in range(2))
     count, width = dense_ref.shape[0] // 2, dense_ref.shape[1]
-    half = outs[2]
     half[0:count, 0:width] = dense_ref[pl.ds(pl.multiple_of(core * count, count), count), :]
     half[0:count, width:] = proj_ref[pl.ds(pl.multiple_of((tp * 2 + core) * count, count), count), :]
     lines, line = [], []
@@ -618,20 +634,20 @@
 
 
 def dense_natural_kernel(index_ref, own_ref, core_ref, out_ref, vec_ref, up_ref):
-    core, place = (index_ref[i] for i in range(2))
-    size, rows = own_ref.shape[0] // 2, own_ref.shape[1] - 16
+    core, place, tp = (index_ref[i] for i in range(3))
+    size, rows = own_ref.shape[0], own_ref.shape[2] - 16
     units = up_ref.shape[1] // 4
     strip, quarter = units // size, vec_ref.shape[1] // size
     for f in range(size):
         for t in range(2):
-            own, other = own_ref[t * size + f, 0:rows], core_ref[t * size + f, 0:rows]
+            own, other = own_ref[f, tp ^ t, 0:rows], core_ref[f, tp ^ t, 0:rows]
             for k in range(2):
                 at = ((t * size + f) * 2 + k) * rows
                 out_ref[at:at + rows, :] = jnp.where(core == k, own, other)
-        vecs = own_ref[f, rows:rows + 16].astype(f32)
-        far = own_ref[size + f, rows:rows + 16].astype(f32)
+        vecs = own_ref[f, 0, rows:rows + 16].astype(f32)
+        wanted = own_ref[f, tp ^ core, rows:rows + 16].astype(f32)
         cut = 4 * strip
-        ups = jnp.where(core == 0, vecs[0:1, 0:cut], far[0:1, 0:cut])
+        ups = wanted[0:1, 0:cut]
         for i in range(6):
             r, c = divmod(cut + i * quarter, 4 * quarter)
             vec_ref[i:i + 1, f * quarter:(f + 1) * quarter] = vecs[r:r + 1, c:c + quarter]
@@ -642,23 +658,63 @@
             up_ref[:, v * units + f * strip:v * units + (f + 1) * strip] = picked
 
 
-def hidden_join_kernel(part_ref, up_ref, down_ref):
+def hidden_split_kernel(core_ref, *refs):
+    keep_ref, away_ref, dense_ref = refs[-3:]
+    ups, downs = refs[:-7], refs[-7:-3]
+    rows, units = keep_ref.shape
+    strip, width = downs[0].shape
+
+    def total(parts, where):
+        out = parts[0][where].astype(f32)
+        for p in parts[1:]:
+            out = out + p[where].astype(f32)
+        return out.astype(bf16)
+
+    def store(up_ref, down_ref):
+        up_ref[...] = total(ups, (slice(0, rows), slice(None)))
+        down_ref[...] = jnp.zeros(down_ref.shape, bf16)
+        for s in range(width // units):
+            down_ref[s * strip:(s + 1) * strip] = total(downs, (slice(None), slice(s * units, (s + 1) * units)))
+
+    dense_ref[...] = total(ups, (slice(rows, None), slice(None)))
+
+    @pl.when(core_ref[0] == 0)
+    def _():
+        store(keep_ref, away_ref)
+
+    @pl.when(core_ref[0] == 1)
+    def _():
+        store(away_ref, keep_ref)
+
+
+def hidden_join_kernel(core_ref, own_ref, core_peer_ref, up_ref, down_ref, bias_ref):
     strip = down_ref.shape[0] // 4
-    shard, units = up_ref.shape[0], part_ref.shape[2]
-    for q in range(4):
-        for f in range(units // strip):
-            at = (f * 4 + q) * strip
-            up_ref[:, at:at + strip] = part_ref[q, 0:shard, f * strip:(f + 1) * strip].astype(f32)
-        for s in range(down_ref.shape[1] // units):
-            at = shard + 16 + s * strip
-            down_ref[q * strip:(q + 1) * strip, s * units:(s + 1) * units] = part_ref[q, at:at + strip].astype(f32)
-
-
-def first_back_kernel(second_ref, own_ref, recv_ref, hat_ref, rstd_ref, gain_ref, w_ref,
+    shard, units = up_ref.shape[0], own_ref.shape[2]
+
+    def store(ups, downs):
+        for q in range(4):
+            for f in range(units // strip):
+                at = (f * 4 + q) * strip
+                up_ref[:, at:at + strip] = ups[q, 0:shard, f * strip:(f + 1) * strip].astype(f32)
+            bias_ref[q] = ups[q, shard:shard + 16].astype(f32)
+            for s in range(down_ref.shape[1] // units):
+                down_ref[q * strip:(q + 1) * strip, s * units:(s + 1) * units] = (
+                    downs[q, s * strip:(s + 1) * strip].astype(f32))
+
+    @pl.when(core_ref[0] == 0)
+    def _():
+        store(own_ref, core_peer_ref)
+
+    @pl.when(core_ref[0] == 1)
+    def _():
+        store(core_peer_ref, own_ref)
+
+
+def first_back_kernel(second_ref, own_ref, recv_ref, hat_ref, rstd_ref, all_vec_ref, w_ref,
                       grad_ref, low_ref, att_grad_ref, vec_ref):
     grad_normed = second_ref[...] + own_ref[...] + recv_ref[...].astype(f32)
     x_hat = hat_ref[...]
-    grad_first = norm_back(grad_normed, x_hat, rstd_ref[...], gain_ref[...])
+    grad_first = norm_back(grad_normed, x_hat, rstd_ref[...], all_vec_ref[1:2])
     grad_ref[...] = grad_first
     low = grad_first.astype(bf16)
     low_ref[...] = low
@@ -772,12 +828,12 @@
     return total.astype(bf16)
 
 
-def collect_z(value):
+def send_z(value):
     size = lax.axis_size("fsdp")
     if size > 4:
-        return add_all(trade(value, "fsdp"))
-    return add_all([value[0]] + [
-        lax.ppermute(value[s], "fsdp", [(i, (i + s) % size) for i in range(size)]) for s in range(1, size)])
+        return list(trade(value, "fsdp"))
+    return [value[0]] + [
+        lax.ppermute(value[s], "fsdp", [(i, (i + s) % size) for i in range(size)]) for s in range(1, size)]
 
 
 def around_ctx(value, ctx):
@@ -790,8 +846,14 @@
     return jnp.stack([lax.dynamic_index_in_dim(stacked, own ^ i, 0, keepdims=False) for i in range(len(parts))])
 
 
-def pair_rows(own, peer, tp):
-    return jnp.concatenate([jnp.where(tp == 0, own, peer), jnp.where(tp == 0, peer, own)], axis=0)
+def pair_rows(own, peers, tp):
+    half = own.shape[0]
+    out = jnp.concatenate([own, own], axis=0)
+    at = (1 - tp) * half
+    for p in peers:
+        out = lax.dynamic_update_slice_in_dim(out, p, at, axis=0)
+        at = at + p.shape[0]
+    return out
 
 
 def shards(
@@ -835,6 +897,7 @@
     units = size * strip
     shard = up_weight.shape[0]
     place_ref = place.astype(jnp.int32).reshape(1)
+    tp_ref = tp.astype(jnp.int32).reshape(1)
     ctx_ref = ctx.astype(jnp.int32).reshape(1)
     sides = width // units
     hidden_rows = shard + sides * strip
@@ -857,11 +920,7 @@
         dense_half = jnp.concatenate(
             [lax.dynamic_slice_in_dim(beside, core * half_rows, half_rows, axis=0), vec_block], axis=0)
     else:
-        *blocks, dense_half = run(
-            pick_kernel, (shape((hidden_rows, units), bf16),) * 2 + (shape((shard_rows // 2 + 16, width + emb), bf16),),
-            "pick", 1)(jnp.stack([place, core, tp]).astype(jnp.int32), up_weight, down_weight, out_weight, proj_weight,
-                       *[v.reshape(1, -1) for v in vectors])
-
+        blocks = run(pick_kernel, (shape((hidden_rows, units), bf16),) * 2, "pick", 1)(place_ref, up_weight, down_weight)
     lanes = shard
     own_qkv = lax.dynamic_slice_in_dim(qkv_weight, ctx * 128, 128, axis=2)
     own_qkv = jnp.transpose(own_qkv, (1, 2, 0)).reshape(384, lanes)
@@ -882,78 +941,79 @@
     quarter = half // 2
     x4 = [hop_x(x0[:quarter]), hop_x(x0[quarter:])]
     other = hop_y(blocks[1])
-    near = [layer_input, hop_core(layer_input)]
+    hidden_own = jnp.where(tp == core, blocks[0], other)
     pair = jnp.stack([deal_order, hop_core(deal_order)])
     order = jnp.concatenate([pair, hop_x(pair)]).reshape(-1) % rows
+    near = [layer_input, hop_core(layer_input)]
+    hidden_own, weights = lax.optimization_barrier((hidden_own, weights))
+    hidden0 = gather(hidden_own, "fsdp", size)
     x5 = [hop_y(p) for p in x4]
     far = x4 + x5 + [hop_core(p) for p in x4 + x5]
     u = jnp.arange(8, dtype=jnp.int32)
     dest = dev ^ jnp.where(u < 4, (u & 6) | ((u & 1) ^ tp), u)
     slot = jnp.arange(rows, dtype=jnp.int32)
-    dest_of = dev ^ jnp.where(slot < 4 * half, ((slot // half) & 6) | (((slot // half) & 1) ^ tp), slot // half)
-    arrival = dest_of * half + slot % half
     first_len = seq_lengths[0, :1]
     packed_index = (ctx ^ (slot // own_rows)) * own_rows + slot % own_rows
-    position, rank, meet = row_places(order, packed_index, seq_lengths[0], arrival)
+    position, rank, meet = row_places(order, packed_index, seq_lengths[0], dest)
     rank = rank[None]
     cos_t, sin_t = rope_tables_t(position)
 
-    hidden_own = jnp.where(tp == core, blocks[0], other)
-    hidden_own, weights = lax.optimization_barrier((hidden_own, weights))
-    hidden0 = gather(hidden_own, "fsdp", size)
-
-    near_mixed = qkv_rope(ctx_ref, near, weights, cos_t[:, :rows // 2], sin_t[:, :rows // 2])
-    far, near_mixed, dense_half = lax.optimization_barrier((far, near_mixed, dense_half))
-    dense_parts = lax.all_gather(dense_half, ("tp", "fsdp"), axis=0)
-    far_mixed = qkv_rope(ctx_ref, far, weights, cos_t[:, rows // 2:], sin_t[:, rows // 2:])
-    hidden0, far_mixed = lax.optimization_barrier((hidden0, far_mixed))
-    cut = size // 2
-    hiddens = [hidden0, hop_y(hidden0), hop_x(hidden0), hop(hidden0[:cut], 5), None]
+    near_mixed = qkv_rope(ctx_ref, near, weights, cos_t, sin_t, 0)
+    far, near_mixed = lax.optimization_barrier((far, near_mixed))
+    if size <= 4:
+        dense_half = run(dense_half_kernel, shape((shard_rows // 2 + 16, width + emb), bf16), "dense_half", 1)(
+            jnp.stack([core, tp]).astype(jnp.int32), after(out_weight, near_mixed), proj_weight,
+            *[v.reshape(1, -1) for v in vectors])
+    dense_pair = jnp.stack([dense_half, hop_y(dense_half)])
+    far_mixed = qkv_rope(ctx_ref, far, weights, cos_t, sin_t, rows // 2)
+    hidden0, far_mixed, dense_pair = lax.optimization_barrier((hidden0, far_mixed, dense_pair))
+    dense_parts = gather(dense_pair, "fsdp", size)
+    hiddens = [hidden0, hop_y(hidden0), hop_x(hidden0), hop(hidden0, 5)]
     att, sorted_t, att_t, lse = attention_forward(first_len, meet, dest, rank, near_mixed, far_mixed)
-    att, dense_parts, hiddens[1:4] = lax.optimization_barrier((att, dense_parts, hiddens[1:4]))
+    att, dense_parts, hiddens[1:3] = lax.optimization_barrier((att, dense_parts, hiddens[1:3]))
     att = trade(att, CT)
     dense, vec, up_b = run(
         dense_natural_kernel,
         (shape((width, width + emb), bf16), shape((8, width), f32), shape((1, 4 * units), f32)), "dense_natural", 1)(
-        jnp.stack([core, place]).astype(jnp.int32), dense_parts, hop_core(dense_parts))
-    out_b, gain1, shift1, down_b, gain2, shift2 = (vec[i:i + 1] for i in range(6))
-    hiddens[4] = hop(after(hidden0[cut:], att), 5)
+        jnp.stack([core, place, tp]).astype(jnp.int32), dense_parts, hop_core(dense_parts))
+    att, dense, vec, up_b = lax.optimization_barrier((att, dense, vec, up_b))
 
     f_rows, b_rows = shape((half, width), f32), shape((half, width), bf16)
     normed, hat1, rstd1, normed_low = run(
-        out_proj_kernel, (f_rows, f_rows, shape((half, 1), f32), b_rows), "out_proj")(
-        dense, x0, att, out_b, gain1, shift1)
+        out_proj_kernel, (f_rows, f_rows, shape((half, 1), f32), b_rows), "out_proj", 1)(
+        tp_ref, dense, layer_input, att, vec)
     normed_peer = hop_core(normed_low)
     hidden = shape((own_rows, 4 * units), bf16)
-    act, slope, own_down, peer_down = run(mlp_kernel, (hidden, hidden, f_rows, b_rows), "mlp", flops=8_000_000_000)(
+    act, slope, own_down, peer_down = run(mlp_kernel, (hidden, hidden, f_rows, b_rows), "mlp")(
         normed_low, normed_peer, up_b, *hiddens)
-    w_own = after(weights, normed_low)
+    w_own = after(weights, hiddens[3])
     w_y, w_x = hop_y(w_own), hop_x(w_own)
-    own_down, peer_down, w_y, w_x = lax.optimization_barrier((own_down, peer_down, w_y, w_x))
+    act, slope, own_down, peer_down, w_y, w_x = lax.optimization_barrier((act, slope, own_down, peer_down, w_y, w_x))
     w_cut = max(1, w_own.shape[0] // 2)
     w_xy = [hop(after(w_own[:w_cut], own_down), 5)]
     vec_shape = shape((8, width), f32)
     final_low, embed_low, grad_second, g2, proj_grad, vec2 = run(
         partial(head_kernel, shard_rows),
-        (b_rows, shape((half, emb), bf16), f_rows, b_rows, shape((width, emb), bf16), vec_shape), "heads",
-        scratch=[pltpu.VMEM((width, emb), bf16)])(
-        normed, own_down, hop_core(peer_down), down_b, gain2, shift2, dense,
-        own_half(cot_output, tp), own_half(cot_embed, tp))
-    g2, w_xy[0] = lax.optimization_barrier((g2, w_xy[0]))
+        (b_rows, shape((half, emb), bf16), f_rows, b_rows, shape((width, emb), bf16), vec_shape), "heads", 1,
+        scratch=[pltpu.VMEM((width, emb), bf16)], flops=2_000_000_000)(
+        tp_ref, normed, own_down, hop_core(peer_down), vec, dense, cot_output, cot_embed)
+    final_low, embed_low, grad_second, g2, proj_grad, vec2, w_xy[0] = lax.optimization_barrier(
+        (final_low, embed_low, grad_second, g2, proj_grad, vec2, w_xy[0]))
     g2_peer = hop_core(g2)
     if w_cut < w_own.shape[0]:
         w_xy.append(hop(after(w_own[w_cut:], w_xy[0]), 5))
     final_halves = [hop_y(after(final_low[:half // 2], g2))]
     g1, up_bias_part, own_normed, peer_normed = run(
-        mlp_back_kernel, (hidden, shape((1, 4 * units), f32), f_rows, b_rows), "mlp_back", flops=16_000_000_000)(
+        mlp_back_kernel, (hidden, shape((1, 4 * units), f32), f_rows, b_rows), "mlp_back")(
         g2, g2_peer, slope, *hiddens)
-    own_normed, final_halves[0], w_xy = lax.optimization_barrier((own_normed, final_halves[0], w_xy))
+    g1, up_bias_part, own_normed, peer_normed, final_halves[0], w_xy = lax.optimization_barrier(
+        (g1, up_bias_part, own_normed, peer_normed, final_halves[0], w_xy))
     w_near = [w_own, w_y, w_x, jnp.concatenate(w_xy, axis=0)]
     w_all = w_near + [hop_core(after(w, own_normed)) for w in w_near]
     grad_first, g0, att_grad, vec1 = run(
         first_back_kernel, (f_rows, b_rows, shape((8, half, 128), bf16), vec_shape), "first_back")(
-        grad_second, own_normed, hop_core(peer_normed), hat1, rstd1, gain1, dense)
-    att_grad, w_all = lax.optimization_barrier((att_grad, w_all))
+        grad_second, own_normed, hop_core(peer_normed), hat1, rstd1, vec, dense)
+    grad_first, g0, att_grad, vec1, w_all = lax.optimization_barrier((grad_first, g0, att_grad, vec1, w_all))
     att_grad = lax.all_to_all(att_grad, CT, 0, 0, tiled=True)
     dense_rows = (shard_rows // 4 + shard_rows // 8) * sides
     dense_grad = run(out_weight_kernel, shape((2, 4, size, dense_rows, units), bf16), "out_weight")(
@@ -963,7 +1023,7 @@
     *up_grads, down_grad = run(
         mlp_weights_kernel,
         (shape((size, shard + 16 + dense_rows, units), bf16),) * 4 + (shape((size, 4, strip, width), bf16),),
-        "mlp_weights", 1, flops=16_000_000_000)(
+        "mlp_weights", 1)(
         place_ref, normed_low, normed_peer, g2, g2_peer, act, g1, up_bias_part, dense_own, dense_recv)
     att_grad, up_grads, down_grad = lax.optimization_barrier((att_grad, up_grads, down_grad))
     XY = ("cx", "tp")
@@ -976,33 +1036,42 @@
         first_len, meet, dest, rank, sorted_t, att_t, lse, cos_t, sin_t, att_grad)
     grad_qkv, up_parts, down_parts, final_halves, embed_peer = lax.optimization_barrier(
         (grad_qkv, up_parts, down_parts, final_halves, embed_peer))
-    final_peer = jnp.concatenate(final_halves, axis=0)
     grad_rows = trade(grad_qkv, CT)
 
     base = fs if size <= 4 else jnp.zeros_like(fs)
+    qkv_sums = run(qkv_weight_kernel, shape((size, 400, lanes), bf16), "qkv_weight", 1)(
+        jnp.concatenate([dest, base[None]]).astype(jnp.int32), grad_qkv, qkv_bias_part, *near, *far)
+    qkv_sums, up_parts, down_parts = lax.optimization_barrier((qkv_sums, up_parts, down_parts))
     up_sum, *down_sums = run(
         sum_kernel, (shape(up_grads[0].shape, bf16),) + (shape((strip, width), bf16),) * 4, "sums", 1)(
         jnp.stack([base, place]).astype(jnp.int32), *up_parts, down_parts)
-    up_own = collect_z(up_sum)
-    down_own = add_all([down_sums[0], hop_y(down_sums[1]), hop_x(down_sums[2]), hop(down_sums[3], 5)])
-
-    own_q = collect_z(run(qkv_weight_kernel, shape((size, 400, lanes), bf16), "qkv_weight", 1)(
-        jnp.concatenate([dest, base[None]]).astype(jnp.int32), grad_qkv, qkv_bias_part, *near, *far))
-    q_all = around_ctx(own_q, ctx)
-    dense_all = around_ctx(up_own[shard + 16:], ctx)
-
+    up_parts = send_z(up_sum)
+    down_parts = [down_sums[0], hop_y(down_sums[1]), hop_x(down_sums[2]), hop(down_sums[3], 5)]
+
+    qkv_sums, grad_rows = lax.optimization_barrier((qkv_sums, grad_rows))
     input_low = run(input_grad_kernel, b_rows, "input_grad", 1)(dev_ref, grad_first, grad_rows, *w_all)
     input_peer = hop_y(input_low)
-
-    hidden_grad = jnp.concatenate(
-        [up_own[:shard + 16]] + [down_own[:, s * units:(s + 1) * units] for s in range(sides)], axis=0)
-    hidden_core = hop_core(hidden_grad)
-    halves = jnp.stack([jnp.where(core == 0, hidden_grad, hidden_core), jnp.where(core == 0, hidden_core, hidden_grad)])
+    up_parts, down_parts, qkv_sums, final_low, embed_low = lax.optimization_barrier(
+        (up_parts, down_parts, qkv_sums, final_low, embed_low, input_low))[:5]
+    own_q = add_all(send_z(qkv_sums))
+    q_all = around_ctx(own_q, ctx)
+
+    side_rows = shape((shard + 16, units), bf16)
+    send, away, dense_own = run(
+        hidden_split_kernel, (side_rows, side_rows, shape((dense_rows, units), bf16)), "hidden_split", 1)(
+        core.astype(jnp.int32).reshape(1), *up_parts, *down_parts)
+    recv = hop_core(away)
+    dense_all = around_ctx(dense_own, ctx)
+    halves = jnp.stack([jnp.where(core == 0, send, recv), jnp.where(core == 0, recv, send)])
     joined = trade(jnp.concatenate([halves, halves], axis=0), XY)
-    up_weight_grad, down_weight_grad = run(
-        hidden_join_kernel, (shape(up_weight.shape, f32), shape(down_weight.shape, f32)), "hidden_join")(joined)
-    up_bias_grad = lax.dynamic_slice_in_dim(joined[:, shard], fs * strip, strip, axis=1).reshape(-1).astype(f32)
-
+    joined, input_peer = lax.optimization_barrier((joined, input_peer))
+    joined_core = hop_core(joined)
+    up_weight_grad, down_weight_grad, bias_rows = run(
+        hidden_join_kernel, (shape(up_weight.shape, f32), shape(down_weight.shape, f32), shape((4, 16, units), f32)),
+        "hidden_join", 1)(core.astype(jnp.int32).reshape(1), joined, joined_core)
+    up_bias_grad = lax.dynamic_slice_in_dim(bias_rows[:, 0], fs * strip, strip, axis=1).reshape(-1)
+
+    q_all = q_all.reshape(4, 400, lanes)
     qkv_weight_grad = jnp.transpose(q_all[:, :384].reshape(4, 3, 128, lanes), (3, 1, 0, 2)).reshape(
         lanes, 3, 512).astype(f32)
     qb = jnp.transpose(q_all[:, 384:].reshape(4, -1)[:, :384].reshape(4, 3, 128), (1, 0, 2)).reshape(3, 512)
@@ -1014,14 +1083,14 @@
         dense_all[:, :thin * sides].reshape(4, sides, thin, units), (0, 2, 1, 3)).reshape(shard_rows, width).astype(f32)
     rest = dense_all[:, thin * sides:].reshape(4, sides, tail_rows, units // 128, 128)[:3]
     rest = jnp.transpose(rest, (1, 3, 2, 0, 4)).reshape(shard_rows, 384)
-    rest = pair_rows(rest, hop_y(rest), tp).astype(f32)
+    rest = pair_rows(rest, [hop_y(rest)], tp).astype(f32)
     proj_weight_grad = rest[:, :emb]
     sums = jnp.transpose(rest[:, emb:emb + 6])
 
     return (
-        pair_rows(final_low, final_peer, tp),
-        pair_rows(embed_low, embed_peer, tp),
-        pair_rows(input_low, input_peer, tp),
+        pair_rows(final_low, final_halves, tp),
+        pair_rows(embed_low, [embed_peer], tp),
+        pair_rows(after(input_low, send), [input_peer], tp),
         qkv_weight_grad,
         qkv_bias_grad,
         out_weight_grad,

time: 631 us -> 545 us (0.86)
  waiting for transfers between devices: 139 us -> 97.8 us
  other arithmetic: 38.5 us -> 13.3 us
  between operations: 15 us -> 2 us
    ppermute x6 -> x5, waiting for transfers between devices: 28.5 us -> 0.01 us  [hop(): return lax.ppermute(value, CT, [(i, i ^ u) for i in range(8)])]
    unnamed x114 -> x185, local copies, waits for them, and re-layouts: 19.2 us -> 31.3 us
    ppermute x6, waiting for transfers between devices: 18.8 us -> 7.19 us  [send_z(): lax.ppermute(value[s], 'fsdp', [(i, (i + s) % size) for i in range(size)])]
    reduce_sum x1, other arithmetic: 8.65 us -> 0.12 us  [row_places(): jnp.sum(jnp.where(picked, table[None], 0.0), axis=1).reshape(rows)]
    slice x7 -> x2, local copies, waits for them, and re-layouts: 7.79 us -> 0.87 us  [the longest x1 0.84 us: shards(): bias_rows[:, 0]]
    all_to_all x6 -> x7, starting transfers between devices: 28.2 us -> 32.2 us  [trade(): return lax.all_to_all(value, axes, 0, 0, tiled=True)]
    pallas_call x15 -> x17, Pallas kernels: 132 us -> 130 us  [call(): pl.pallas_call(kernel, out_shape=out_shape, in_specs=[sm] * scalars + [vm...]
    ppermute x12 -> x13, waiting for transfers between devices: 49.4 us -> 48.5 us  [hop_y(): return lax.ppermute(value, 'tp', [(0, 1), (1, 0)])]
  transfers between devices with their start and end apart: 62 -> 63, of which waited for: 20 -> 15; matrix products, arithmetic and copies ran while one was open for 12% -> 8% of each run, Pallas kernels for 42% -> 52%
where the time goes in v3:
time: 545 us; the launch traced here: 543 us
  Pallas kernels  291 us (53%)
  waiting for transfers between devices  97.8 us (18%)
  starting transfers between devices  80.1 us (15%)
  local copies, waits for them, and re-layouts  57.5 us (11%)
  other arithmetic  13.3 us (2%)
    pallas_call x17, Pallas kernels, call(): pl.pallas_call(kernel, out_shape=out_shape, in_specs=[sm] * scalars + [vm...  130 us
    pallas_call x1, Pallas kernels, attention_backward(): pl.pallas_call(backward_kernel, out_shape=(jax.ShapeDtypeStruct((8, 384,...  93.8 us
    pallas_call x1, Pallas kernels, attention_forward(): pl.pallas_call(forward_kernel, out_shape=(jax.ShapeDtypeStruct((8, rows /...  67.9 us
    ppermute x13, waiting for transfers between devices, hop_y(): return lax.ppermute(value, 'tp', [(0, 1), (1, 0)])  48.5 us
    all_to_all x7, starting transfers between devices, trade(): return lax.all_to_all(value, axes, 0, 0, tiled=True)  32.2 us
    unnamed x185, local copies, waits for them, and re-layouts  31.3 us
    all_to_all x7, waiting for transfers between devices, trade(): return lax.all_to_all(value, axes, 0, 0, tiled=True)  26.3 us
    ppermute x13, starting transfers between devices, hop_y(): return lax.ppermute(value, 'tp', [(0, 1), (1, 0)])  15.2 us
  transfers between devices with their start and end apart: 63, of which 15 were waited for; matrix products, arithmetic and copies ran while one was open for 8% of the time, Pallas kernels for 52%

profile of v3, /device:TPU:0, one launch (start us, length us, event | category | flops | bytes accessed | tf_op | source)
XLA Modules:
  0.0 542.7 jit_solution(695673271348492110)
XLA Ops:
  12.4 4.9 all-to-all-start
  24.6 5.6 %collective-permute-done.1 = s32[2,1024]{1,0:T(2,128)S(1)} collective-permute-done((s32[2,1024]{1,0:T(2,128)S(1)}, s32[2,1024]{1,0:T(2,128)S(1)}, u32[]{:S(2)}, u32[]{:S(2)}) %collective-permute-start.1) | collective-permute-done | bytes 8224 | tf_op jit(solution)/shard_map/ppermute | solution.py:805
  32.7 4.8 all-to-all-done.w_ref.refs_0_
  39.1 4.5 all-to-all-start.1
  50.4 11.9 %collective-permute-done.4.refs_2_.refs_4_ = bf16[256,1024]{1,0:T(8,128)(2,1)S(1)} collective-permute-done((bf16[256,1024]{1,0:T(8,128)(2,1)}, bf16[256,1024]{1,0:T(8,128)(2,1)S(1)}, u32[]{:S(2)}, u32[]{:S(2)}) %collective-permute-start.4) | collective-permute-done | bytes 524320 | tf_op jit(solution)/shard_map/ppermute | solution.py:809
  62.3 9.2 %collective-permute-done.5.refs_3_.refs_5_ = bf16[256,1024]{1,0:T(8,128)(2,1)S(1)} collective-permute-done((bf16[256,1024]{1,0:T(8,128)(2,1)}, bf16[256,1024]{1,0:T(8,128)(2,1)S(1)}, u32[]{:S(2)}, u32[]{:S(2)}) %collective-permute-start.5) | collective-permute-done | bytes 524320 | tf_op jit(solution)/shard_map/ppermute | solution.py:809
  73.1 5.8 %qkv_rope.2.near_ref = bf16[384,2048]{1,0:T(8,128)(2,1)} custom-call(s32[1]{0:T(128)} %bitcast.8.ctx_ref, f32[32,4096]{1,0:T(8,128)} %get-tuple-element.436.cos_ref, f32[32,4096]{1,0:T(8,128)} %get-tuple-element.435.sin_ref, bf16[4,400,256]{2,1,0:T(8,128)(2,1)} %copy-done.30, bf16[1024,1024]{1,0:T(8,128)(2,1)} %refs_0_.3, bf16[1024,1024]{1,0:T(8,128)(2,1)} %copy-done.33), custom_call_target="tpu_custom_call" | custom-call | flops 1000000 | bytes 10000 | tf_op jit(solution)/shard_map/qkv_rope/pallas_call | solution.py:36
  83.0 5.8 %qkv_rope.3.far_ref = bf16[384,2048]{1,0:T(8,128)(2,1)} custom-call(s32[1]{0:T(128)} %bitcast.8.ctx_ref, f32[32,4096]{1,0:T(8,128)} %get-tuple-element.436.cos_ref, f32[32,4096]{1,0:T(8,128)} %get-tuple-element.435.sin_ref, bf16[4,400,256]{2,1,0:T(8,128)(2,1)} %copy-done.30, bf16[256,1024]{1,0:T(8,128)(2,1)} %collective-permute-done.2.refs_0_.refs_2_, ...), custom_call_target="tpu_custom_call" | custom-call | flops 1000000 | bytes 10000 | tf_op jit(solution)/shard_map/qkv_rope/pallas_call | solution.py:36
  96.2 4.7 all-to-all-start.2
  100.8 67.9 %attention_forward.1 = (bf16[8,512,128]{2,1,0:T(8,128)(2,1)}, bf16[384,4096]{1,0:T(8,128)(2,1)}, bf16[128,4096]{1,0:T(8,128)(2,1)}, f32[8,4096]{1,0:T(8,128)}) custom-call(s32[1]{0:T(128)} %bitcast.130, s32[64]{0:T(128)} %reshape.514.meet_ref, s32[8]{0:T(128)} %copy-done.84, s32[1,4096]{1,0:T(1,128)} %subtract_select_fusion.rank_ref, ...), custom_call_target="tpu_custom_call" | custom-call | flops 60000002048 | bytes 10000 | tf_op jit(solution)/shard_map/attention_forward/pallas_call | solution.py:160
  168.9 4.2 all-to-all-start.3
  175.5 20.0 %all-to-all-done.3.att_ref = bf16[8,512,128]{2,1,0:T(8,128)(2,1)} async-done(((bf16[8,512,128]{2,1,0:T(8,128)(2,1)}), bf16[8,512,128]{2,1,0:T(8,128)(2,1)}, u32[]{:S(2)}, u32[]{:S(2)}) %all-to-all-start.3) | async-done | bytes 1048608 | tf_op jit(solution)/shard_map/all_to_all | solution.py:817
  197.1 4.3 out_proj.1
  207.6 15.7 %mlp.1 = (bf16[1024,2048]{1,0:T(8,128)(2,1)S(1)}, bf16[1024,2048]{1,0:T(8,128)(2,1)}, f32[512,1024]{1,0:T(8,128)S(1)}, bf16[512,1024]{1,0:T(8,128)(2,1)S(1)}) custom-call(bf16[512,1024]{1,0:T(8,128)(2,1)S(1)} %get-tuple-element.197.own_ref.own_n, bf16[512,1024]{1,0:T(8,128)(2,1)S(1)} %collective-permute-done.16.peer_ref.peer_n, ...), custom_call_target="tpu_custom_call" | custom-call | flops 1000000 | bytes 10000 | tf_op jit(solution)/shard_map/mlp/pallas_call | solution.py:36
  231.5 18.6 %heads.1 = (bf16[512,1024]{1,0:T(8,128)(2,1)}, bf16[512,288]{1,0:T(8,128)(2,1)}, f32[512,1024]{1,0:T(8,128)}, bf16[512,1024]{1,0:T(8,128)(2,1)}, bf16[1024,288]{1,0:T(8,128)(2,1)}, /*index=5*/f32[8,1024]{1,0:T(8,128)}) custom-call(s32[1]{0:T(128)} %bitcast.13.tp_ref, f32[512,1024]{1,0:T(8,128)} %copy-done.15, f32[512,1024]{1,0:T(8,128)} %copy-done.16, ...), custom_call_target="tpu_custom_call" | custom-call | flops 2000000000 | bytes 8000000 | tf_op jit(solution)/shard_map/heads/pallas_call | solution.py:36
  255.8 16.6 %mlp_back.1 = (bf16[1024,2048]{1,0:T(8,128)(2,1)}, f32[1,2048]{1,0:T(1,128)}, f32[512,1024]{1,0:T(8,128)}, bf16[512,1024]{1,0:T(8,128)(2,1)}) custom-call(bf16[512,1024]{1,0:T(8,128)(2,1)} %get-tuple-element.216.own_ref.own_g, bf16[512,1024]{1,0:T(8,128)(2,1)} %copy-done.7, bf16[1024,2048]{1,0:T(8,128)(2,1)} %get-tuple-element.217.slope_ref, ...), custom_call_target="tpu_custom_call" | custom-call | flops 1000000 | bytes 10000 | tf_op jit(solution)/shard_map/mlp_back/pallas_call | solution.py:36
  272.4 2.9 collective-permute-done.23
  279.9 8.9 %first_back.1 = (f32[512,1024]{1,0:T(8,128)}, bf16[512,1024]{1,0:T(8,128)(2,1)}, bf16[8,512,128]{2,1,0:T(8,128)(2,1)}, f32[8,1024]{1,0:T(8,128)}) custom-call(f32[512,1024]{1,0:T(8,128)} %get-tuple-element.215.second_ref, f32[512,1024]{1,0:T(8,128)} %get-tuple-element.226.own_ref, bf16[512,1024]{1,0:T(8,128)(2,1)} %copy-done.48, f32[512,1024]{1,0:T(8,128)} %copy-done.14, ...), custom_call_target="tpu_custom_call" | custom-call | flops 1000000 | bytes 10000 | tf_op jit(solution)/shard_map/first_back/pallas_call | solution.py:36
  294.9 4.4 all-to-all-start.4
  303.0 15.0 %mlp_weights.1 = (bf16[4,368,512]{2,1,0:T(8,128)(2,1)S(1)}, bf16[4,368,512]{2,1,0:T(8,128)(2,1)S(1)}, bf16[4,368,512]{2,1,0:T(8,128)(2,1)S(1)}, bf16[4,368,512]{...) custom-call(s32[1]{0:T(128)} %bitcast.1.place_ref, bf16[512,1024]{1,0:T(8,128)(2,1)S(1)} %copy-done.10, ...), custom_call_target="tpu_custom_call" | custom-call | flops 1000000 | bytes 10000 | tf_op jit(solution)/shard_map/mlp_weights/pallas_call | solution.py:36
  326.0 5.3 all-to-all-start.5
  333.4 93.8 %attention_backward.1 = (bf16[8,384,512]{2,1,0:T(8,128)(2,1)}, f32[384,1]{1,0:T(8,128)}) custom-call(s32[1]{0:T(128)} %bitcast.131, s32[64]{0:T(128)} %reshape.514.meet_ref, s32[8]{0:T(128)} %copy-done.84, s32[1,4096]{1,0:T(1,128)} %subtract_select_fusion.rank_ref, bf16[384,4096]{1,0:T(8,128)(2,1)} %get-tuple-element.182.sorted_ref, ...), custom_call_target="tpu_custom_call" | custom-call | flops 89999998976 | bytes 10000 | tf_op jit(solution)/shard_map/attention_backward/pallas_call | solution.py:295
  428.1 4.5 all-to-all-start.6
  433.2 8.8 %qkv_weight.1 = bf16[4,400,256]{2,1,0:T(8,128)(2,1)} custom-call(s32[9]{0:T(128)} %pad_add_fusion.2.dest_ref, bf16[8,384,512]{2,1,0:T(8,128)(2,1)} %get-tuple-element.266.d_ref, f32[384,1]{1,0:T(8,128)} %get-tuple-element.267.bias_ref, bf16[1024,1024]{1,0:T(8,128)(2,1)} %refs_0_.3, bf16[1024,1024]{1,0:T(8,128)(2,1)} %copy-done.33, ...), custom_call_target="tpu_custom_call" | custom-call | flops 1000000 | bytes 10000 | tf_op jit(solution)/shard_map/qkv_weight/pallas_call | solution.py:36
  442.0 3.9 sums.1
  448.7 4.0 collective-permute-start.38
  454.2 20.8 %collective-permute-done.39.refs_5_ = bf16[128,1024]{1,0:T(8,128)(2,1)S(1)} collective-permute-done((bf16[128,1024]{1,0:T(8,128)(2,1)S(1)}, bf16[128,1024]{1,0:T(8,128)(2,1)S(1)}, u32[]{:S(2)}, u32[]{:S(2)}) %collective-permute-start.39) | collective-permute-done | bytes 262176 | tf_op jit(solution)/shard_map/ppermute | solution.py:809
  476.2 9.9 %input_grad.1 = bf16[512,1024]{1,0:T(8,128)(2,1)} custom-call(s32[1]{0:T(128)} %bitcast.22.dev_ref, f32[512,1024]{1,0:T(8,128)} %get-tuple-element.285.first_ref, bf16[8,384,512]{2,1,0:T(8,128)(2,1)} %all-to-all-done.6.d_ref, bf16[4,400,256]{2,1,0:T(8,128)(2,1)} %copy-done.30, bf16[4,400,256]{2,1,0:T(8,128)(2,1)} %copy-done.51, ...), custom_call_target="tpu_custom_call" | custom-call | flops 1000000 | bytes 10000 | tf_op jit(solution)/shard_map/input_grad/pallas_call | solution.py:36
  504.8 4.3 all-to-all-start.7
  509.1 7.2 %collective-permute-done.45 = bf16[400,256]{1,0:T(8,128)(2,1)S(1)} collective-permute-done((bf16[400,256]{1,0:T(8,128)(2,1)S(1)}, bf16[400,256]{1,0:T(8,128)(2,1)S(1)}, u32[]{:S(2)}, u32[]{:S(2)}) %collective-permute-start.45) | collective-permute-done | bytes 204832 | tf_op jit(solution)/shard_map/ppermute | solution.py:836
  520.6 7.2 %collective-permute-done.48 = bf16[400,256]{1,0:T(8,128)(2,1)S(1)} collective-permute-done((bf16[400,256]{1,0:T(8,128)(2,1)S(1)}, bf16[400,256]{1,0:T(8,128)(2,1)S(1)}, u32[]{:S(2)}, u32[]{:S(2)}) %collective-permute-start.48) | collective-permute-done | bytes 204832 | tf_op jit(solution)/shard_map/ppermute | solution.py:805
  537.0 4.0 hidden_join.1
  (394 shorter events, 131.4 us)
Async XLA Ops:
  1.2 70.6 %collective-permute-start.11 = (bf16[1024,1024]{1,0:T(8,128)(2,1)}, bf16[1024,1024]{1,0:T(8,128)(2,1)S(1)}, u32[]{:S(2)}, u32[]{:S(2)}) collective-permute-start(bf16[1024,1024]{1,0:T(8,128)(2,1)} %refs_0_.3), channel_id=1, source_target_pairs={{0,2},{2,0},{1,3},{3,1},{4,6},{6,4},{5,7},{7,5},{8,10},{10,8},{9,1... | collective-permute-start | bytes 6291464 | tf_op jit(solution)/shard_map/ppermute | solution.py:801
  3.5 43.6 %collective-permute-start.2 = (bf16[256,1024]{1,0:T(8,128)(2,1)}, bf16[256,1024]{1,0:T(8,128)(2,1)}, u32[]{:S(2)}, u32[]{:S(2)}) collective-permute-start(bf16[256,1024]{1,0:T(8,128)(2,1)} %get-tuple-element.413), channel_id=1, source_target_pairs={{0,4},{4,0},{1,5},{5,1},{2,6},{6,2},{3,7},{7,3},{8,12},{12,8},{9,1... | collective-permute-start | bytes 1572872 | tf_op jit(solution)/shard_map/ppermute | solution.py:805
  6.4 41.3 %collective-permute-start.3 = (bf16[256,1024]{1,0:T(8,128)(2,1)}, bf16[256,1024]{1,0:T(8,128)(2,1)}, u32[]{:S(2)}, u32[]{:S(2)}) collective-permute-start(bf16[256,1024]{1,0:T(8,128)(2,1)} %get-tuple-element.412), channel_id=1, source_target_pairs={{0,4},{4,0},{1,5},{5,1},{2,6},{6,2},{3,7},{7,3},{8,12},{12,8},{9,1... | collective-permute-start | bytes 1572872 | tf_op jit(solution)/shard_map/ppermute | solution.py:805
  9.1 22.4 %collective-permute-start.10 = (bf16[512,512]{1,0:T(8,128)(2,1)}, bf16[512,512]{1,0:T(8,128)(2,1)}, u32[]{:S(2)}, u32[]{:S(2)}) collective-permute-start(bf16[512,512]{1,0:T(8,128)(2,1)} %get-tuple-element.168), channel_id=1, source_target_pairs={{0,1},{1,0},{2,3},{3,2},{4,5},{5,4},{6,7},{7,6},{8,9},{9,8},{10,11... | collective-permute-start | bytes 1572872 | tf_op jit(solution)/shard_map/ppermute | solution.py:809
  12.4 25.1 %all-to-all-start = ((bf16[4,400,256]{2,1,0:T(8,128)(2,1)}), bf16[4,400,256]{2,1,0:T(8,128)(2,1)S(1)}, u32[]{:S(2)}, u32[]{:S(2)}) async-start(bf16[4,400,256]{2,1,0:T(8,128)(2,1)} %broadcast_in_dim.83), calls=%async_computation | async-start | bytes 1638400 | tf_op jit(solution)/shard_map/all_to_all | solution.py:817
  39.1 52.2 %all-to-all-start.1 = ((bf16[4,512,512]{2,1,0:T(8,128)(2,1)}), bf16[4,512,512]{2,1,0:T(8,128)(2,1)}, u32[]{:S(2)}, u32[]{:S(2)}) async-start(bf16[4,512,512]{2,1,0:T(8,128)(2,1)} %broadcast_in_dim.124), calls=%async_computation.1 | async-start | bytes 4194304 | tf_op jit(solution)/shard_map/all_to_all | solution.py:817
  47.7 23.8 %collective-permute-start.5 = (bf16[256,1024]{1,0:T(8,128)(2,1)}, bf16[256,1024]{1,0:T(8,128)(2,1)S(1)}, u32[]{:S(2)}, u32[]{:S(2)}) collective-permute-start(bf16[256,1024]{1,0:T(8,128)(2,1)} %collective-permute-done.3.refs_1_.refs_3_), channel_id=1, source_target_pairs={{0,1},{1,0},{2,3},{3,2},{4,5},{5,4},{6,7},{7,6},{8,9},{9,8},{10,11... | collective-permute-start | bytes 1572872 | tf_op jit(solution)/shard_map/ppermute | solution.py:809
  49.9 29.0 %collective-permute-start.6 = (bf16[256,1024]{1,0:T(8,128)(2,1)}, bf16[256,1024]{1,0:T(8,128)(2,1)S(1)}, u32[]{:S(2)}, u32[]{:S(2)}) collective-permute-start(bf16[256,1024]{1,0:T(8,128)(2,1)} %collective-permute-done.2.refs_0_.refs_2_), channel_id=1, source_target_pairs={{0,2},{2,0},{1,3},{3,1},{4,6},{6,4},{5,7},{7,5},{8,10},{10,8},{9,1... | collective-permute-start | bytes 1572872 | tf_op jit(solution)/shard_map/ppermute | solution.py:801
  49.9 29.0 %collective-permute-start.7 = (bf16[256,1024]{1,0:T(8,128)(2,1)}, bf16[256,1024]{1,0:T(8,128)(2,1)S(1)}, u32[]{:S(2)}, u32[]{:S(2)}) collective-permute-start(bf16[256,1024]{1,0:T(8,128)(2,1)} %collective-permute-done.3.refs_1_.refs_3_), channel_id=1, source_target_pairs={{0,2},{2,0},{1,3},{3,1},{4,6},{6,4},{5,7},{7,5},{8,10},{10,8},{9,1... | collective-permute-start | bytes 1572872 | tf_op jit(solution)/shard_map/ppermute | solution.py:801
  91.3 77.4 %collective-permute-start.13 = (bf16[4,512,512]{2,1,0:T(8,128)(2,1)}, bf16[4,512,512]{2,1,0:T(8,128)(2,1)S(1)}, u32[]{:S(2)}, u32[]{:S(2)}) collective-permute-start(bf16[4,512,512]{2,1,0:T(8,128)(2,1)} %all-to-all-done.1.refs_0_), channel_id=1, source_target_pairs={{0,1},{1,0},{2,3},{3,2},{4,5},{5,4},{6,7},{7,6},{8,9},{9,8},{10,11... | collective-permute-start | bytes 6291464 | tf_op jit(solution)/shard_map/ppermute | solution.py:809
  91.8 76.9 %collective-permute-start.14 = (bf16[4,512,512]{2,1,0:T(8,128)(2,1)}, bf16[4,512,512]{2,1,0:T(8,128)(2,1)}, u32[]{:S(2)}, u32[]{:S(2)}) collective-permute-start(bf16[4,512,512]{2,1,0:T(8,128)(2,1)} %all-to-all-done.1.refs_0_), channel_id=1, source_target_pairs={{0,4},{4,0},{1,5},{5,1},{2,6},{6,2},{3,7},{7,3},{8,12},{12,8},{9,1... | collective-permute-start | bytes 6291464 | tf_op jit(solution)/shard_map/ppermute | solution.py:805
  93.3 111.7 %collective-permute-start.17 = (bf16[4,512,512]{2,1,0:T(8,128)(2,1)}, bf16[4,512,512]{2,1,0:T(8,128)(2,1)}, u32[]{:S(2)}, u32[]{:S(2)}) collective-permute-start(bf16[4,512,512]{2,1,0:T(8,128)(2,1)} %all-to-all-done.1.refs_0_), channel_id=1, source_target_pairs={{0,5},{1,4},{2,7},{3,6},{4,1},{5,0},{6,3},{7,2},{8,13},{9,12},{10,... | collective-permute-start | bytes 6291464 | tf_op jit(solution)/shard_map/ppermute | solution.py:797
  96.2 72.6 %all-to-all-start.2 = ((bf16[4,2,80,1312]{3,2,1,0:T(8,128)(2,1)}), bf16[4,2,80,1312]{3,2,1,0:T(8,128)(2,1)}, u32[]{:S(2)}, u32[]{:S(2)}) async-start(bf16[4,2,80,1312]{3,2,1,0:T(8,128)(2,1)} %broadcast_in_dim.125), calls=%async_computation.2 | async-start | bytes 3604480 | tf_op jit(solution)/shard_map/all_to_all | solution.py:817
  168.9 26.7 %all-to-all-start.3 = ((bf16[8,512,128]{2,1,0:T(8,128)(2,1)}), bf16[8,512,128]{2,1,0:T(8,128)(2,1)}, u32[]{:S(2)}, u32[]{:S(2)}) async-start(bf16[8,512,128]{2,1,0:T(8,128)(2,1)} %get-tuple-element.188), calls=%async_computation.3 | async-start | bytes 2097152 | tf_op jit(solution)/shard_map/all_to_all | solution.py:817
  205.0 21.6 %collective-permute-start.18 = (bf16[4,400,256]{2,1,0:T(8,128)(2,1)S(1)}, bf16[4,400,256]{2,1,0:T(8,128)(2,1)S(1)}, u32[]{:S(2)}, u32[]{:S(2)}) collective-permute-start(bf16[4,400,256]{2,1,0:T(8,128)(2,1)S(1)} %copy-done.31), channel_id=1, source_target_pairs={{0,1},{1,0},{2,3},{3,2},{4,5},{5,4},{6,7},{7,6},{8,9},{9,8},{10,11... | collective-permute-start | bytes 2457608 | tf_op jit(solution)/shard_map/ppermute | solution.py:809
  227.7 22.4 %collective-permute-start.21 = (bf16[2,400,256]{2,1,0:T(8,128)(2,1)S(1)}, bf16[2,400,256]{2,1,0:T(8,128)(2,1)S(1)}, u32[]{:S(2)}, u32[]{:S(2)}) collective-permute-start(bf16[2,400,256]{2,1,0:T(8,128)(2,1)S(1)} %get-tuple-element.214), channel_id=1, source_target_pairs={{0,5},{1,4},{2,7},{3,6},{4,1},{5,0},{6,3},{7,2},{8,13},{9,12},{10,... | collective-permute-start | bytes 1228808 | tf_op jit(solution)/shard_map/ppermute | solution.py:797
  252.4 22.9 %collective-permute-start.23 = (bf16[256,1024]{1,0:T(8,128)(2,1)S(1)}, bf16[256,1024]{1,0:T(8,128)(2,1)S(1)}, u32[]{:S(2)}, u32[]{:S(2)}) collective-permute-start(bf16[256,1024]{1,0:T(8,128)(2,1)S(1)} %get-tuple-element.223), channel_id=1, source_target_pairs={{0,1},{1,0},{2,3},{3,2},{4,5},{5,4},{6,7},{7,6},{8,9},{9,8},{10,11... | collective-permute-start | bytes 1572872 | tf_op jit(solution)/shard_map/ppermute | solution.py:809
  294.9 27.6 %all-to-all-start.4 = ((bf16[8,512,128]{2,1,0:T(8,128)(2,1)}), bf16[8,512,128]{2,1,0:T(8,128)(2,1)}, u32[]{:S(2)}, u32[]{:S(2)}) async-start(bf16[8,512,128]{2,1,0:T(8,128)(2,1)} %get-tuple-element.242), calls=%async_computation.4 | async-start | bytes 2097152 | tf_op jit(solution)/shard_map/all_to_all | solution.py:1017
  322.5 104.7 %collective-permute-start.31 = (bf16[4,368,512]{2,1,0:T(8,128)(2,1)}, bf16[4,368,512]{2,1,0:T(8,128)(2,1)S(1)}, u32[]{:S(2)}, u32[]{:S(2)}) collective-permute-start(bf16[4,368,512]{2,1,0:T(8,128)(2,1)} %copy-done.29), channel_id=1, source_target_pairs={{0,1},{1,0},{2,3},{3,2},{4,5},{5,4},{6,7},{7,6},{8,9},{9,8},{10,11... | collective-permute-start | bytes 4521992 | tf_op jit(solution)/shard_map/ppermute | solution.py:809
  324.4 102.8 %collective-permute-start.32 = (bf16[4,368,512]{2,1,0:T(8,128)(2,1)}, bf16[4,368,512]{2,1,0:T(8,128)(2,1)S(1)}, u32[]{:S(2)}, u32[]{:S(2)}) collective-permute-start(bf16[4,368,512]{2,1,0:T(8,128)(2,1)} %copy-done.28), channel_id=1, source_target_pairs={{0,4},{4,0},{1,5},{5,1},{2,6},{6,2},{3,7},{7,3},{8,12},{12,8},{9,1... | collective-permute-start | bytes 4521992 | tf_op jit(solution)/shard_map/ppermute | solution.py:805
  325.9 102.2 %collective-permute-start.33 = (bf16[4,368,512]{2,1,0:T(8,128)(2,1)}, bf16[4,368,512]{2,1,0:T(8,128)(2,1)}, u32[]{:S(2)}, u32[]{:S(2)}) collective-permute-start(bf16[4,368,512]{2,1,0:T(8,128)(2,1)} %copy-done.27), channel_id=1, source_target_pairs={{0,5},{1,4},{2,7},{3,6},{4,1},{5,0},{6,3},{7,2},{8,13},{9,12},{10,... | collective-permute-start | bytes 4521992 | tf_op jit(solution)/shard_map/ppermute | solution.py:797
  326.0 102.1 %all-to-all-start.5 = ((bf16[4,4,128,1024]{3,2,1,0:T(8,128)(2,1)}), bf16[4,4,128,1024]{3,2,1,0:T(8,128)(2,1)}, u32[]{:S(2)}, u32[]{:S(2)}) async-start(bf16[4,4,128,1024]{3,2,1,0:T(8,128)(2,1)} %get-tuple-element.261), calls=%async_computation.5 | async-start | bytes 8388608 | tf_op jit(solution)/shard_map/all_to_all | solution.py:817
  331.3 95.9 %collective-permute-start.34 = (bf16[256,1024]{1,0:T(8,128)(2,1)S(1)}, bf16[256,1024]{1,0:T(8,128)(2,1)S(1)}, u32[]{:S(2)}, u32[]{:S(2)}) collective-permute-start(bf16[256,1024]{1,0:T(8,128)(2,1)S(1)} %copy-done.58), channel_id=1, source_target_pairs={{0,1},{1,0},{2,3},{3,2},{4,5},{5,4},{6,7},{7,6},{8,9},{9,8},{10,11... | collective-permute-start | bytes 1572872 | tf_op jit(solution)/shard_map/ppermute | solution.py:809
  333.2 93.9 %collective-permute-start.35 = (bf16[512,288]{1,0:T(8,128)(2,1)}, bf16[512,288]{1,0:T(8,128)(2,1)S(1)}, u32[]{:S(2)}, u32[]{:S(2)}) collective-permute-start(bf16[512,288]{1,0:T(8,128)(2,1)} %get-tuple-element.298), channel_id=1, source_target_pairs={{0,1},{1,0},{2,3},{3,2},{4,5},{5,4},{6,7},{7,6},{8,9},{9,8},{10,11... | collective-permute-start | bytes 884744 | tf_op jit(solution)/shard_map/ppermute | solution.py:809
  428.1 48.2 %all-to-all-start.6 = ((bf16[8,384,512]{2,1,0:T(8,128)(2,1)}), bf16[8,384,512]{2,1,0:T(8,128)(2,1)}, u32[]{:S(2)}, u32[]{:S(2)}) async-start(bf16[8,384,512]{2,1,0:T(8,128)(2,1)} %get-tuple-element.266.d_ref), calls=%async_computation.6 | async-start | bytes 6291456 | tf_op jit(solution)/shard_map/all_to_all | solution.py:817
  445.9 29.1 %collective-permute-start.39 = (bf16[128,1024]{1,0:T(8,128)(2,1)S(1)}, bf16[128,1024]{1,0:T(8,128)(2,1)S(1)}, u32[]{:S(2)}, u32[]{:S(2)}) collective-permute-start(bf16[128,1024]{1,0:T(8,128)(2,1)S(1)} %get-tuple-element.280), channel_id=1, source_target_pairs={{0,1},{1,0},{2,3},{3,2},{4,5},{5,4},{6,7},{7,6},{8,9},{9,8},{10,11... | collective-permute-start | bytes 786440 | tf_op jit(solution)/shard_map/ppermute | solution.py:809
  448.7 39.2 %collective-permute-start.36 = (bf16[368,512]{1,0:T(8,128)(2,1)S(1)}, bf16[368,512]{1,0:T(8,128)(2,1)S(1)}, u32[]{:S(2)}, u32[]{:S(2)}) collective-permute-start(bf16[368,512]{1,0:T(8,128)(2,1)S(1)} %get-tuple-element.416), channel_id=1, source_target_pairs={{0,8},{8,16},{16,24},{24,0},{1,9},{9,17},{17,25},{25,1},{2,10},{10... | collective-permute-start | bytes 1130504 | tf_op jit(solution)/shard_map/ppermute | solution.py:836
  448.7 39.2 %collective-permute-start.37 = (bf16[368,512]{1,0:T(8,128)(2,1)S(1)}, bf16[368,512]{1,0:T(8,128)(2,1)S(1)}, u32[]{:S(2)}, u32[]{:S(2)}) collective-permute-start(bf16[368,512]{1,0:T(8,128)(2,1)S(1)} %get-tuple-element.415), channel_id=1, source_target_pairs={{0,16},{8,24},{16,0},{24,8},{1,17},{9,25},{17,1},{25,9},{2,18},{10... | collective-permute-start | bytes 1130504 | tf_op jit(solution)/shard_map/ppermute | solution.py:836
  448.7 39.2 %collective-permute-start.38 = (bf16[368,512]{1,0:T(8,128)(2,1)S(1)}, bf16[368,512]{1,0:T(8,128)(2,1)S(1)}, u32[]{:S(2)}, u32[]{:S(2)}) collective-permute-start(bf16[368,512]{1,0:T(8,128)(2,1)S(1)} %get-tuple-element.414), channel_id=1, source_target_pairs={{0,24},{8,0},{16,8},{24,16},{1,25},{9,1},{17,9},{25,17},{2,26},{10... | collective-permute-start | bytes 1130504 | tf_op jit(solution)/shard_map/ppermute | solution.py:836
  452.7 33.5 %collective-permute-start.40 = (bf16[128,1024]{1,0:T(8,128)(2,1)S(1)}, bf16[128,1024]{1,0:T(8,128)(2,1)S(1)}, u32[]{:S(2)}, u32[]{:S(2)}) collective-permute-start(bf16[128,1024]{1,0:T(8,128)(2,1)S(1)} %get-tuple-element.281), channel_id=1, source_target_pairs={{0,4},{4,0},{1,5},{5,1},{2,6},{6,2},{3,7},{7,3},{8,12},{12,8},{9,1... | collective-permute-start | bytes 786440 | tf_op jit(solution)/shard_map/ppermute | solution.py:805
  486.1 43.8 %collective-permute-start.43 = (bf16[512,1024]{1,0:T(8,128)(2,1)}, bf16[512,1024]{1,0:T(8,128)(2,1)}, u32[]{:S(2)}, u32[]{:S(2)}) collective-permute-start(bf16[512,1024]{1,0:T(8,128)(2,1)} %input_grad.1), channel_id=1, source_target_pairs={{0,1},{1,0},{2,3},{3,2},{4,5},{5,4},{6,7},{7,6},{8,9},{9,8},{10,11... | collective-permute-start | bytes 3145736 | tf_op jit(solution)/shard_map/ppermute | solution.py:809
  504.8 25.2 %all-to-all-start.7 = ((bf16[4,272,512]{2,1,0:T(8,128)(2,1)}), bf16[4,272,512]{2,1,0:T(8,128)(2,1)}, u32[]{:S(2)}, u32[]{:S(2)}) async-start(bf16[4,272,512]{2,1,0:T(8,128)(2,1)} %pad_maximum_fusion.2), calls=%async_computation.7 | async-start | bytes 2228224 | tf_op jit(solution)/shard_map/all_to_all | solution.py:817
  (117 other events, 874.6 us)

commit v4 on v3

--- a/solution.py
+++ b/solution.py
@@ -497,24 +497,18 @@
                 peer_out[:, s * units:(s + 1) * units] = out[s].astype(bf16)
 
 
-def head_kernel(strip_rows, tp_ref, normed_ref, own_ref, recv_ref, all_vec_ref, dense_ref, cot_ref, cot_embed_ref,
-                final_ref, embed_ref, grad_ref, low_ref, proj_grad_ref, vec_ref, proj_ref):
-    width, emb = proj_ref.shape
-    strip = strip_rows
-    for f in range(width // (2 * strip)):
-        for t in range(2):
-            at = (f * 2 + t) * strip
-            src = (t * (width // (2 * strip)) + f) * strip
-            proj_ref[at:at + strip, :] = dense_ref[src:src + strip, width:width + emb]
+def head_kernel(tp_ref, normed_ref, own_ref, recv_ref, all_vec_ref, proj_ref, cot_ref, cot_embed_ref,
+                first_ref, last_ref, embed_ref, grad_ref, low_ref, proj_grad_ref, vec_ref):
     half = normed_ref.shape[0]
     mine = pl.ds(pl.multiple_of(tp_ref[0] * half, half), half)
     gain = all_vec_ref[4:5]
     second = normed_ref[...] + own_ref[...] + recv_ref[...].astype(f32) + all_vec_ref[3:4]
     x_hat, rstd = norm_parts(second)
     final = (x_hat * gain + all_vec_ref[5:6]).astype(bf16)
-    final_ref[...] = final
+    first_ref[...] = final[:half // 2]
+    last_ref[...] = final[half // 2:]
     projected = nn(final, proj_ref[...])
-    cot = cot_embed_ref[mine, :].astype(f32)
+    cot = cot_embed_ref[...].astype(f32)
     col = lax.broadcasted_iota(jnp.int32, projected.shape, 1)
     embedded = jnp.zeros(projected.shape, f32)
     grad_proj = jnp.zeros(projected.shape, f32)
@@ -633,7 +627,7 @@
     half[count:count + 16, width:] = jnp.zeros((16, half.shape[1] - width), bf16)
 
 
-def dense_natural_kernel(index_ref, own_ref, core_ref, out_ref, vec_ref, up_ref):
+def dense_natural_kernel(index_ref, own_ref, core_ref, out_ref, proj_ref, vec_ref, up_ref):
     core, place, tp = (index_ref[i] for i in range(3))
     size, rows = own_ref.shape[0], own_ref.shape[2] - 16
     units = up_ref.shape[1] // 4
@@ -643,7 +637,10 @@
             own, other = own_ref[f, tp ^ t, 0:rows], core_ref[f, tp ^ t, 0:rows]
             for k in range(2):
                 at = ((t * size + f) * 2 + k) * rows
-                out_ref[at:at + rows, :] = jnp.where(core == k, own, other)
+                value = jnp.where(core == k, own, other)
+                out_ref[at:at + rows, :] = value[:, 0:out_ref.shape[1]]
+                at = ((f * 2 + t) * 2 + k) * rows
+                proj_ref[at:at + rows, :] = value[:, out_ref.shape[1]:]
         vecs = own_ref[f, 0, rows:rows + 16].astype(f32)
         wanted = own_ref[f, tp ^ core, rows:rows + 16].astype(f32)
         cut = 4 * strip
@@ -847,8 +844,9 @@
 
 
 def pair_rows(own, peers, tp):
-    half = own.shape[0]
-    out = jnp.concatenate([own, own], axis=0)
+    own = own if isinstance(own, list) else [own]
+    half = sum(p.shape[0] for p in own)
+    out = jnp.concatenate(own + own, axis=0)
     at = (1 - tp) * half
     for p in peers:
         out = lax.dynamic_update_slice_in_dim(out, p, at, axis=0)
@@ -959,24 +957,27 @@
     cos_t, sin_t = rope_tables_t(position)
 
     near_mixed = qkv_rope(ctx_ref, near, weights, cos_t, sin_t, 0)
-    far, near_mixed = lax.optimization_barrier((far, near_mixed))
+    cot_embed_own = own_half(cot_embed, tp)
+    far, near_mixed, cot_embed_own = lax.optimization_barrier((far, near_mixed, cot_embed_own))
     if size <= 4:
         dense_half = run(dense_half_kernel, shape((shard_rows // 2 + 16, width + emb), bf16), "dense_half", 1)(
             jnp.stack([core, tp]).astype(jnp.int32), after(out_weight, near_mixed), proj_weight,
             *[v.reshape(1, -1) for v in vectors])
     dense_pair = jnp.stack([dense_half, hop_y(dense_half)])
     far_mixed = qkv_rope(ctx_ref, far, weights, cos_t, sin_t, rows // 2)
-    hidden0, far_mixed, dense_pair = lax.optimization_barrier((hidden0, far_mixed, dense_pair))
-    dense_parts = gather(dense_pair, "fsdp", size)
+    dense_copies = jnp.broadcast_to(dense_pair[None], (size,) + dense_pair.shape)
+    hidden0, far_mixed, dense_copies = lax.optimization_barrier((hidden0, far_mixed, dense_copies))
+    dense_parts = trade(dense_copies, "fsdp")
     hiddens = [hidden0, hop_y(hidden0), hop_x(hidden0), hop(hidden0, 5)]
     att, sorted_t, att_t, lse = attention_forward(first_len, meet, dest, rank, near_mixed, far_mixed)
     att, dense_parts, hiddens[1:3] = lax.optimization_barrier((att, dense_parts, hiddens[1:3]))
     att = trade(att, CT)
-    dense, vec, up_b = run(
+    dense, proj_full, vec, up_b = run(
         dense_natural_kernel,
-        (shape((width, width + emb), bf16), shape((8, width), f32), shape((1, 4 * units), f32)), "dense_natural", 1)(
+        (shape((width, width), bf16), shape((width, emb), bf16), shape((8, width), f32), shape((1, 4 * units), f32)),
+        "dense_natural", 1)(
         jnp.stack([core, place, tp]).astype(jnp.int32), dense_parts, hop_core(dense_parts))
-    att, dense, vec, up_b = lax.optimization_barrier((att, dense, vec, up_b))
+    att, dense, proj_full, vec, up_b = lax.optimization_barrier((att, dense, proj_full, vec, up_b))
 
     f_rows, b_rows = shape((half, width), f32), shape((half, width), bf16)
     normed, hat1, rstd1, normed_low = run(
@@ -992,17 +993,18 @@
     w_cut = max(1, w_own.shape[0] // 2)
     w_xy = [hop(after(w_own[:w_cut], own_down), 5)]
     vec_shape = shape((8, width), f32)
-    final_low, embed_low, grad_second, g2, proj_grad, vec2 = run(
-        partial(head_kernel, shard_rows),
-        (b_rows, shape((half, emb), bf16), f_rows, b_rows, shape((width, emb), bf16), vec_shape), "heads", 1,
-        scratch=[pltpu.VMEM((width, emb), bf16)], flops=2_000_000_000)(
-        tp_ref, normed, own_down, hop_core(peer_down), vec, dense, cot_output, cot_embed)
-    final_low, embed_low, grad_second, g2, proj_grad, vec2, w_xy[0] = lax.optimization_barrier(
-        (final_low, embed_low, grad_second, g2, proj_grad, vec2, w_xy[0]))
+    final_top, final_end, embed_low, grad_second, g2, proj_grad, vec2 = run(
+        head_kernel,
+        (shape((half // 2, width), bf16),) * 2
+        + (shape((half, emb), bf16), f_rows, b_rows, shape((width, emb), bf16), vec_shape), "heads", 1,
+        flops=2_000_000_000)(
+        tp_ref, normed, own_down, hop_core(peer_down), vec, proj_full, cot_output, cot_embed_own)
+    final_top, final_end, embed_low, grad_second, g2, proj_grad, vec2, w_xy[0] = lax.optimization_barrier(
+        (final_top, final_end, embed_low, grad_second, g2, proj_grad, vec2, w_xy[0]))
     g2_peer = hop_core(g2)
     if w_cut < w_own.shape[0]:
         w_xy.append(hop(after(w_own[w_cut:], w_xy[0]), 5))
-    final_halves = [hop_y(after(final_low[:half // 2], g2))]
+    final_halves = [hop_y(after(final_top, g2))]
     g1, up_bias_part, own_normed, peer_normed = run(
         mlp_back_kernel, (hidden, shape((1, 4 * units), f32), f_rows, b_rows), "mlp_back")(
         g2, g2_peer, slope, *hiddens)
@@ -1029,7 +1031,7 @@
     XY = ("cx", "tp")
     down_parts = trade(down_grad, "fsdp")
     up_parts = [up_grads[0], hop_y(up_grads[1]), hop_x(up_grads[2]), hop(up_grads[3], 5)]
-    final_rest, embed_late = after(final_low[half // 2:], att_grad), after(embed_low, att_grad)
+    final_rest, embed_late = after(final_end, att_grad), after(embed_low, att_grad)
     final_halves.append(hop_y(final_rest))
     embed_peer = hop_y(embed_late)
     grad_qkv, qkv_bias_part = attention_backward(
@@ -1051,8 +1053,8 @@
     qkv_sums, grad_rows = lax.optimization_barrier((qkv_sums, grad_rows))
     input_low = run(input_grad_kernel, b_rows, "input_grad", 1)(dev_ref, grad_first, grad_rows, *w_all)
     input_peer = hop_y(input_low)
-    up_parts, down_parts, qkv_sums, final_low, embed_low = lax.optimization_barrier(
-        (up_parts, down_parts, qkv_sums, final_low, embed_low, input_low))[:5]
+    up_parts, down_parts, qkv_sums, final_top, final_end, embed_low = lax.optimization_barrier(
+        (up_parts, down_parts, qkv_sums, final_top, final_end, embed_low, input_low))[:6]
     own_q = add_all(send_z(qkv_sums))
     q_all = around_ctx(own_q, ctx)
 
@@ -1088,7 +1090,7 @@
     sums = jnp.transpose(rest[:, emb:emb + 6])
 
     return (
-        pair_rows(final_low, final_halves, tp),
+        pair_rows([final_top, final_end], final_halves, tp),
         pair_rows(embed_low, [embed_peer], tp),
         pair_rows(after(input_low, send), [input_peer], tp),
         qkv_weight_grad,

time: 545 us -> 539 us (0.989)
  starting transfers between devices: 80.1 us -> 91.4 us
  Pallas kernels: 291 us -> 280 us
    ppermute x6, starting transfers between devices: 6.03 us -> 17 us  [send_z(): lax.ppermute(value[s], 'fsdp', [(i, (i + s) % size) for i in range(size)])]
    ppermute x13, waiting for transfers between devices: 48.5 us -> 40 us  [hop_y(): return lax.ppermute(value, 'tp', [(0, 1), (1, 0)])]
    pallas_call x1, Pallas kernels: 93.8 us -> 88 us  [attention_backward(): pl.pallas_call(backward_kernel, out_shape=(jax.ShapeDtypeStruct((8, 384,...]
    unnamed x185 -> x176, local copies, waits for them, and re-layouts: 31.3 us -> 30.5 us
  transfers between devices with their start and end apart: 63 -> 63, of which waited for: 15 -> 16; matrix products, arithmetic and copies ran while one was open for 8% -> 7% of each run, Pallas kernels for 52% -> 51%
where the time goes in v4:
time: 539 us; the launch traced here: 534 us
  Pallas kernels  280 us (52%)
  waiting for transfers between devices  94.1 us (17%)
  starting transfers between devices  91.4 us (17%)
  local copies, waits for them, and re-layouts  54.2 us (10%)
  other arithmetic  12 us (2%)
    pallas_call x17, Pallas kernels, call(): pl.pallas_call(kernel, out_shape=out_shape, in_specs=[sm] * scalars + [vm...  126 us
    pallas_call x1, Pallas kernels, attention_backward(): pl.pallas_call(backward_kernel, out_shape=(jax.ShapeDtypeStruct((8, 384,...  88 us
    pallas_call x1, Pallas kernels, attention_forward(): pl.pallas_call(forward_kernel, out_shape=(jax.ShapeDtypeStruct((8, rows /...  66 us
    ppermute x13, waiting for transfers between devices, hop_y(): return lax.ppermute(value, 'tp', [(0, 1), (1, 0)])  40 us
    all_to_all x7, starting transfers between devices, trade(): return lax.all_to_all(value, axes, 0, 0, tiled=True)  31.7 us
    unnamed x176, local copies, waits for them, and re-layouts  30.5 us
    all_to_all x7, waiting for transfers between devices, trade(): return lax.all_to_all(value, axes, 0, 0, tiled=True)  28.7 us
    ppermute x6, starting transfers between devices, send_z(): lax.ppermute(value[s], 'fsdp', [(i, (i + s) % size) for i in range(size)])  17 us
  transfers between devices with their start and end apart: 63, of which 16 were waited for; matrix products, arithmetic and copies ran while one was open for 7% of the time, Pallas kernels for 51%

profile of v4, /device:TPU:0, one launch (start us, length us, event | category | flops | bytes accessed | tf_op | source)
XLA Modules:
  0.0 533.9 jit_solution(5118298244284459504)
XLA Ops:
  12.5 4.9 all-to-all-start
  26.6 3.6 collective-permute-done.1
  32.7 4.9 all-to-all-done.w_ref.refs_0_
  39.1 4.5 all-to-all-start.1
  50.5 11.9 %collective-permute-done.4.refs_2_.refs_4_ = bf16[256,1024]{1,0:T(8,128)(2,1)S(1)} collective-permute-done((bf16[256,1024]{1,0:T(8,128)(2,1)}, bf16[256,1024]{1,0:T(8,128)(2,1)S(1)}, u32[]{:S(2)}, u32[]{:S(2)}) %collective-permute-start.4) | collective-permute-done | bytes 524320 | tf_op jit(solution)/shard_map/ppermute | solution.py:806
  62.3 9.2 %collective-permute-done.5.refs_3_.refs_5_ = bf16[256,1024]{1,0:T(8,128)(2,1)S(1)} collective-permute-done((bf16[256,1024]{1,0:T(8,128)(2,1)}, bf16[256,1024]{1,0:T(8,128)(2,1)S(1)}, u32[]{:S(2)}, u32[]{:S(2)}) %collective-permute-start.5) | collective-permute-done | bytes 524320 | tf_op jit(solution)/shard_map/ppermute | solution.py:806
  73.1 5.8 %qkv_rope.2.near_ref = bf16[384,2048]{1,0:T(8,128)(2,1)} custom-call(s32[1]{0:T(128)} %bitcast.8.ctx_ref, f32[32,4096]{1,0:T(8,128)} %get-tuple-element.446.cos_ref, f32[32,4096]{1,0:T(8,128)} %get-tuple-element.445.sin_ref, bf16[4,400,256]{2,1,0:T(8,128)(2,1)} %copy-done.32, bf16[1024,1024]{1,0:T(8,128)(2,1)} %refs_0_.3, bf16[1024,1024]{1,0:T(8,128)(2,1)} %copy-done.35), custom_call_target="tpu_custom_call" | custom-call | flops 1000000 | bytes 10000 | tf_op jit(solution)/shard_map/qkv_rope/pallas_call | solution.py:36
  83.0 5.8 %qkv_rope.3.far_ref = bf16[384,2048]{1,0:T(8,128)(2,1)} custom-call(s32[1]{0:T(128)} %bitcast.8.ctx_ref, f32[32,4096]{1,0:T(8,128)} %get-tuple-element.446.cos_ref, f32[32,4096]{1,0:T(8,128)} %get-tuple-element.445.sin_ref, bf16[4,400,256]{2,1,0:T(8,128)(2,1)} %copy-done.32, bf16[256,1024]{1,0:T(8,128)(2,1)} %collective-permute-done.2.refs_0_.refs_2_, ...), custom_call_target="tpu_custom_call" | custom-call | flops 1000000 | bytes 10000 | tf_op jit(solution)/shard_map/qkv_rope/pallas_call | solution.py:36
  96.2 4.7 all-to-all-start.2
  100.9 66.0 %attention_forward.1 = (bf16[8,512,128]{2,1,0:T(8,128)(2,1)}, bf16[384,4096]{1,0:T(8,128)(2,1)}, bf16[128,4096]{1,0:T(8,128)(2,1)}, f32[8,4096]{1,0:T(8,128)}) custom-call(s32[1]{0:T(128)} %bitcast.130, s32[64]{0:T(128)} %reshape.514.meet_ref, s32[8]{0:T(128)} %copy-done.80, s32[1,4096]{1,0:T(1,128)} %subtract_select_fusion.rank_ref, ...), custom_call_target="tpu_custom_call" | custom-call | flops 60000002048 | bytes 10000 | tf_op jit(solution)/shard_map/attention_forward/pallas_call | solution.py:160
  168.2 3.6 all-to-all-start.3
  176.5 20.3 %all-to-all-done.3.att_ref = bf16[8,512,128]{2,1,0:T(8,128)(2,1)S(1)} async-done(((bf16[8,512,128]{2,1,0:T(8,128)(2,1)}), bf16[8,512,128]{2,1,0:T(8,128)(2,1)S(1)}, u32[]{:S(2)}, u32[]{:S(2)}) %all-to-all-start.3) | async-done | bytes 1048608 | tf_op jit(solution)/shard_map/all_to_all | solution.py:814
  198.4 3.0 out_proj.1
  205.4 15.6 %mlp.1 = (bf16[1024,2048]{1,0:T(8,128)(2,1)S(1)}, bf16[1024,2048]{1,0:T(8,128)(2,1)}, f32[512,1024]{1,0:T(8,128)S(1)}, bf16[512,1024]{1,0:T(8,128)(2,1)S(1)}) custom-call(bf16[512,1024]{1,0:T(8,128)(2,1)S(1)} %get-tuple-element.204.own_ref.own_n, bf16[512,1024]{1,0:T(8,128)(2,1)S(1)} %collective-permute-done.16.peer_ref.peer_n, ...), custom_call_target="tpu_custom_call" | custom-call | flops 1000000 | bytes 10000 | tf_op jit(solution)/shard_map/mlp/pallas_call | solution.py:36
  227.9 17.6 %heads.1 = (bf16[256,1024]{1,0:T(8,128)(2,1)}, bf16[256,1024]{1,0:T(8,128)(2,1)}, bf16[512,288]{1,0:T(8,128)(2,1)}, f32[512,1024]{1,0:T(8,128)}, bf16[512,1024]{...) custom-call(s32[1]{0:T(128)} %bitcast.13.tp_ref, f32[512,1024]{1,0:T(8,128)} %copy-done.16, ...), custom_call_target="tpu_custom_call" | custom-call | flops 2000000000 | bytes 8000000 | tf_op jit(solution)/shard_map/heads/pallas_call | solution.py:36
  249.6 16.6 %mlp_back.1 = (bf16[1024,2048]{1,0:T(8,128)(2,1)}, f32[1,2048]{1,0:T(1,128)}, f32[512,1024]{1,0:T(8,128)}, bf16[512,1024]{1,0:T(8,128)(2,1)}) custom-call(bf16[512,1024]{1,0:T(8,128)(2,1)} %get-tuple-element.226.own_ref.own_g, bf16[512,1024]{1,0:T(8,128)(2,1)} %copy-done.8, bf16[1024,2048]{1,0:T(8,128)(2,1)} %get-tuple-element.227.slope_ref, ...), custom_call_target="tpu_custom_call" | custom-call | flops 1000000 | bytes 10000 | tf_op jit(solution)/shard_map/mlp_back/pallas_call | solution.py:36
  272.6 8.7 %first_back.1 = (f32[512,1024]{1,0:T(8,128)}, bf16[512,1024]{1,0:T(8,128)(2,1)}, bf16[8,512,128]{2,1,0:T(8,128)(2,1)}, f32[8,1024]{1,0:T(8,128)}) custom-call(f32[512,1024]{1,0:T(8,128)} %get-tuple-element.225.second_ref, f32[512,1024]{1,0:T(8,128)} %get-tuple-element.236.own_ref, bf16[512,1024]{1,0:T(8,128)(2,1)} %collective-permute-done.25.recv_ref, ...), custom_call_target="tpu_custom_call" | custom-call | flops 1000000 | bytes 10000 | tf_op jit(solution)/shard_map/first_back/pallas_call | solution.py:36
  286.1 4.4 all-to-all-start.4
  294.2 15.0 %mlp_weights.1 = (bf16[4,368,512]{2,1,0:T(8,128)(2,1)S(1)}, bf16[4,368,512]{2,1,0:T(8,128)(2,1)S(1)}, bf16[4,368,512]{2,1,0:T(8,128)(2,1)S(1)}, bf16[4,368,512]{...) custom-call(s32[1]{0:T(128)} %bitcast.1.place_ref, bf16[512,1024]{1,0:T(8,128)(2,1)S(1)} %copy-done.11, ...), custom_call_target="tpu_custom_call" | custom-call | flops 1000000 | bytes 10000 | tf_op jit(solution)/shard_map/mlp_weights/pallas_call | solution.py:36
  317.2 5.3 all-to-all-start.5
  324.6 88.0 %attention_backward.1 = (bf16[8,384,512]{2,1,0:T(8,128)(2,1)}, f32[384,1]{1,0:T(8,128)}) custom-call(s32[1]{0:T(128)} %bitcast.131, s32[64]{0:T(128)} %reshape.514.meet_ref, s32[8]{0:T(128)} %copy-done.80, s32[1,4096]{1,0:T(1,128)} %subtract_select_fusion.rank_ref, bf16[384,4096]{1,0:T(8,128)(2,1)} %get-tuple-element.188.sorted_ref, ...), custom_call_target="tpu_custom_call" | custom-call | flops 89999998976 | bytes 10000 | tf_op jit(solution)/shard_map/attention_backward/pallas_call | solution.py:295
  415.6 4.6 all-to-all-start.6
  420.9 8.8 %qkv_weight.1 = bf16[4,400,256]{2,1,0:T(8,128)(2,1)} custom-call(s32[9]{0:T(128)} %pad_add_fusion.2.dest_ref, bf16[8,384,512]{2,1,0:T(8,128)(2,1)} %get-tuple-element.277.d_ref, f32[384,1]{1,0:T(8,128)} %get-tuple-element.278.bias_ref, bf16[1024,1024]{1,0:T(8,128)(2,1)} %refs_0_.3, bf16[1024,1024]{1,0:T(8,128)(2,1)} %copy-done.35, ...), custom_call_target="tpu_custom_call" | custom-call | flops 1000000 | bytes 10000 | tf_op jit(solution)/shard_map/qkv_weight/pallas_call | solution.py:36
  429.7 3.9 sums.1
  436.5 5.5 %collective-permute-start.36 = (bf16[368,512]{1,0:T(8,128)(2,1)}, bf16[368,512]{1,0:T(8,128)(2,1)S(1)}, u32[]{:S(2)}, u32[]{:S(2)}) collective-permute-start(bf16[368,512]{1,0:T(8,128)(2,1)} %get-tuple-element.428), channel_id=1, source_target_pairs={{0,8},{8,16},{16,24},{24,0},{1,9},{9,17},{17,25},{25,1},{2,10},{10... | collective-permute-start | bytes 1130504 | tf_op jit(solution)/shard_map/ppermute | solution.py:833
  447.5 15.2 %collective-permute-done.39.refs_5_ = bf16[128,1024]{1,0:T(8,128)(2,1)S(1)} collective-permute-done((bf16[128,1024]{1,0:T(8,128)(2,1)S(1)}, bf16[128,1024]{1,0:T(8,128)(2,1)S(1)}, u32[]{:S(2)}, u32[]{:S(2)}) %collective-permute-start.39) | collective-permute-done | bytes 262176 | tf_op jit(solution)/shard_map/ppermute | solution.py:806
  463.9 9.9 %input_grad.1 = bf16[512,1024]{1,0:T(8,128)(2,1)} custom-call(s32[1]{0:T(128)} %bitcast.22.dev_ref, f32[512,1024]{1,0:T(8,128)} %get-tuple-element.296.first_ref, bf16[8,384,512]{2,1,0:T(8,128)(2,1)} %all-to-all-done.6.d_ref, bf16[4,400,256]{2,1,0:T(8,128)(2,1)} %copy-done.32, bf16[4,400,256]{2,1,0:T(8,128)(2,1)} %collective-permute-done.18.refs_1_, ...), custom_call_target="tpu_custom_call" | custom-call | flops 1000000 | bytes 10000 | tf_op jit(solution)/shard_map/input_grad/pallas_call | solution.py:36
  483.3 7.4 %collective-permute-start.46 = (bf16[400,256]{1,0:T(8,128)(2,1)S(1)}, bf16[400,256]{1,0:T(8,128)(2,1)S(1)}, u32[]{:S(2)}, u32[]{:S(2)}) collective-permute-start(bf16[400,256]{1,0:T(8,128)(2,1)S(1)} %get-tuple-element.435), channel_id=1, source_target_pairs={{0,24},{8,0},{16,8},{24,16},{1,25},{9,1},{17,9},{25,17},{2,26},{10... | collective-permute-start | bytes 614408 | tf_op jit(solution)/shard_map/ppermute | solution.py:833
  495.8 4.2 all-to-all-start.7
  500.0 8.4 %collective-permute-done.45 = bf16[400,256]{1,0:T(8,128)(2,1)S(1)} collective-permute-done((bf16[400,256]{1,0:T(8,128)(2,1)S(1)}, bf16[400,256]{1,0:T(8,128)(2,1)S(1)}, u32[]{:S(2)}, u32[]{:S(2)}) %collective-permute-start.45) | collective-permute-done | bytes 204832 | tf_op jit(solution)/shard_map/ppermute | solution.py:833
  510.3 8.7 %collective-permute-done.48 = bf16[400,256]{1,0:T(8,128)(2,1)S(1)} collective-permute-done((bf16[400,256]{1,0:T(8,128)(2,1)S(1)}, bf16[400,256]{1,0:T(8,128)(2,1)S(1)}, u32[]{:S(2)}, u32[]{:S(2)}) %collective-permute-start.48) | collective-permute-done | bytes 204832 | tf_op jit(solution)/shard_map/ppermute | solution.py:802
  528.3 4.0 hidden_join.1
  (386 shorter events, 132.1 us)
Async XLA Ops:
  1.2 70.6 %collective-permute-start.11 = (bf16[1024,1024]{1,0:T(8,128)(2,1)}, bf16[1024,1024]{1,0:T(8,128)(2,1)S(1)}, u32[]{:S(2)}, u32[]{:S(2)}) collective-permute-start(bf16[1024,1024]{1,0:T(8,128)(2,1)} %refs_0_.3), channel_id=1, source_target_pairs={{0,2},{2,0},{1,3},{3,1},{4,6},{6,4},{5,7},{7,5},{8,10},{10,8},{9,1... | collective-permute-start | bytes 6291464 | tf_op jit(solution)/shard_map/ppermute | solution.py:798
  3.5 43.6 %collective-permute-start.2 = (bf16[256,1024]{1,0:T(8,128)(2,1)}, bf16[256,1024]{1,0:T(8,128)(2,1)}, u32[]{:S(2)}, u32[]{:S(2)}) collective-permute-start(bf16[256,1024]{1,0:T(8,128)(2,1)} %get-tuple-element.425), channel_id=1, source_target_pairs={{0,4},{4,0},{1,5},{5,1},{2,6},{6,2},{3,7},{7,3},{8,12},{12,8},{9,1... | collective-permute-start | bytes 1572872 | tf_op jit(solution)/shard_map/ppermute | solution.py:802
  6.4 41.3 %collective-permute-start.3 = (bf16[256,1024]{1,0:T(8,128)(2,1)}, bf16[256,1024]{1,0:T(8,128)(2,1)}, u32[]{:S(2)}, u32[]{:S(2)}) collective-permute-start(bf16[256,1024]{1,0:T(8,128)(2,1)} %get-tuple-element.424), channel_id=1, source_target_pairs={{0,4},{4,0},{1,5},{5,1},{2,6},{6,2},{3,7},{7,3},{8,12},{12,8},{9,1... | collective-permute-start | bytes 1572872 | tf_op jit(solution)/shard_map/ppermute | solution.py:802
  9.1 22.4 %collective-permute-start.10 = (bf16[512,512]{1,0:T(8,128)(2,1)}, bf16[512,512]{1,0:T(8,128)(2,1)}, u32[]{:S(2)}, u32[]{:S(2)}) collective-permute-start(bf16[512,512]{1,0:T(8,128)(2,1)} %get-tuple-element.174), channel_id=1, source_target_pairs={{0,1},{1,0},{2,3},{3,2},{4,5},{5,4},{6,7},{7,6},{8,9},{9,8},{10,11... | collective-permute-start | bytes 1572872 | tf_op jit(solution)/shard_map/ppermute | solution.py:806
  12.5 25.1 %all-to-all-start = ((bf16[4,400,256]{2,1,0:T(8,128)(2,1)}), bf16[4,400,256]{2,1,0:T(8,128)(2,1)S(1)}, u32[]{:S(2)}, u32[]{:S(2)}) async-start(bf16[4,400,256]{2,1,0:T(8,128)(2,1)} %broadcast_in_dim.83), calls=%async_computation | async-start | bytes 1638400 | tf_op jit(solution)/shard_map/all_to_all | solution.py:814
  39.1 52.2 %all-to-all-start.1 = ((bf16[4,512,512]{2,1,0:T(8,128)(2,1)}), bf16[4,512,512]{2,1,0:T(8,128)(2,1)}, u32[]{:S(2)}, u32[]{:S(2)}) async-start(bf16[4,512,512]{2,1,0:T(8,128)(2,1)} %broadcast_in_dim.124), calls=%async_computation.1 | async-start | bytes 4194304 | tf_op jit(solution)/shard_map/all_to_all | solution.py:814
  47.8 23.8 %collective-permute-start.5 = (bf16[256,1024]{1,0:T(8,128)(2,1)}, bf16[256,1024]{1,0:T(8,128)(2,1)S(1)}, u32[]{:S(2)}, u32[]{:S(2)}) collective-permute-start(bf16[256,1024]{1,0:T(8,128)(2,1)} %collective-permute-done.3.refs_1_.refs_3_), channel_id=1, source_target_pairs={{0,1},{1,0},{2,3},{3,2},{4,5},{5,4},{6,7},{7,6},{8,9},{9,8},{10,11... | collective-permute-start | bytes 1572872 | tf_op jit(solution)/shard_map/ppermute | solution.py:806
  49.9 29.0 %collective-permute-start.6 = (bf16[256,1024]{1,0:T(8,128)(2,1)}, bf16[256,1024]{1,0:T(8,128)(2,1)S(1)}, u32[]{:S(2)}, u32[]{:S(2)}) collective-permute-start(bf16[256,1024]{1,0:T(8,128)(2,1)} %collective-permute-done.2.refs_0_.refs_2_), channel_id=1, source_target_pairs={{0,2},{2,0},{1,3},{3,1},{4,6},{6,4},{5,7},{7,5},{8,10},{10,8},{9,1... | collective-permute-start | bytes 1572872 | tf_op jit(solution)/shard_map/ppermute | solution.py:798
  49.9 29.0 %collective-permute-start.7 = (bf16[256,1024]{1,0:T(8,128)(2,1)}, bf16[256,1024]{1,0:T(8,128)(2,1)S(1)}, u32[]{:S(2)}, u32[]{:S(2)}) collective-permute-start(bf16[256,1024]{1,0:T(8,128)(2,1)} %collective-permute-done.3.refs_1_.refs_3_), channel_id=1, source_target_pairs={{0,2},{2,0},{1,3},{3,1},{4,6},{6,4},{5,7},{7,5},{8,10},{10,8},{9,1... | collective-permute-start | bytes 1572872 | tf_op jit(solution)/shard_map/ppermute | solution.py:798
  92.7 74.2 %collective-permute-start.13 = (bf16[4,512,512]{2,1,0:T(8,128)(2,1)}, bf16[4,512,512]{2,1,0:T(8,128)(2,1)S(1)}, u32[]{:S(2)}, u32[]{:S(2)}) collective-permute-start(bf16[4,512,512]{2,1,0:T(8,128)(2,1)} %all-to-all-done.1.refs_0_), channel_id=1, source_target_pairs={{0,1},{1,0},{2,3},{3,2},{4,5},{5,4},{6,7},{7,6},{8,9},{9,8},{10,11... | collective-permute-start | bytes 6291464 | tf_op jit(solution)/shard_map/ppermute | solution.py:806
  93.2 73.7 %collective-permute-start.14 = (bf16[4,512,512]{2,1,0:T(8,128)(2,1)}, bf16[4,512,512]{2,1,0:T(8,128)(2,1)}, u32[]{:S(2)}, u32[]{:S(2)}) collective-permute-start(bf16[4,512,512]{2,1,0:T(8,128)(2,1)} %all-to-all-done.1.refs_0_), channel_id=1, source_target_pairs={{0,4},{4,0},{1,5},{5,1},{2,6},{6,2},{3,7},{7,3},{8,12},{12,8},{9,1... | collective-permute-start | bytes 6291464 | tf_op jit(solution)/shard_map/ppermute | solution.py:802
  94.7 108.1 %collective-permute-start.17 = (bf16[4,512,512]{2,1,0:T(8,128)(2,1)}, bf16[4,512,512]{2,1,0:T(8,128)(2,1)}, u32[]{:S(2)}, u32[]{:S(2)}) collective-permute-start(bf16[4,512,512]{2,1,0:T(8,128)(2,1)} %all-to-all-done.1.refs_0_), channel_id=1, source_target_pairs={{0,5},{1,4},{2,7},{3,6},{4,1},{5,0},{6,3},{7,2},{8,13},{9,12},{10,... | collective-permute-start | bytes 6291464 | tf_op jit(solution)/shard_map/ppermute | solution.py:794
  96.2 70.7 %all-to-all-start.2 = ((bf16[4,2,80,1312]{3,2,1,0:T(8,128)(2,1)}), bf16[4,2,80,1312]{3,2,1,0:T(8,128)(2,1)}, u32[]{:S(2)}, u32[]{:S(2)}) async-start(bf16[4,2,80,1312]{3,2,1,0:T(8,128)(2,1)} %broadcast_in_dim.125), calls=%async_computation.2 | async-start | bytes 3604480 | tf_op jit(solution)/shard_map/all_to_all | solution.py:814
  168.2 28.6 %all-to-all-start.3 = ((bf16[8,512,128]{2,1,0:T(8,128)(2,1)}), bf16[8,512,128]{2,1,0:T(8,128)(2,1)S(1)}, u32[]{:S(2)}, u32[]{:S(2)}) async-start(bf16[8,512,128]{2,1,0:T(8,128)(2,1)} %get-tuple-element.194), calls=%async_computation.3 | async-start | bytes 2097152 | tf_op jit(solution)/shard_map/all_to_all | solution.py:814
  202.8 21.4 %collective-permute-start.18 = (bf16[4,400,256]{2,1,0:T(8,128)(2,1)S(1)}, bf16[4,400,256]{2,1,0:T(8,128)(2,1)}, u32[]{:S(2)}, u32[]{:S(2)}) collective-permute-start(bf16[4,400,256]{2,1,0:T(8,128)(2,1)S(1)} %copy-done.33), channel_id=1, source_target_pairs={{0,1},{1,0},{2,3},{3,2},{4,5},{5,4},{6,7},{7,6},{8,9},{9,8},{10,11... | collective-permute-start | bytes 2457608 | tf_op jit(solution)/shard_map/ppermute | solution.py:806
  224.5 21.0 %collective-permute-start.21 = (bf16[2,400,256]{2,1,0:T(8,128)(2,1)S(1)}, bf16[2,400,256]{2,1,0:T(8,128)(2,1)S(1)}, u32[]{:S(2)}, u32[]{:S(2)}) collective-permute-start(bf16[2,400,256]{2,1,0:T(8,128)(2,1)S(1)} %get-tuple-element.224), channel_id=1, source_target_pairs={{0,5},{1,4},{2,7},{3,6},{4,1},{5,0},{6,3},{7,2},{8,13},{9,12},{10,... | collective-permute-start | bytes 1228808 | tf_op jit(solution)/shard_map/ppermute | solution.py:794
  245.6 23.2 %collective-permute-start.23 = (bf16[256,1024]{1,0:T(8,128)(2,1)}, bf16[256,1024]{1,0:T(8,128)(2,1)S(1)}, u32[]{:S(2)}, u32[]{:S(2)}) collective-permute-start(bf16[256,1024]{1,0:T(8,128)(2,1)} %get-tuple-element.306), channel_id=1, source_target_pairs={{0,1},{1,0},{2,3},{3,2},{4,5},{5,4},{6,7},{7,6},{8,9},{9,8},{10,11... | collective-permute-start | bytes 1572872 | tf_op jit(solution)/shard_map/ppermute | solution.py:806
  286.1 27.6 %all-to-all-start.4 = ((bf16[8,512,128]{2,1,0:T(8,128)(2,1)}), bf16[8,512,128]{2,1,0:T(8,128)(2,1)}, u32[]{:S(2)}, u32[]{:S(2)}) async-start(bf16[8,512,128]{2,1,0:T(8,128)(2,1)} %get-tuple-element.252), calls=%async_computation.4 | async-start | bytes 2097152 | tf_op jit(solution)/shard_map/all_to_all | solution.py:1019
  313.7 98.9 %collective-permute-start.31 = (bf16[4,368,512]{2,1,0:T(8,128)(2,1)}, bf16[4,368,512]{2,1,0:T(8,128)(2,1)S(1)}, u32[]{:S(2)}, u32[]{:S(2)}) collective-permute-start(bf16[4,368,512]{2,1,0:T(8,128)(2,1)} %copy-done.31), channel_id=1, source_target_pairs={{0,1},{1,0},{2,3},{3,2},{4,5},{5,4},{6,7},{7,6},{8,9},{9,8},{10,11... | collective-permute-start | bytes 4521992 | tf_op jit(solution)/shard_map/ppermute | solution.py:806
  315.6 97.0 %collective-permute-start.32 = (bf16[4,368,512]{2,1,0:T(8,128)(2,1)}, bf16[4,368,512]{2,1,0:T(8,128)(2,1)S(1)}, u32[]{:S(2)}, u32[]{:S(2)}) collective-permute-start(bf16[4,368,512]{2,1,0:T(8,128)(2,1)} %copy-done.30), channel_id=1, source_target_pairs={{0,4},{4,0},{1,5},{5,1},{2,6},{6,2},{3,7},{7,3},{8,12},{12,8},{9,1... | collective-permute-start | bytes 4521992 | tf_op jit(solution)/shard_map/ppermute | solution.py:802
  317.1 96.4 %collective-permute-start.33 = (bf16[4,368,512]{2,1,0:T(8,128)(2,1)}, bf16[4,368,512]{2,1,0:T(8,128)(2,1)}, u32[]{:S(2)}, u32[]{:S(2)}) collective-permute-start(bf16[4,368,512]{2,1,0:T(8,128)(2,1)} %copy-done.29), channel_id=1, source_target_pairs={{0,5},{1,4},{2,7},{3,6},{4,1},{5,0},{6,3},{7,2},{8,13},{9,12},{10,... | collective-permute-start | bytes 4521992 | tf_op jit(solution)/shard_map/ppermute | solution.py:794
  317.2 98.4 %all-to-all-start.5 = ((bf16[4,4,128,1024]{3,2,1,0:T(8,128)(2,1)}), bf16[4,4,128,1024]{3,2,1,0:T(8,128)(2,1)}, u32[]{:S(2)}, u32[]{:S(2)}) async-start(bf16[4,4,128,1024]{3,2,1,0:T(8,128)(2,1)} %get-tuple-element.271), calls=%async_computation.5 | async-start | bytes 8388608 | tf_op jit(solution)/shard_map/all_to_all | solution.py:814
  322.5 90.1 %collective-permute-start.34 = (bf16[256,1024]{1,0:T(8,128)(2,1)S(1)}, bf16[256,1024]{1,0:T(8,128)(2,1)S(1)}, u32[]{:S(2)}, u32[]{:S(2)}) collective-permute-start(bf16[256,1024]{1,0:T(8,128)(2,1)S(1)} %copy-done.57), channel_id=1, source_target_pairs={{0,1},{1,0},{2,3},{3,2},{4,5},{5,4},{6,7},{7,6},{8,9},{9,8},{10,11... | collective-permute-start | bytes 1572872 | tf_op jit(solution)/shard_map/ppermute | solution.py:806
  324.4 88.1 %collective-permute-start.35 = (bf16[512,288]{1,0:T(8,128)(2,1)}, bf16[512,288]{1,0:T(8,128)(2,1)S(1)}, u32[]{:S(2)}, u32[]{:S(2)}) collective-permute-start(bf16[512,288]{1,0:T(8,128)(2,1)} %get-tuple-element.310), channel_id=1, source_target_pairs={{0,1},{1,0},{2,3},{3,2},{4,5},{5,4},{6,7},{7,6},{8,9},{9,8},{10,11... | collective-permute-start | bytes 884744 | tf_op jit(solution)/shard_map/ppermute | solution.py:806
  415.6 48.3 %all-to-all-start.6 = ((bf16[8,384,512]{2,1,0:T(8,128)(2,1)}), bf16[8,384,512]{2,1,0:T(8,128)(2,1)}, u32[]{:S(2)}, u32[]{:S(2)}) async-start(bf16[8,384,512]{2,1,0:T(8,128)(2,1)} %get-tuple-element.277.d_ref), calls=%async_computation.6 | async-start | bytes 6291456 | tf_op jit(solution)/shard_map/all_to_all | solution.py:814
  433.6 29.1 %collective-permute-start.39 = (bf16[128,1024]{1,0:T(8,128)(2,1)S(1)}, bf16[128,1024]{1,0:T(8,128)(2,1)S(1)}, u32[]{:S(2)}, u32[]{:S(2)}) collective-permute-start(bf16[128,1024]{1,0:T(8,128)(2,1)S(1)} %get-tuple-element.291), channel_id=1, source_target_pairs={{0,1},{1,0},{2,3},{3,2},{4,5},{5,4},{6,7},{7,6},{8,9},{9,8},{10,11... | collective-permute-start | bytes 786440 | tf_op jit(solution)/shard_map/ppermute | solution.py:806
  436.5 39.0 %collective-permute-start.36 = (bf16[368,512]{1,0:T(8,128)(2,1)}, bf16[368,512]{1,0:T(8,128)(2,1)S(1)}, u32[]{:S(2)}, u32[]{:S(2)}) collective-permute-start(bf16[368,512]{1,0:T(8,128)(2,1)} %get-tuple-element.428), channel_id=1, source_target_pairs={{0,8},{8,16},{16,24},{24,0},{1,9},{9,17},{17,25},{25,1},{2,10},{10... | collective-permute-start | bytes 1130504 | tf_op jit(solution)/shard_map/ppermute | solution.py:833
  442.0 33.5 %collective-permute-start.37 = (bf16[368,512]{1,0:T(8,128)(2,1)S(1)}, bf16[368,512]{1,0:T(8,128)(2,1)S(1)}, u32[]{:S(2)}, u32[]{:S(2)}) collective-permute-start(bf16[368,512]{1,0:T(8,128)(2,1)S(1)} %get-tuple-element.427), channel_id=1, source_target_pairs={{0,16},{8,24},{16,0},{24,8},{1,17},{9,25},{17,1},{25,9},{2,18},{10... | collective-permute-start | bytes 1130504 | tf_op jit(solution)/shard_map/ppermute | solution.py:833
  444.4 31.1 %collective-permute-start.38 = (bf16[368,512]{1,0:T(8,128)(2,1)S(1)}, bf16[368,512]{1,0:T(8,128)(2,1)S(1)}, u32[]{:S(2)}, u32[]{:S(2)}) collective-permute-start(bf16[368,512]{1,0:T(8,128)(2,1)S(1)} %get-tuple-element.426), channel_id=1, source_target_pairs={{0,24},{8,0},{16,8},{24,16},{1,25},{9,1},{17,9},{25,17},{2,26},{10... | collective-permute-start | bytes 1130504 | tf_op jit(solution)/shard_map/ppermute | solution.py:833
  446.0 27.8 %collective-permute-start.40 = (bf16[128,1024]{1,0:T(8,128)(2,1)S(1)}, bf16[128,1024]{1,0:T(8,128)(2,1)}, u32[]{:S(2)}, u32[]{:S(2)}) collective-permute-start(bf16[128,1024]{1,0:T(8,128)(2,1)S(1)} %get-tuple-element.292), channel_id=1, source_target_pairs={{0,4},{4,0},{1,5},{5,1},{2,6},{6,2},{3,7},{7,3},{8,12},{12,8},{9,1... | collective-permute-start | bytes 786440 | tf_op jit(solution)/shard_map/ppermute | solution.py:802
  473.8 47.4 %collective-permute-start.43 = (bf16[512,1024]{1,0:T(8,128)(2,1)}, bf16[512,1024]{1,0:T(8,128)(2,1)}, u32[]{:S(2)}, u32[]{:S(2)}) collective-permute-start(bf16[512,1024]{1,0:T(8,128)(2,1)} %input_grad.1), channel_id=1, source_target_pairs={{0,1},{1,0},{2,3},{3,2},{4,5},{5,4},{6,7},{7,6},{8,9},{9,8},{10,11... | collective-permute-start | bytes 3145736 | tf_op jit(solution)/shard_map/ppermute | solution.py:806
  495.8 25.4 %all-to-all-start.7 = ((bf16[4,272,512]{2,1,0:T(8,128)(2,1)}), bf16[4,272,512]{2,1,0:T(8,128)(2,1)}, u32[]{:S(2)}, u32[]{:S(2)}) async-start(bf16[4,272,512]{2,1,0:T(8,128)(2,1)} %pad_maximum_fusion.2), calls=%async_computation.7 | async-start | bytes 2228224 | tf_op jit(solution)/shard_map/all_to_all | solution.py:814
  (113 other events, 873.2 us)

commit v5 on v4

--- a/solution.py
+++ b/solution.py
@@ -11,7 +11,7 @@
 HEAD_DIM = 64
 VMEM_CAP = 56 * 1024 * 1024
 MASKED = -1e30
-SMALL_GRANT = ("mlp", "mlp_weights", "out_proj", "sums", "out_weight", "dense_natural")
+SMALL_GRANT = ("mlp", "mlp_weights", "out_proj", "sums", "out_weight", "dense_natural", "hidden_join", "hidden_split", "dense_half", "pick")
 SPARE = 14
 TS = 256
 FQ, FK = 1024, 512

time: 539 us -> 536 us (level)
  waiting for transfers between devices: 94.1 us -> 102 us
  starting transfers between devices: 91.4 us -> 83.8 us
  local copies, waits for them, and re-layouts: 54.2 us -> 48.8 us
    ppermute x6, starting transfers between devices: 17 us -> 9.96 us  [send_z(): lax.ppermute(value[s], 'fsdp', [(i, (i + s) % size) for i in range(size)])]
    pallas_call x17, Pallas kernels: 126 us -> 119 us  [call(): pl.pallas_call(kernel, out_shape=out_shape, in_specs=[sm] * scalars + [vm...]
    ppermute x13, waiting for transfers between devices: 40 us -> 46.8 us  [hop_y(): return lax.ppermute(value, 'tp', [(0, 1), (1, 0)])]
    pallas_call x1, Pallas kernels: 88 us -> 93.8 us  [attention_backward(): pl.pallas_call(backward_kernel, out_shape=(jax.ShapeDtypeStruct((8, 384,...]
    unnamed x176 -> x156, local copies, waits for them, and re-layouts: 30.5 us -> 26.7 us
  transfers between devices with their start and end apart: 63 -> 63, of which waited for: 16 -> 16; matrix products, arithmetic and copies ran while one was open for 7% -> 7% of each run, Pallas kernels for 51% -> 52%
where the time goes in v5:
time: 536 us; the launch traced here: 531 us
  Pallas kernels  280 us (52%)
  waiting for transfers between devices  102 us (19%)
  starting transfers between devices  83.8 us (16%)
  local copies, waits for them, and re-layouts  48.8 us (9%)
  other arithmetic  13.6 us (3%)
    pallas_call x17, Pallas kernels, call(): pl.pallas_call(kernel, out_shape=out_shape, in_specs=[sm] * scalars + [vm...  119 us
    pallas_call x1, Pallas kernels, attention_backward(): pl.pallas_call(backward_kernel, out_shape=(jax.ShapeDtypeStruct((8, 384,...  93.8 us
    pallas_call x1, Pallas kernels, attention_forward(): pl.pallas_call(forward_kernel, out_shape=(jax.ShapeDtypeStruct((8, rows /...  67.9 us
    ppermute x13, waiting for transfers between devices, hop_y(): return lax.ppermute(value, 'tp', [(0, 1), (1, 0)])  46.8 us
    all_to_all x7, starting transfers between devices, trade(): return lax.all_to_all(value, axes, 0, 0, tiled=True)  31.3 us
    all_to_all x7, waiting for transfers between devices, trade(): return lax.all_to_all(value, axes, 0, 0, tiled=True)  27.3 us
    unnamed x156, local copies, waits for them, and re-layouts  26.7 us
    ppermute x13, starting transfers between devices, hop_y(): return lax.ppermute(value, 'tp', [(0, 1), (1, 0)])  14.8 us
  transfers between devices with their start and end apart: 63, of which 16 were waited for; matrix products, arithmetic and copies ran while one was open for 7% of the time, Pallas kernels for 52%

profile of v5, /device:TPU:0, one launch (start us, length us, event | category | flops | bytes accessed | tf_op | source)
XLA Modules:
  0.0 531.3 jit_solution(8205704201908785520)
XLA Ops:
  10.9 4.9 all-to-all-start
  19.0 11.2 %collective-permute-done.1 = s32[2,1024]{1,0:T(2,128)S(1)} collective-permute-done((s32[2,1024]{1,0:T(2,128)S(1)}, s32[2,1024]{1,0:T(2,128)S(1)}, u32[]{:S(2)}, u32[]{:S(2)}) %collective-permute-start.1) | collective-permute-done | bytes 8224 | tf_op jit(solution)/shard_map/ppermute | solution.py:802
  31.7 4.2 all-to-all-done.w_ref.refs_0_
  37.5 4.5 all-to-all-start.1
  48.8 11.9 %collective-permute-done.4.refs_2_.refs_4_ = bf16[256,1024]{1,0:T(8,128)(2,1)S(1)} collective-permute-done((bf16[256,1024]{1,0:T(8,128)(2,1)}, bf16[256,1024]{1,0:T(8,128)(2,1)S(1)}, u32[]{:S(2)}, u32[]{:S(2)}) %collective-permute-start.4) | collective-permute-done | bytes 524320 | tf_op jit(solution)/shard_map/ppermute | solution.py:806
  60.7 9.2 %collective-permute-done.5.refs_3_.refs_5_ = bf16[256,1024]{1,0:T(8,128)(2,1)S(1)} collective-permute-done((bf16[256,1024]{1,0:T(8,128)(2,1)}, bf16[256,1024]{1,0:T(8,128)(2,1)S(1)}, u32[]{:S(2)}, u32[]{:S(2)}) %collective-permute-start.5) | collective-permute-done | bytes 524320 | tf_op jit(solution)/shard_map/ppermute | solution.py:806
  70.1 5.9 %qkv_rope.2.near_ref = bf16[384,2048]{1,0:T(8,128)(2,1)} custom-call(s32[1]{0:T(128)} %bitcast.8.ctx_ref, f32[32,4096]{1,0:T(8,128)} %get-tuple-element.446.cos_ref, f32[32,4096]{1,0:T(8,128)} %get-tuple-element.445.sin_ref, bf16[4,400,256]{2,1,0:T(8,128)(2,1)} %copy-done.34, bf16[1024,1024]{1,0:T(8,128)(2,1)} %refs_0_.3, ...), custom_call_target="tpu_custom_call" | custom-call | flops 1000000 | bytes 10000 | tf_op jit(solution)/shard_map/qkv_rope/pallas_call | solution.py:36
  78.3 5.7 %qkv_rope.3.far_ref = bf16[384,2048]{1,0:T(8,128)(2,1)} custom-call(s32[1]{0:T(128)} %bitcast.8.ctx_ref, f32[32,4096]{1,0:T(8,128)} %get-tuple-element.446.cos_ref, f32[32,4096]{1,0:T(8,128)} %get-tuple-element.445.sin_ref, bf16[4,400,256]{2,1,0:T(8,128)(2,1)} %copy-done.34, bf16[256,1024]{1,0:T(8,128)(2,1)} %collective-permute-done.2.refs_0_.refs_2_, ...), custom_call_target="tpu_custom_call" | custom-call | flops 1000000 | bytes 10000 | tf_op jit(solution)/shard_map/qkv_rope/pallas_call | solution.py:36
  85.0 4.7 all-to-all-done.1.refs_0_
  94.5 4.7 all-to-all-start.2
  99.2 67.9 %attention_forward.1 = (bf16[8,512,128]{2,1,0:T(8,128)(2,1)}, bf16[384,4096]{1,0:T(8,128)(2,1)}, bf16[128,4096]{1,0:T(8,128)(2,1)}, f32[8,4096]{1,0:T(8,128)}) custom-call(s32[1]{0:T(128)} %bitcast.130, s32[64]{0:T(128)} %reshape.514.meet_ref, s32[8]{0:T(128)} %copy-done.70, s32[1,4096]{1,0:T(1,128)} %subtract_select_fusion.rank_ref, ...), custom_call_target="tpu_custom_call" | custom-call | flops 60000002048 | bytes 10000 | tf_op jit(solution)/shard_map/attention_forward/pallas_call | solution.py:160
  168.4 3.6 all-to-all-start.3
  176.7 18.4 %all-to-all-done.3.att_ref = bf16[8,512,128]{2,1,0:T(8,128)(2,1)S(1)} async-done(((bf16[8,512,128]{2,1,0:T(8,128)(2,1)}), bf16[8,512,128]{2,1,0:T(8,128)(2,1)S(1)}, u32[]{:S(2)}, u32[]{:S(2)}) %all-to-all-start.3) | async-done | bytes 1048608 | tf_op jit(solution)/shard_map/all_to_all | solution.py:814
  203.7 15.6 %mlp.1 = (bf16[1024,2048]{1,0:T(8,128)(2,1)S(1)}, bf16[1024,2048]{1,0:T(8,128)(2,1)}, f32[512,1024]{1,0:T(8,128)S(1)}, bf16[512,1024]{1,0:T(8,128)(2,1)S(1)}) custom-call(bf16[512,1024]{1,0:T(8,128)(2,1)S(1)} %get-tuple-element.204.own_ref.own_n, bf16[512,1024]{1,0:T(8,128)(2,1)S(1)} %collective-permute-done.16.peer_ref.peer_n, ...), custom_call_target="tpu_custom_call" | custom-call | flops 1000000 | bytes 10000 | tf_op jit(solution)/shard_map/mlp/pallas_call | solution.py:36
  226.4 17.6 %heads.1 = (bf16[256,1024]{1,0:T(8,128)(2,1)}, bf16[256,1024]{1,0:T(8,128)(2,1)}, bf16[512,288]{1,0:T(8,128)(2,1)}, f32[512,1024]{1,0:T(8,128)}, bf16[512,1024]{...) custom-call(s32[1]{0:T(128)} %bitcast.13.tp_ref, f32[512,1024]{1,0:T(8,128)} %copy-done.16, ...), custom_call_target="tpu_custom_call" | custom-call | flops 2000000000 | bytes 8000000 | tf_op jit(solution)/shard_map/heads/pallas_call | solution.py:36
  248.1 16.6 %mlp_back.1 = (bf16[1024,2048]{1,0:T(8,128)(2,1)}, f32[1,2048]{1,0:T(1,128)}, f32[512,1024]{1,0:T(8,128)}, bf16[512,1024]{1,0:T(8,128)(2,1)}) custom-call(bf16[512,1024]{1,0:T(8,128)(2,1)} %get-tuple-element.226.own_ref.own_g, bf16[512,1024]{1,0:T(8,128)(2,1)} %copy-done.8, bf16[1024,2048]{1,0:T(8,128)(2,1)} %get-tuple-element.227.slope_ref, ...), custom_call_target="tpu_custom_call" | custom-call | flops 1000000 | bytes 10000 | tf_op jit(solution)/shard_map/mlp_back/pallas_call | solution.py:36
  271.1 8.7 %first_back.1 = (f32[512,1024]{1,0:T(8,128)}, bf16[512,1024]{1,0:T(8,128)(2,1)}, bf16[8,512,128]{2,1,0:T(8,128)(2,1)}, f32[8,1024]{1,0:T(8,128)}) custom-call(f32[512,1024]{1,0:T(8,128)} %get-tuple-element.225.second_ref, f32[512,1024]{1,0:T(8,128)} %get-tuple-element.236.own_ref, bf16[512,1024]{1,0:T(8,128)(2,1)} %collective-permute-done.25.recv_ref, ...), custom_call_target="tpu_custom_call" | custom-call | flops 1000000 | bytes 10000 | tf_op jit(solution)/shard_map/first_back/pallas_call | solution.py:36
  284.7 4.4 all-to-all-start.4
  292.8 14.9 %mlp_weights.1 = (bf16[4,368,512]{2,1,0:T(8,128)(2,1)S(1)}, bf16[4,368,512]{2,1,0:T(8,128)(2,1)S(1)}, bf16[4,368,512]{2,1,0:T(8,128)(2,1)S(1)}, bf16[4,368,512]{...) custom-call(s32[1]{0:T(128)} %bitcast.1.place_ref, bf16[512,1024]{1,0:T(8,128)(2,1)S(1)} %copy-done.11, ...), custom_call_target="tpu_custom_call" | custom-call | flops 1000000 | bytes 10000 | tf_op jit(solution)/shard_map/mlp_weights/pallas_call | solution.py:36
  315.6 5.3 all-to-all-start.5
  323.0 93.8 %attention_backward.1 = (bf16[8,384,512]{2,1,0:T(8,128)(2,1)}, f32[384,1]{1,0:T(8,128)}) custom-call(s32[1]{0:T(128)} %bitcast.131, s32[64]{0:T(128)} %reshape.514.meet_ref, s32[8]{0:T(128)} %copy-done.70, s32[1,4096]{1,0:T(1,128)} %subtract_select_fusion.rank_ref, bf16[384,4096]{1,0:T(8,128)(2,1)} %get-tuple-element.188.sorted_ref, ...), custom_call_target="tpu_custom_call" | custom-call | flops 89999998976 | bytes 10000 | tf_op jit(solution)/shard_map/attention_backward/pallas_call | solution.py:295
  417.7 4.6 all-to-all-start.6
  423.0 8.8 %qkv_weight.1 = bf16[4,400,256]{2,1,0:T(8,128)(2,1)} custom-call(s32[9]{0:T(128)} %pad_add_fusion.2.dest_ref, bf16[8,384,512]{2,1,0:T(8,128)(2,1)} %get-tuple-element.277.d_ref, f32[384,1]{1,0:T(8,128)} %get-tuple-element.278.bias_ref, bf16[1024,1024]{1,0:T(8,128)(2,1)} %refs_0_.3, bf16[1024,1024]{1,0:T(8,128)(2,1)} %collective-permute-done.11.refs_1_, ...), custom_call_target="tpu_custom_call" | custom-call | flops 1000000 | bytes 10000 | tf_op jit(solution)/shard_map/qkv_weight/pallas_call | solution.py:36
  431.8 4.2 sums.1
  440.2 3.0 collective-permute-start.37
  446.3 18.5 %collective-permute-done.39.refs_5_ = bf16[128,1024]{1,0:T(8,128)(2,1)S(1)} collective-permute-done((bf16[128,1024]{1,0:T(8,128)(2,1)S(1)}, bf16[128,1024]{1,0:T(8,128)(2,1)S(1)}, u32[]{:S(2)}, u32[]{:S(2)}) %collective-permute-start.39) | collective-permute-done | bytes 262176 | tf_op jit(solution)/shard_map/ppermute | solution.py:806
  466.1 9.9 %input_grad.1 = bf16[512,1024]{1,0:T(8,128)(2,1)} custom-call(s32[1]{0:T(128)} %bitcast.22.dev_ref, f32[512,1024]{1,0:T(8,128)} %get-tuple-element.296.first_ref, bf16[8,384,512]{2,1,0:T(8,128)(2,1)} %all-to-all-done.6.d_ref, bf16[4,400,256]{2,1,0:T(8,128)(2,1)} %copy-done.34, bf16[4,400,256]{2,1,0:T(8,128)(2,1)} %collective-permute-done.18.refs_1_, ...), custom_call_target="tpu_custom_call" | custom-call | flops 1000000 | bytes 10000 | tf_op jit(solution)/shard_map/input_grad/pallas_call | solution.py:36
  482.1 3.9 collective-permute-start.46
  491.0 3.8 all-to-all-start.7
  494.8 8.9 %collective-permute-done.45 = bf16[400,256]{1,0:T(8,128)(2,1)} collective-permute-done((bf16[400,256]{1,0:T(8,128)(2,1)S(1)}, bf16[400,256]{1,0:T(8,128)(2,1)}, u32[]{:S(2)}, u32[]{:S(2)}) %collective-permute-start.45) | collective-permute-done | bytes 204832 | tf_op jit(solution)/shard_map/ppermute | solution.py:833
  506.6 3.7 collective-permute-done.53
  510.4 3.1 collective-permute-done.48
  (366 shorter events, 123.4 us)
Async XLA Ops:
  1.2 68.9 %collective-permute-start.11 = (bf16[1024,1024]{1,0:T(8,128)(2,1)}, bf16[1024,1024]{1,0:T(8,128)(2,1)}, u32[]{:S(2)}, u32[]{:S(2)}) collective-permute-start(bf16[1024,1024]{1,0:T(8,128)(2,1)} %refs_0_.3), channel_id=1, source_target_pairs={{0,2},{2,0},{1,3},{3,1},{4,6},{6,4},{5,7},{7,5},{8,10},{10,8},{9,1... | collective-permute-start | bytes 6291464 | tf_op jit(solution)/shard_map/ppermute | solution.py:798
  3.6 41.9 %collective-permute-start.2 = (bf16[256,1024]{1,0:T(8,128)(2,1)}, bf16[256,1024]{1,0:T(8,128)(2,1)}, u32[]{:S(2)}, u32[]{:S(2)}) collective-permute-start(bf16[256,1024]{1,0:T(8,128)(2,1)} %get-tuple-element.425), channel_id=1, source_target_pairs={{0,4},{4,0},{1,5},{5,1},{2,6},{6,2},{3,7},{7,3},{8,12},{12,8},{9,1... | collective-permute-start | bytes 1572872 | tf_op jit(solution)/shard_map/ppermute | solution.py:802
  6.6 39.5 %collective-permute-start.3 = (bf16[256,1024]{1,0:T(8,128)(2,1)}, bf16[256,1024]{1,0:T(8,128)(2,1)}, u32[]{:S(2)}, u32[]{:S(2)}) collective-permute-start(bf16[256,1024]{1,0:T(8,128)(2,1)} %get-tuple-element.424), channel_id=1, source_target_pairs={{0,4},{4,0},{1,5},{5,1},{2,6},{6,2},{3,7},{7,3},{8,12},{12,8},{9,1... | collective-permute-start | bytes 1572872 | tf_op jit(solution)/shard_map/ppermute | solution.py:802
  7.6 24.1 %collective-permute-start.10 = (bf16[512,512]{1,0:T(8,128)(2,1)}, bf16[512,512]{1,0:T(8,128)(2,1)}, u32[]{:S(2)}, u32[]{:S(2)}) collective-permute-start(bf16[512,512]{1,0:T(8,128)(2,1)} %get-tuple-element.174), channel_id=1, source_target_pairs={{0,1},{1,0},{2,3},{3,2},{4,5},{5,4},{6,7},{7,6},{8,9},{9,8},{10,11... | collective-permute-start | bytes 1572872 | tf_op jit(solution)/shard_map/ppermute | solution.py:806
  10.9 25.0 %all-to-all-start = ((bf16[4,400,256]{2,1,0:T(8,128)(2,1)}), bf16[4,400,256]{2,1,0:T(8,128)(2,1)S(1)}, u32[]{:S(2)}, u32[]{:S(2)}) async-start(bf16[4,400,256]{2,1,0:T(8,128)(2,1)} %broadcast_in_dim.83), calls=%async_computation | async-start | bytes 1638400 | tf_op jit(solution)/shard_map/all_to_all | solution.py:814
  37.5 52.2 %all-to-all-start.1 = ((bf16[4,512,512]{2,1,0:T(8,128)(2,1)}), bf16[4,512,512]{2,1,0:T(8,128)(2,1)}, u32[]{:S(2)}, u32[]{:S(2)}) async-start(bf16[4,512,512]{2,1,0:T(8,128)(2,1)} %broadcast_in_dim.124), calls=%async_computation.1 | async-start | bytes 4194304 | tf_op jit(solution)/shard_map/all_to_all | solution.py:814
  46.1 23.8 %collective-permute-start.5 = (bf16[256,1024]{1,0:T(8,128)(2,1)}, bf16[256,1024]{1,0:T(8,128)(2,1)S(1)}, u32[]{:S(2)}, u32[]{:S(2)}) collective-permute-start(bf16[256,1024]{1,0:T(8,128)(2,1)} %collective-permute-done.3.refs_1_.refs_3_), channel_id=1, source_target_pairs={{0,1},{1,0},{2,3},{3,2},{4,5},{5,4},{6,7},{7,6},{8,9},{9,8},{10,11... | collective-permute-start | bytes 1572872 | tf_op jit(solution)/shard_map/ppermute | solution.py:806
  48.3 27.7 %collective-permute-start.6 = (bf16[256,1024]{1,0:T(8,128)(2,1)}, bf16[256,1024]{1,0:T(8,128)(2,1)S(1)}, u32[]{:S(2)}, u32[]{:S(2)}) collective-permute-start(bf16[256,1024]{1,0:T(8,128)(2,1)} %collective-permute-done.2.refs_0_.refs_2_), channel_id=1, source_target_pairs={{0,2},{2,0},{1,3},{3,1},{4,6},{6,4},{5,7},{7,5},{8,10},{10,8},{9,1... | collective-permute-start | bytes 1572872 | tf_op jit(solution)/shard_map/ppermute | solution.py:798
  48.3 27.7 %collective-permute-start.7 = (bf16[256,1024]{1,0:T(8,128)(2,1)}, bf16[256,1024]{1,0:T(8,128)(2,1)S(1)}, u32[]{:S(2)}, u32[]{:S(2)}) collective-permute-start(bf16[256,1024]{1,0:T(8,128)(2,1)} %collective-permute-done.3.refs_1_.refs_3_), channel_id=1, source_target_pairs={{0,2},{2,0},{1,3},{3,1},{4,6},{6,4},{5,7},{7,5},{8,10},{10,8},{9,1... | collective-permute-start | bytes 1572872 | tf_op jit(solution)/shard_map/ppermute | solution.py:798
  91.0 76.1 %collective-permute-start.13 = (bf16[4,512,512]{2,1,0:T(8,128)(2,1)}, bf16[4,512,512]{2,1,0:T(8,128)(2,1)S(1)}, u32[]{:S(2)}, u32[]{:S(2)}) collective-permute-start(bf16[4,512,512]{2,1,0:T(8,128)(2,1)} %all-to-all-done.1.refs_0_), channel_id=1, source_target_pairs={{0,1},{1,0},{2,3},{3,2},{4,5},{5,4},{6,7},{7,6},{8,9},{9,8},{10,11... | collective-permute-start | bytes 6291464 | tf_op jit(solution)/shard_map/ppermute | solution.py:806
  91.6 75.6 %collective-permute-start.14 = (bf16[4,512,512]{2,1,0:T(8,128)(2,1)}, bf16[4,512,512]{2,1,0:T(8,128)(2,1)}, u32[]{:S(2)}, u32[]{:S(2)}) collective-permute-start(bf16[4,512,512]{2,1,0:T(8,128)(2,1)} %all-to-all-done.1.refs_0_), channel_id=1, source_target_pairs={{0,4},{4,0},{1,5},{5,1},{2,6},{6,2},{3,7},{7,3},{8,12},{12,8},{9,1... | collective-permute-start | bytes 6291464 | tf_op jit(solution)/shard_map/ppermute | solution.py:802
  93.1 108.1 %collective-permute-start.17 = (bf16[4,512,512]{2,1,0:T(8,128)(2,1)}, bf16[4,512,512]{2,1,0:T(8,128)(2,1)}, u32[]{:S(2)}, u32[]{:S(2)}) collective-permute-start(bf16[4,512,512]{2,1,0:T(8,128)(2,1)} %all-to-all-done.1.refs_0_), channel_id=1, source_target_pairs={{0,5},{1,4},{2,7},{3,6},{4,1},{5,0},{6,3},{7,2},{8,13},{9,12},{10,... | collective-permute-start | bytes 6291464 | tf_op jit(solution)/shard_map/ppermute | solution.py:794
  94.5 72.6 %all-to-all-start.2 = ((bf16[4,2,80,1312]{3,2,1,0:T(8,128)(2,1)}), bf16[4,2,80,1312]{3,2,1,0:T(8,128)(2,1)}, u32[]{:S(2)}, u32[]{:S(2)}) async-start(bf16[4,2,80,1312]{3,2,1,0:T(8,128)(2,1)} %broadcast_in_dim.125), calls=%async_computation.2 | async-start | bytes 3604480 | tf_op jit(solution)/shard_map/all_to_all | solution.py:814
  168.4 26.7 %all-to-all-start.3 = ((bf16[8,512,128]{2,1,0:T(8,128)(2,1)}), bf16[8,512,128]{2,1,0:T(8,128)(2,1)S(1)}, u32[]{:S(2)}, u32[]{:S(2)}) async-start(bf16[8,512,128]{2,1,0:T(8,128)(2,1)} %get-tuple-element.194), calls=%async_computation.3 | async-start | bytes 2097152 | tf_op jit(solution)/shard_map/all_to_all | solution.py:814
  201.2 21.5 %collective-permute-start.18 = (bf16[4,400,256]{2,1,0:T(8,128)(2,1)S(1)}, bf16[4,400,256]{2,1,0:T(8,128)(2,1)}, u32[]{:S(2)}, u32[]{:S(2)}) collective-permute-start(bf16[4,400,256]{2,1,0:T(8,128)(2,1)S(1)} %copy-done.35), channel_id=1, source_target_pairs={{0,1},{1,0},{2,3},{3,2},{4,5},{5,4},{6,7},{7,6},{8,9},{9,8},{10,11... | collective-permute-start | bytes 2457608 | tf_op jit(solution)/shard_map/ppermute | solution.py:806
  222.9 21.0 %collective-permute-start.21 = (bf16[2,400,256]{2,1,0:T(8,128)(2,1)S(1)}, bf16[2,400,256]{2,1,0:T(8,128)(2,1)S(1)}, u32[]{:S(2)}, u32[]{:S(2)}) collective-permute-start(bf16[2,400,256]{2,1,0:T(8,128)(2,1)S(1)} %get-tuple-element.224), channel_id=1, source_target_pairs={{0,5},{1,4},{2,7},{3,6},{4,1},{5,0},{6,3},{7,2},{8,13},{9,12},{10,... | collective-permute-start | bytes 1228808 | tf_op jit(solution)/shard_map/ppermute | solution.py:794
  244.2 23.2 %collective-permute-start.23 = (bf16[256,1024]{1,0:T(8,128)(2,1)}, bf16[256,1024]{1,0:T(8,128)(2,1)S(1)}, u32[]{:S(2)}, u32[]{:S(2)}) collective-permute-start(bf16[256,1024]{1,0:T(8,128)(2,1)} %get-tuple-element.306), channel_id=1, source_target_pairs={{0,1},{1,0},{2,3},{3,2},{4,5},{5,4},{6,7},{7,6},{8,9},{9,8},{10,11... | collective-permute-start | bytes 1572872 | tf_op jit(solution)/shard_map/ppermute | solution.py:806
  284.7 27.4 %all-to-all-start.4 = ((bf16[8,512,128]{2,1,0:T(8,128)(2,1)}), bf16[8,512,128]{2,1,0:T(8,128)(2,1)}, u32[]{:S(2)}, u32[]{:S(2)}) async-start(bf16[8,512,128]{2,1,0:T(8,128)(2,1)} %get-tuple-element.252), calls=%async_computation.4 | async-start | bytes 2097152 | tf_op jit(solution)/shard_map/all_to_all | solution.py:1019
  312.1 104.7 %collective-permute-start.31 = (bf16[4,368,512]{2,1,0:T(8,128)(2,1)}, bf16[4,368,512]{2,1,0:T(8,128)(2,1)S(1)}, u32[]{:S(2)}, u32[]{:S(2)}) collective-permute-start(bf16[4,368,512]{2,1,0:T(8,128)(2,1)} %copy-done.33), channel_id=1, source_target_pairs={{0,1},{1,0},{2,3},{3,2},{4,5},{5,4},{6,7},{7,6},{8,9},{9,8},{10,11... | collective-permute-start | bytes 4521992 | tf_op jit(solution)/shard_map/ppermute | solution.py:806
  314.0 102.8 %collective-permute-start.32 = (bf16[4,368,512]{2,1,0:T(8,128)(2,1)}, bf16[4,368,512]{2,1,0:T(8,128)(2,1)S(1)}, u32[]{:S(2)}, u32[]{:S(2)}) collective-permute-start(bf16[4,368,512]{2,1,0:T(8,128)(2,1)} %copy-done.32), channel_id=1, source_target_pairs={{0,4},{4,0},{1,5},{5,1},{2,6},{6,2},{3,7},{7,3},{8,12},{12,8},{9,1... | collective-permute-start | bytes 4521992 | tf_op jit(solution)/shard_map/ppermute | solution.py:802
  315.5 102.2 %collective-permute-start.33 = (bf16[4,368,512]{2,1,0:T(8,128)(2,1)}, bf16[4,368,512]{2,1,0:T(8,128)(2,1)}, u32[]{:S(2)}, u32[]{:S(2)}) collective-permute-start(bf16[4,368,512]{2,1,0:T(8,128)(2,1)} %copy-done.31), channel_id=1, source_target_pairs={{0,5},{1,4},{2,7},{3,6},{4,1},{5,0},{6,3},{7,2},{8,13},{9,12},{10,... | collective-permute-start | bytes 4521992 | tf_op jit(solution)/shard_map/ppermute | solution.py:794
  315.6 102.1 %all-to-all-start.5 = ((bf16[4,4,128,1024]{3,2,1,0:T(8,128)(2,1)}), bf16[4,4,128,1024]{3,2,1,0:T(8,128)(2,1)}, u32[]{:S(2)}, u32[]{:S(2)}) async-start(bf16[4,4,128,1024]{3,2,1,0:T(8,128)(2,1)} %get-tuple-element.271), calls=%async_computation.5 | async-start | bytes 8388608 | tf_op jit(solution)/shard_map/all_to_all | solution.py:814
  320.9 95.9 %collective-permute-start.34 = (bf16[256,1024]{1,0:T(8,128)(2,1)S(1)}, bf16[256,1024]{1,0:T(8,128)(2,1)S(1)}, u32[]{:S(2)}, u32[]{:S(2)}) collective-permute-start(bf16[256,1024]{1,0:T(8,128)(2,1)S(1)} %copy-done.53), channel_id=1, source_target_pairs={{0,1},{1,0},{2,3},{3,2},{4,5},{5,4},{6,7},{7,6},{8,9},{9,8},{10,11... | collective-permute-start | bytes 1572872 | tf_op jit(solution)/shard_map/ppermute | solution.py:806
  322.9 93.9 %collective-permute-start.35 = (bf16[512,288]{1,0:T(8,128)(2,1)}, bf16[512,288]{1,0:T(8,128)(2,1)S(1)}, u32[]{:S(2)}, u32[]{:S(2)}) collective-permute-start(bf16[512,288]{1,0:T(8,128)(2,1)} %get-tuple-element.310), channel_id=1, source_target_pairs={{0,1},{1,0},{2,3},{3,2},{4,5},{5,4},{6,7},{7,6},{8,9},{9,8},{10,11... | collective-permute-start | bytes 884744 | tf_op jit(solution)/shard_map/ppermute | solution.py:806
  417.7 48.3 %all-to-all-start.6 = ((bf16[8,384,512]{2,1,0:T(8,128)(2,1)}), bf16[8,384,512]{2,1,0:T(8,128)(2,1)}, u32[]{:S(2)}, u32[]{:S(2)}) async-start(bf16[8,384,512]{2,1,0:T(8,128)(2,1)} %get-tuple-element.277.d_ref), calls=%async_computation.6 | async-start | bytes 6291456 | tf_op jit(solution)/shard_map/all_to_all | solution.py:814
  436.0 28.8 %collective-permute-start.39 = (bf16[128,1024]{1,0:T(8,128)(2,1)S(1)}, bf16[128,1024]{1,0:T(8,128)(2,1)S(1)}, u32[]{:S(2)}, u32[]{:S(2)}) collective-permute-start(bf16[128,1024]{1,0:T(8,128)(2,1)S(1)} %get-tuple-element.291), channel_id=1, source_target_pairs={{0,1},{1,0},{2,3},{3,2},{4,5},{5,4},{6,7},{7,6},{8,9},{9,8},{10,11... | collective-permute-start | bytes 786440 | tf_op jit(solution)/shard_map/ppermute | solution.py:806
  438.9 38.8 %collective-permute-start.36 = (bf16[368,512]{1,0:T(8,128)(2,1)}, bf16[368,512]{1,0:T(8,128)(2,1)S(1)}, u32[]{:S(2)}, u32[]{:S(2)}) collective-permute-start(bf16[368,512]{1,0:T(8,128)(2,1)} %get-tuple-element.428), channel_id=1, source_target_pairs={{0,8},{8,16},{16,24},{24,0},{1,9},{9,17},{17,25},{25,1},{2,10},{10... | collective-permute-start | bytes 1130504 | tf_op jit(solution)/shard_map/ppermute | solution.py:833
  440.2 37.5 %collective-permute-start.37 = (bf16[368,512]{1,0:T(8,128)(2,1)}, bf16[368,512]{1,0:T(8,128)(2,1)S(1)}, u32[]{:S(2)}, u32[]{:S(2)}) collective-permute-start(bf16[368,512]{1,0:T(8,128)(2,1)} %get-tuple-element.427), channel_id=1, source_target_pairs={{0,16},{8,24},{16,0},{24,8},{1,17},{9,25},{17,1},{25,9},{2,18},{10... | collective-permute-start | bytes 1130504 | tf_op jit(solution)/shard_map/ppermute | solution.py:833
  443.2 34.4 %collective-permute-start.38 = (bf16[368,512]{1,0:T(8,128)(2,1)S(1)}, bf16[368,512]{1,0:T(8,128)(2,1)S(1)}, u32[]{:S(2)}, u32[]{:S(2)}) collective-permute-start(bf16[368,512]{1,0:T(8,128)(2,1)S(1)} %get-tuple-element.426), channel_id=1, source_target_pairs={{0,24},{8,0},{16,8},{24,16},{1,25},{9,1},{17,9},{25,17},{2,26},{10... | collective-permute-start | bytes 1130504 | tf_op jit(solution)/shard_map/ppermute | solution.py:833
  444.8 31.1 %collective-permute-start.40 = (bf16[128,1024]{1,0:T(8,128)(2,1)}, bf16[128,1024]{1,0:T(8,128)(2,1)S(1)}, u32[]{:S(2)}, u32[]{:S(2)}) collective-permute-start(bf16[128,1024]{1,0:T(8,128)(2,1)} %get-tuple-element.292), channel_id=1, source_target_pairs={{0,4},{4,0},{1,5},{5,1},{2,6},{6,2},{3,7},{7,3},{8,12},{12,8},{9,1... | collective-permute-start | bytes 786440 | tf_op jit(solution)/shard_map/ppermute | solution.py:802
  475.9 40.6 %collective-permute-start.43 = (bf16[512,1024]{1,0:T(8,128)(2,1)}, bf16[512,1024]{1,0:T(8,128)(2,1)}, u32[]{:S(2)}, u32[]{:S(2)}) collective-permute-start(bf16[512,1024]{1,0:T(8,128)(2,1)} %input_grad.1), channel_id=1, source_target_pairs={{0,1},{1,0},{2,3},{3,2},{4,5},{5,4},{6,7},{7,6},{8,9},{9,8},{10,11... | collective-permute-start | bytes 3145736 | tf_op jit(solution)/shard_map/ppermute | solution.py:806
  491.0 25.6 %all-to-all-start.7 = ((bf16[4,272,512]{2,1,0:T(8,128)(2,1)}), bf16[4,272,512]{2,1,0:T(8,128)(2,1)S(1)}, u32[]{:S(2)}, u32[]{:S(2)}) async-start(bf16[4,272,512]{2,1,0:T(8,128)(2,1)} %pad_maximum_fusion.2), calls=%async_computation.7 | async-start | bytes 2228224 | tf_op jit(solution)/shard_map/all_to_all | solution.py:814
  (103 other events, 776.6 us)
